TPU v7x, 32 devices: a whole 2x2x4 slice. The times are simulated.
32 devices in a mesh: seq: 2 (over core), depth: 2 (over x), vocab: 8 (over z, y).
Axes of the slice: x: 2, y: 2, z: 4, core: 2. Of those that a mesh axis runs over, the one named last changes fastest.
Arguments:
- hidden: bfloat16 [2, 128, 7168], P('depth', ('seq', 'vocab')), may hold values from -24 to 24
- embedding: bfloat16 [16160, 7168], P(('seq', 'vocab')), may hold values from -1 to 1
- targets: int32 [2, 128], P('depth', ('seq', 'vocab')), may hold values from 0 to 16159
- mask: int32 [2, 128], P('depth', ('seq', 'vocab')), may hold values 0 or 1
Outputs:
- nll: float32 [2, 128], P('depth', ('seq', 'vocab'))
- loss: float32 [], replicated
- grad_norm: float32 [], replicated
All inputs are finite; a program needn't handle non-finite values. No bound on the sum of `mask` on one device may be relied on, other than what follows from the above.
Results may differ from a plain program's by a relative error of at most 0.0023.
Values may be sent and summed in bfloat16 or wider, within the bound.
No kernel may reach another device: no remote copies, remote signals or barrier semaphores. Data moves between devices by JAX's collectives and lax.ppermute only.
A program may use at most 128 MiB of HBM per device.

v0:
```python
import jax
import jax.numpy as jnp
from jax import lax
from jax.sharding import PartitionSpec as P


def swapped(value, axis, apart):
    mask = 2**apart
    pairs = [(source, source ^ mask) for source in range(lax.axis_size(axis))]
    return lax.ppermute(value, axis, pairs)


def rows_product(grad_rows, states):
    part = lax.dot_general(
        grad_rows, states, (((0,), (0,)), ((), ())), preferred_element_type=jnp.float32
    )
    return part


def local(hidden, embedding, targets, mask):
    states, picks, flags = (
        lax.all_gather(hidden, ("seq", "vocab"), axis=1, tiled=True),
        lax.all_gather(targets, ("seq", "vocab"), axis=1, tiled=True),
        lax.all_gather(mask, ("seq", "vocab"), axis=1, tiled=True),
    )
    states = states[0]
    picks = picks[0]
    live = flags[0].astype(jnp.float32)
    width = embedding.shape[0]
    offset = lax.axis_index(("seq", "vocab")) * width
    logits = lax.dot_general(
        states, embedding, (((1,), (1,)), ((), ())), preferred_element_type=jnp.float32
    )
    ids = offset + lax.broadcasted_iota(jnp.int32, (1, width), 1)
    onehot = picks[:, None] == ids
    local_peak = jnp.max(logits, axis=1)
    chosen = jnp.sum(jnp.where(onehot, logits, jnp.zeros((), jnp.float32)), axis=1)
    peak = lax.pmax(local_peak, ("seq", "vocab"))
    total, target = lax.psum(
        (jnp.sum(jnp.exp(logits - peak[:, None]), axis=1), chosen), ("seq", "vocab")
    )
    lse = peak + jnp.log(total)
    nll = lse - target
    side = lax.axis_index("depth")
    weight = jnp.where(side == 0, jnp.float32(1.0), jnp.float32(0.3))
    coef = weight / jnp.maximum(jnp.sum(live), jnp.float32(1.0))
    loss = lax.psum(coef * jnp.sum(live * nll), "depth")
    grad_rows = (
        coef * live[:, None] * (jnp.exp(logits - lse[:, None]) - onehot.astype(jnp.float32))
    ).astype(jnp.bfloat16)
    half = width // 2
    mine = lax.dynamic_slice_in_dim(grad_rows, side * half, half, 1)
    other = lax.dynamic_slice_in_dim(grad_rows, (1 - side) * half, half, 1)
    recv_grad, recv_states = swapped((other, states), "depth", 0)
    own_part = rows_product(mine, states).astype(jnp.bfloat16)
    peer_part = rows_product(recv_grad, recv_states).astype(jnp.bfloat16)
    own_part, peer_part = lax.optimization_barrier((own_part, peer_part))
    summed = own_part.astype(jnp.float32) + peer_part.astype(jnp.float32)
    square = jnp.sum(summed * summed)
    grad_norm = jnp.sqrt(lax.psum(square, ("seq", "depth", "vocab")))
    count = hidden.shape[1]
    start = lax.axis_index(("seq", "vocab")) * count
    nll_own = lax.dynamic_slice_in_dim(nll, start, count, 0)[None, :]
    return (nll_own, loss, grad_norm)


def solution(mesh):
    placed = (
        P("depth", ("seq", "vocab"), None),
        P(("seq", "vocab"), None),
        P("depth", ("seq", "vocab")),
        P("depth", ("seq", "vocab")),
    )
    return jax.shard_map(
        local,
        mesh=mesh,
        in_specs=placed,
        out_specs=(P("depth", ("seq", "vocab")), P(), P()),
        check_vma=False,
    )
```

profile of v0, /device:TPU:0, one launch (start us, length us, event | category | flops | bytes accessed | tf_op | source)
XLA Modules:
  0.0 201.8 jit_solution(6596375111063482655)
XLA Ops:
  7.2 0.0 all-gather.2.cloned.1.call-start
  7.2 0.7 all-gather.2.cloned.1.call-update
  7.9 1.2 dynamic-slice
  9.8 0.8 bitcast_dynamic-update-slice_fusion.1
  10.6 0.7 bitcast_dynamic-update-slice_fusion
  11.3 13.9 %all-reduce.2 = (s32[128]{0:T(128)S(1)}, s32[128]{0:T(128)S(1)}) all-reduce(s32[128]{0:T(128)S(1)} %bitcast_dynamic-update-slice_fusion.1, s32[128]{0:T(128)S(1)} %bitcast_dynamic-update-slice_fusion), channel_id=1, replica_groups=mesh['seq'=2,'depth'=2,'vocab'=8] {'seq','vocab'}, use_global_device_ids=true, to_apply=%add | all-reduce | flops 256 | bytes 2048
  25.2 28.3 %all-gather.2.cloned.1.call-done = bf16[1,128,7168]{2,1,0:T(8,128)(2,1)} async-done(((bf16[1,8,7168]{2,1,0:T(8,128)(2,1)}), bf16[1,128,7168]{2,1,0:T(8,128)(2,1)}) %all-gather.2.cloned.1.call-update) | async-done | bytes 1835024 | tf_op jit(solution)/shard_map/all_gather | solution.py:22
  53.6 0.0 copy-start.1
  53.6 1.5 collective-permute-start.1
  55.0 7.9 %fusion.10 = (f32[128]{0:T(128)S(1)}, f32[128,1010]{0,1:T(8,128)S(1)}) fusion(bf16[1010,7168]{1,0:T(8,128)(2,1)} %param.5, bf16[1,128,7168]{2,1,0:T(8,128)(2,1)} %all-gather.2.cloned.1.call-done), kind=kOutput, calls=%fused_computation.25 | convolution fusion | flops 1853487232 | bytes 16832000 | tf_op jit(solution)/shard_map/dot_general | solution.py:31
  63.0 33.1 %pmax.7 = f32[128]{0:T(128)S(1)} all-reduce(f32[128]{0:T(128)S(1)} %get-tuple-element.17), channel_id=1, replica_groups=mesh['seq'=2,'depth'=2,'vocab'=8] {'seq','vocab'}, use_global_device_ids=true, to_apply=%region_1.2 | all-reduce | flops 128 | bytes 1024 | tf_op jit(solution)/shard_map/pmax | solution.py:38
  96.1 0.2 fusion
  96.3 29.5 %all-reduce.3 = (f32[128]{0:T(128)S(1)}, f32[128]{0:T(128)S(1)}) all-reduce(f32[128]{0:T(128)S(1)} %get-tuple-element.8, f32[128]{0:T(128)S(1)} %get-tuple-element.7), channel_id=1, replica_groups=mesh['seq'=2,'depth'=2,'vocab'=8] {'seq','vocab'}, use_global_device_ids=true, to_apply=%region_3.4 | all-reduce | flops 256 | bytes 2048 | tf_op jit(solution)/shard_map/psum | solution.py:39
  125.8 0.6 fusion.5
  127.1 0.2 fusion.3
  127.4 1.2 collective-permute-start
  128.6 0.0 copy-done.1
  128.6 5.0 %convolution_convert_fusion.1 = bf16[505,7168]{1,0:T(8,128)(2,1)} fusion(bf16[128,1010]{0,1:T(8,128)(2,1)S(1)} %fusion.3, s32[]{:T(128)S(6)} %select_n.20, bf16[1,128,7168]{2,1,0:T(8,128)(2,1)S(1)} %copy-done.1), kind=kOutput, calls=%fused_computation.2 | convolution fusion | flops 930298880 | bytes 9205764 | tf_op jit(solution)/shard_map/dot_general | solution.py:14
  134.3 0.0 copy-start
  134.3 0.0 collective-permute-done
  134.3 0.0 collective-permute-done.1
  134.3 6.7 %convolution_convert_fusion = bf16[505,7168]{1,0:T(8,128)(2,1)} fusion(bf16[128,505]{0,1:T(8,128)(2,1)S(1)} %collective-permute-done, bf16[128,7168]{1,0:T(8,128)(2,1)} %collective-permute-done.1), kind=kOutput, calls=%fused_computation.1 | convolution fusion | flops 930298880 | bytes 9203968 | tf_op jit(solution)/shard_map/dot_general | solution.py:14
  141.0 0.0 copy-done
  141.0 7.5 %multiply_reduce_fusion = f32[]{:T(128)} fusion(bf16[505,7168]{1,0:T(8,128)(2,1)} %convolution_convert_fusion, bf16[505,7168]{1,0:T(8,128)(2,1)S(1)} %copy-done), kind=kLoop, calls=%fused_computation | loop fusion | flops 18099200 | bytes 14479364 | tf_op jit(solution)/shard_map/reduce_sum | solution.py:59
  148.5 0.6 dynamic-slice_bitcast_fusion
  149.1 5.4 %psum.30 = f32[]{:T(128)} all-reduce(f32[]{:T(128)S(6)} %mul.48), channel_id=1, replica_groups=mesh['seq'=2,'depth'=2,'vocab'=8] {'depth'}, use_global_device_ids=true, to_apply=%region_8.9 | all-reduce | flops 1 | bytes 8 | tf_op jit(solution)/shard_map/psum | solution.py:47
  154.5 38.6 %psum.31 = f32[]{:T(128)} all-reduce(f32[]{:T(128)} %multiply_reduce_fusion), channel_id=1, replica_groups=mesh['seq'=2,'depth'=2,'vocab'=8] {'seq','depth','vocab'}, use_global_device_ids=true, to_apply=%region_10.11 | all-reduce | flops 1 | bytes 8 | tf_op jit(solution)/shard_map/psum | solution.py:60
  (5 shorter events, 0.1 us)
Async XLA Ops:
  7.2 46.4 %all-gather.2.cloned.1.call-start = ((), (), s32[]{:S(2)}) async-start(), calls=%async_computation | async-start | bytes 1949696 | tf_op jit(solution)/shard_map/all_gather | solution.py:22
  53.6 75.0 %copy-start.1 = (bf16[1,128,7168]{2,1,0:T(8,128)(2,1)S(1)}, bf16[1,128,7168]{2,1,0:T(8,128)(2,1)}, u32[]{:S(2)}) copy-start(bf16[1,128,7168]{2,1,0:T(8,128)(2,1)} %all-gather.2.cloned.1.call-done) | copy-start | bytes 5505028
  53.6 80.7 %collective-permute-start.1 = (bf16[128,7168]{1,0:T(8,128)(2,1)}, bf16[128,7168]{1,0:T(8,128)(2,1)}, u32[]{:S(2)}, u32[]{:S(2)}) collective-permute-start(bf16[128,7168]{1,0:T(8,128)(2,1)} %bitcast.17), channel_id=1, source_target_pairs={{0,8},{8,0},{1,9},{9,1},{2,10},{10,2},{3,11},{11,3},{4,12},{12,4},... | collective-permute-start | bytes 5505032 | tf_op jit(solution)/shard_map/ppermute | solution.py:10
  127.4 6.9 %collective-permute-start = (bf16[128,505]{0,1:T(8,128)(2,1)S(1)}, bf16[128,505]{0,1:T(8,128)(2,1)S(1)}, u32[]{:S(2)}, u32[]{:S(2)}) collective-permute-start(bf16[128,505]{0,1:T(8,128)(2,1)S(1)} %constant_dynamic-slice_fusion), channel_id=1, source_target_pairs={{0,8},{8,0},{1,9},{9,1},{2,10},{10,2},{3,11},{11,3},{4,12},{12,4},... | collective-permute-start | bytes 387848 | tf_op jit(solution)/shard_map/ppermute | solution.py:10
  134.3 6.8 %copy-start = (bf16[505,7168]{1,0:T(8,128)(2,1)S(1)}, bf16[505,7168]{1,0:T(8,128)(2,1)}, u32[]{:S(2)}) copy-start(bf16[505,7168]{1,0:T(8,128)(2,1)} %convolution_convert_fusion.1) | copy-start | bytes 21719044
Sparse Core Ops, SparseCore 0:
  10.2 43.3 all-gather.1
where the time goes:
time: 203 us; the launch traced here: 202 us
  blocking collectives  121 us (60%)
  waiting for transfers between devices  29 us (14%)
  matrix products  19.7 us (10%)
  between operations  17.9 us (9%)
  other arithmetic  8.51 us (4%)
  local copies, waits for them, and re-layouts  3.37 us (2%)
  starting transfers between devices  2.7 us (1%)
    psum x1, blocking collectives, local(): grad_norm = jnp.sqrt(lax.psum(square, ('seq', 'depth', 'vocab')))  38.6 us
    pmax x1, blocking collectives, local(): peak = lax.pmax(local_peak, ('seq', 'vocab'))  33.1 us
    psum x1, blocking collectives, local(): lax.psum((jnp.sum(jnp.exp(logits - peak[:, None]), axis=1), chosen), ('se...  29.5 us
    all_gather x1, waiting for transfers between devices, local(): lax.all_gather(hidden, ('seq', 'vocab'), axis=1, tiled=True)  28.3 us
    unnamed x1, blocking collectives  13.9 us
    dot_general x2, matrix products, rows_product(): lax.dot_general(grad_rows, states, (((0,), (0,)), ((), ())), preferred_el...  11.8 us
    dot_general x1, matrix products, local(): lax.dot_general(states, embedding, (((1,), (1,)), ((), ())), preferred_el...  7.92 us
    reduce_sum x1, other arithmetic, local(): square = jnp.sum(summed * summed)  7.46 us
  transfers between devices with their start and end apart: 3, of which 1 were waited for; matrix products, arithmetic and copies ran while one was open for 8% of the time, Pallas kernels for 0%

commit v1 on v0

v1 whole, which is shorter than its diff:
```python
import functools

import jax
import jax.numpy as jnp
from jax import lax
from jax.experimental import pallas as pl
from jax.experimental.pallas import tpu as pltpu
from jax.sharding import PartitionSpec as P

GROUP = ("seq", "vocab")
EVERY = ("seq", "depth", "vocab")
SCALE = 2.0**40
WEIGHTS = (1.0, 0.3)
HIGH = lax.Precision.HIGHEST


def exchange_masks(size):
    bits = size.bit_length() - 1
    assert size == 2**bits
    return [2**bit ^ (2 ** (bit - 1) if bit >= 2 else 0) for bit in range(bits)]


def round_pairs(masks, turn, cores, size):
    pairs = []
    for core in range(cores):
        mask = masks[(turn + core) % len(masks)]
        pairs += [(core * size + at, core * size + (at ^ mask)) for at in range(size)]
    return pairs


def swapped(value, axis):
    return lax.ppermute(value, axis, [(0, 1), (1, 0)])


def token_order(masks, size, count):
    total = 2 * size * count
    row = lax.broadcasted_iota(jnp.int32, (total, 1), 0)
    core = lax.axis_index("seq") ^ (row // (size * count))
    slot = (row // count) % size
    at = jnp.broadcast_to(lax.axis_index("vocab"), row.shape)
    for turn in range(len(masks)):
        bit = (slot >> turn) & 1
        first, second = masks[turn % len(masks)], masks[(turn + 1) % len(masks)]
        at = at ^ (bit * jnp.where(core == 0, first, second))
    return (core * size + at) * count + row % count


def rows_dot(a, b, dims, precision=None):
    return lax.dot_general(
        a, b, ((dims[:1], dims[1:]), ((), ())), precision=precision, preferred_element_type=jnp.float32
    )


def logits_kernel(
    width, half, steps, own_ref, twin_ref, side_ref, table_ref, perm_ref, meta_ref,
    logits_ref, send_ref, gram_ref, pack_ref,
):
    step = pl.program_id(0)

    @pl.when(step == 0)
    def _():
        logits_ref[...] = jnp.zeros_like(logits_ref)
        gram_ref[...] = jnp.zeros_like(gram_ref)
        pack_ref[...] = jnp.zeros_like(pack_ref)

    states = jnp.concatenate([own_ref[...], twin_ref[...]], axis=0)
    logits_ref[:width, :] += rows_dot(table_ref[...], states, (1, 1))
    gram_ref[...] += rows_dot(states, states, (1, 1))
    pack_ref[8:, :] += rows_dot(side_ref[...], states, (1, 1))

    @pl.when(step == steps - 1)
    def _():
        depth = lax.axis_index("depth")
        logits = logits_ref[...]
        valid = lax.broadcasted_iota(jnp.int32, logits.shape, 0) < width
        peak = jnp.max(jnp.where(valid, logits, -jnp.inf), axis=0, keepdims=True)
        total = jnp.sum(jnp.where(valid, jnp.exp(logits - peak), 0.0), axis=0, keepdims=True)
        send_ref[...] = logits_ref[pl.ds(pl.multiple_of((1 - depth) * half, 8), half), :]
        rows = lax.broadcasted_iota(jnp.int32, (8, peak.shape[1]), 0)
        stats = jnp.where(rows == 0, peak, jnp.where(rows == 1, total, 0.0))
        both = jnp.concatenate([stats, pack_ref[8:, :]], axis=0)
        both = rows_dot(both, perm_ref[...], (1, 0), HIGH)
        pack_ref[...] = both + meta_ref[...]


def gradient_kernel(
    width, half, sizes, logits_ref, peer_ref, recv_ref, perm_ref, gram_ref, base_ref, pack_ref, keep_ref
):
    cores, vocabs, count = sizes
    depth = lax.axis_index("depth")
    tokens = perm_ref.shape[0]
    peers = [(core, at) for core in range(cores) for at in range(vocabs)]

    def head(which):
        parts = [recv_ref[core, which, at, 0:8, :] for core, at in peers]
        peak = functools.reduce(jnp.maximum, parts)[0:1, :]
        total = sum(part[1:2, :] * jnp.exp(part[0:1, :] - peak) for part in parts)
        meta = functools.reduce(jnp.add, parts)
        live = meta[3:4, :]
        weight = jnp.where(which == 0, jnp.float32(WEIGHTS[0]), jnp.float32(WEIGHTS[1]))
        scale = live * (weight / jnp.maximum(jnp.sum(live), 1.0))
        return peak + jnp.log(total), meta[2:3, :], scale

    lse, target, scale = head(depth)
    lse_peer, target_peer, scale_peer = head(1 - depth)
    rows = lax.broadcasted_iota(jnp.int32, (8, tokens), 0)
    vectors = jnp.zeros((8, tokens), jnp.float32)
    for at, vector in enumerate((lse, target, scale, lse_peer, target_peer, scale_peer)):
        vectors = jnp.where(rows == at, vector, vectors)
    keep_ref[...] = vectors
    vectors = rows_dot(vectors, perm_ref[...], (1, 1), HIGH)

    base = base_ref[0]
    shift = pl.multiple_of(depth * half, 8)

    def gradient(logits, at, first):
        row = lax.broadcasted_iota(jnp.int32, logits.shape, 0) + first
        hit = (row + base) == vectors[at + 1 : at + 2, :].astype(jnp.int32)
        soft = jnp.exp(logits - vectors[at : at + 1, :]) - jnp.where(hit, 1.0, 0.0)
        grad = (vectors[at + 2 : at + 3, :] * SCALE) * soft
        return hit, jnp.where(row < width, grad, 0.0).astype(jnp.bfloat16)

    logits = logits_ref[...]
    hit, grad = gradient(logits, 0, 0)
    chosen = jnp.sum(jnp.where(hit, logits, 0.0), axis=0, keepdims=True)
    _, mine = gradient(logits_ref[pl.ds(shift, half), :], 0, shift)
    _, grad_peer = gradient(peer_ref[...], 3, shift)
    inner = rows_dot(grad, grad, (0, 0))
    cross = rows_dot(grad_peer, mine, (0, 0))
    cross = rows_dot(perm_ref[...], cross, (0, 0), HIGH)
    cross = rows_dot(cross, perm_ref[...], (1, 0), HIGH)
    sides = jnp.concatenate([recv_ref[core, depth, at, 8 : 8 + count, :] for core, at in peers], axis=0)
    square = jnp.sum(inner * gram_ref[...] + 2.0 * cross * sides, axis=0, keepdims=True)
    chosen = rows_dot(jnp.broadcast_to(chosen, (8, tokens)), perm_ref[...], (1, 0), HIGH)
    pack_ref[...] = jnp.where(rows == depth, chosen, jnp.where(rows == 2, square, 0.0))


def final_kernel(sizes, recv_ref, keep_ref, nll_ref, loss_ref, norm_ref):
    count = sizes[2]
    depth = lax.axis_index("depth")
    total = jnp.sum(recv_ref[...], axis=0)
    keep = keep_ref[...]
    own = jnp.where(depth == 0, total[0:1, :], total[1:2, :])
    peer = jnp.where(depth == 0, total[1:2, :], total[0:1, :])
    nll = keep[0:1, :] - own
    loss_ref[0, 0] = jnp.sum(keep[2:3, :] * nll) + jnp.sum(keep[5:6, :] * (keep[3:4, :] - peer))
    square = jnp.maximum(jnp.sum(total[2:3, :]), 0.0)
    norm_ref[0, 0] = square
    nll_ref[...] = nll


def everyone(value, size):
    spread = jnp.broadcast_to(value[None], (size,) + value.shape)
    return lax.all_to_all(spread, EVERY, 0, 0, tiled=True)


def local(hidden, embedding, targets, mask):
    cores, depths, vocabs = (lax.axis_size(axis) for axis in EVERY)
    assert cores == 2 and depths == 2
    count, dim = hidden.shape[1:]
    width = embedding.shape[0]
    half = -(-width // 16) * 8
    tokens = cores * vocabs * count
    masks = exchange_masks(vocabs)
    place = lax.axis_index(GROUP)
    sizes = (cores, vocabs, count)

    own = hidden[0]
    side = swapped(own, "depth")
    for turn in range(len(masks)):
        own = jnp.concatenate([own, lax.ppermute(own, GROUP, round_pairs(masks, turn, cores, vocabs))], axis=0)
    twin = swapped(own, "seq")

    order = token_order(masks, vocabs, count)
    column = lax.broadcasted_iota(jnp.int32, (tokens, tokens), 1)
    perm = (order == column).astype(jnp.float32)
    lane = lax.broadcasted_iota(jnp.int32, (count, tokens), 1)
    spot = (lane == place * count + lax.broadcasted_iota(jnp.int32, (count, tokens), 0)).astype(jnp.float32)
    placed = [jnp.sum(spot * value[0][:, None].astype(jnp.float32), axis=0) for value in (targets, mask)]
    line = lax.broadcasted_iota(jnp.int32, (8 + count, tokens), 0)
    meta = jnp.where(line == 2, placed[0][None, :], jnp.where(line == 3, placed[1][None, :], 0.0))

    chunk = 512 if dim % 512 == 0 else 128
    steps = dim // chunk
    still = lambda step: (0, 0)
    moving = lambda step: (0, step)
    f32 = jnp.float32
    logits, send, gram, pack = pl.pallas_call(
        functools.partial(logits_kernel, width, half, steps),
        grid=(steps,),
        in_specs=[
            pl.BlockSpec((tokens // 2, chunk), moving),
            pl.BlockSpec((tokens // 2, chunk), moving),
            pl.BlockSpec((count, chunk), moving),
            pl.BlockSpec((width, chunk), moving),
            pl.BlockSpec((tokens, tokens), still),
            pl.BlockSpec((8 + count, tokens), still),
        ],
        out_specs=[
            pl.BlockSpec((2 * half, tokens), still),
            pl.BlockSpec((half, tokens), still),
            pl.BlockSpec((tokens, tokens), still),
            pl.BlockSpec((8 + count, tokens), still),
        ],
        out_shape=[
            jax.ShapeDtypeStruct((2 * half, tokens), f32),
            jax.ShapeDtypeStruct((half, tokens), f32),
            jax.ShapeDtypeStruct((tokens, tokens), f32),
            jax.ShapeDtypeStruct((8 + count, tokens), f32),
        ],
        name="logits",
    )(own, twin, side, embedding, perm, meta)

    peer = swapped(send, "depth")
    recv = everyone(pack, cores * depths * vocabs)
    recv = recv.reshape(cores, depths, vocabs, 8 + count, tokens)
    base = (place * width).astype(jnp.int32).reshape(1)

    vmem = pl.BlockSpec(memory_space=pltpu.VMEM)
    smem = pl.BlockSpec(memory_space=pltpu.SMEM)
    pack, keep = pl.pallas_call(
        functools.partial(gradient_kernel, width, half, sizes),
        in_specs=[vmem] * 5 + [smem],
        out_specs=[vmem] * 2,
        out_shape=[jax.ShapeDtypeStruct((8, tokens), f32)] * 2,
        name="gradient",
    )(logits, peer, recv, perm, gram, base)

    recv = everyone(pack, cores * depths * vocabs)
    nll, loss, square = pl.pallas_call(
        functools.partial(final_kernel, sizes),
        in_specs=[vmem] * 2,
        out_specs=[vmem, smem, smem],
        out_shape=[
            jax.ShapeDtypeStruct((1, tokens), f32),
            jax.ShapeDtypeStruct((1, 1), f32),
            jax.ShapeDtypeStruct((1, 1), f32),
        ],
        name="final",
    )(recv, keep)
    norm = jnp.sqrt(square[0, 0]) * jnp.float32(1.0 / SCALE)
    return (lax.dynamic_slice_in_dim(nll, place * count, count, 1), loss[0, 0], norm)


def solution(mesh):
    placed = (
        P("depth", GROUP, None),
        P(GROUP, None),
        P("depth", GROUP),
        P("depth", GROUP),
    )
    return jax.shard_map(
        local,
        mesh=mesh,
        in_specs=placed,
        out_specs=(P("depth", GROUP), P(), P()),
        check_vma=False,
    )
```

time: 203 us -> 90.9 us (0.45)
  blocking collectives: 121 us -> 0 us
  starting transfers between devices: 2.7 us -> 24.3 us
  matrix products: 19.7 us -> 0 us
  Pallas kernels: 0 us -> 19.7 us
  between operations: 17.9 us -> 2.57 us
  other arithmetic: 8.51 us -> 4.29 us
  waiting for transfers between devices: 29 us -> 32.9 us
  local copies, waits for them, and re-layouts: 3.37 us -> 6.42 us
    psum x3 -> x0, blocking collectives: 73.6 us -> none  [the longest x1 38.6 us: local(): grad_norm = jnp.sqrt(lax.psum(square, ('seq', 'depth', 'vocab')))]
    pmax x1 -> x0, blocking collectives: 33.1 us -> none  [local(): peak = lax.pmax(local_peak, ('seq', 'vocab'))]
    all_gather x1 -> x0, waiting for transfers between devices: 28.3 us -> none  [local(): lax.all_gather(hidden, ('seq', 'vocab'), axis=1, tiled=True)]
    ppermute x2 -> x6, waiting for transfers between devices: 0.01 us -> 24.9 us  [the longest x3 14.5 us: local(): lax.ppermute(own, GROUP, round_pairs(masks, turn, cores, vocabs))]
    pallas_call x0 -> x3, Pallas kernels: none -> 19.7 us  [the longest x1 14.9 us: local(): pl.pallas_call(functools.partial(logits_kernel, width, half, steps), grid...]
    dot_general x3 -> x0, matrix products: 19.7 us -> none  [the longest x2 11.8 us: rows_product(): lax.dot_general(grad_rows, states, (((0,), (0,)), ((), ())), preferred_el...]
    unnamed x1 -> x0, blocking collectives: 13.9 us -> none
    all_to_all x0 -> x2, starting transfers between devices: none -> 11.6 us  [everyone(): return lax.all_to_all(spread, EVERY, 0, 0, tiled=True)]
  transfers between devices with their start and end apart: 3 -> 8, of which waited for: 1 -> 6; matrix products, arithmetic and copies ran while one was open for 8% -> 3% of each run, Pallas kernels for 0% -> 0%
where the time goes in v1:
time: 90.9 us; the launch traced here: 90.2 us
  waiting for transfers between devices  32.9 us (36%)
  starting transfers between devices  24.3 us (27%)
  Pallas kernels  19.7 us (22%)
  local copies, waits for them, and re-layouts  6.42 us (7%)
  other arithmetic  4.29 us (5%)
  between operations  2.57 us (3%)
    pallas_call x1, Pallas kernels, local(): pl.pallas_call(functools.partial(logits_kernel, width, half, steps), grid...  14.9 us
    ppermute x3, waiting for transfers between devices, local(): lax.ppermute(own, GROUP, round_pairs(masks, turn, cores, vocabs))  14.5 us
    all_to_all x2, starting transfers between devices, everyone(): return lax.all_to_all(spread, EVERY, 0, 0, tiled=True)  11.6 us
    ppermute x3, waiting for transfers between devices, swapped(): return lax.ppermute(value, axis, [(0, 1), (1, 0)])  10.4 us
    ppermute x3, starting transfers between devices, local(): lax.ppermute(own, GROUP, round_pairs(masks, turn, cores, vocabs))  9.22 us
    all_to_all x2, waiting for transfers between devices, everyone(): return lax.all_to_all(spread, EVERY, 0, 0, tiled=True)  8.07 us
    ppermute x3, starting transfers between devices, swapped(): return lax.ppermute(value, axis, [(0, 1), (1, 0)])  3.39 us
    pallas_call x1, Pallas kernels, local(): pl.pallas_call(functools.partial(gradient_kernel, width, half, sizes), in...  3.25 us
  transfers between devices with their start and end apart: 8, of which 6 were waited for; matrix products, arithmetic and copies ran while one was open for 3% of the time, Pallas kernels for 0%

profile of v1, /device:TPU:0, one launch (start us, length us, event | category | flops | bytes accessed | tf_op | source)
XLA Modules:
  0.0 90.2 jit_solution(6378585693901613651)
XLA Ops:
  0.7 3.1 %collective-permute-start = (bf16[8,7168]{1,0:T(8,128)(2,1)}, bf16[8,7168]{1,0:T(8,128)(2,1)S(1)}, u32[]{:S(2)}, u32[]{:S(2)}) collective-permute-start(bf16[8,7168]{1,0:T(8,128)(2,1)} %bitcast.10), channel_id=1, source_target_pairs={{0,1},{1,0},{2,3},{3,2},{4,5},{5,4},{6,7},{7,6},{16,18},{17,19},{1... | collective-permute-start | bytes 344072 | tf_op jit(solution)/shard_map/ppermute | solution.py:171
  3.7 3.0 %collective-permute-done = bf16[8,7168]{1,0:T(8,128)(2,1)S(1)} collective-permute-done((bf16[8,7168]{1,0:T(8,128)(2,1)}, bf16[8,7168]{1,0:T(8,128)(2,1)S(1)}, u32[]{:S(2)}, u32[]{:S(2)}) %collective-permute-start) | collective-permute-done | bytes 114720 | tf_op jit(solution)/shard_map/ppermute | solution.py:171
  6.7 0.9 %pad_maximum_fusion.2 = bf16[16,7168]{1,0:T(8,128)(2,1)S(1)} fusion(bf16[8,7168]{1,0:T(8,128)(2,1)S(1)} %collective-permute-done, bf16[8,7168]{1,0:T(8,128)(2,1)} %bitcast.11), kind=kLoop, calls=%fused_computation.2 | loop fusion | flops 458752 | bytes 458752 | tf_op jit(solution)/shard_map/concatenate | solution.py:171
  7.6 2.1 %collective-permute-start.1 = (bf16[16,7168]{1,0:T(8,128)(2,1)S(1)}, bf16[16,7168]{1,0:T(8,128)(2,1)S(1)}, u32[]{:S(2)}, u32[]{:S(2)}) collective-permute-start(bf16[16,7168]{1,0:T(8,128)(2,1)S(1)} %pad_maximum_fusion.2), channel_id=1, source_target_pairs={{0,2},{1,3},{2,0},{3,1},{4,6},{5,7},{6,4},{7,5},{16,22},{17,23},{1... | collective-permute-start | bytes 688136 | tf_op jit(solution)/shard_map/ppermute | solution.py:171
  9.8 6.5 %collective-permute-done.1 = bf16[16,7168]{1,0:T(8,128)(2,1)S(1)} collective-permute-done((bf16[16,7168]{1,0:T(8,128)(2,1)S(1)}, bf16[16,7168]{1,0:T(8,128)(2,1)S(1)}, u32[]{:S(2)}, u32[]{:S(2)}) %collective-permute-start.1) | collective-permute-done | bytes 229408 | tf_op jit(solution)/shard_map/ppermute | solution.py:171
  16.2 0.9 %pad_maximum_fusion.1 = bf16[32,7168]{1,0:T(8,128)(2,1)S(1)} fusion(bf16[16,7168]{1,0:T(8,128)(2,1)S(1)} %collective-permute-done.1, bf16[8,7168]{1,0:T(8,128)(2,1)S(1)} %collective-permute-done, bf16[8,7168]{1,0:T(8,128)(2,1)} %bitcast.12), kind=kLoop, calls=%fused_computation.1 | loop fusion | flops 1376256 | bytes 917504 | tf_op jit(solution)/shard_map/concatenate | solution.py:171
  17.1 4.0 %collective-permute-start.2 = (bf16[32,7168]{1,0:T(8,128)(2,1)S(1)}, bf16[32,7168]{1,0:T(8,128)(2,1)S(1)}, u32[]{:S(2)}, u32[]{:S(2)}) collective-permute-start(bf16[32,7168]{1,0:T(8,128)(2,1)S(1)} %pad_maximum_fusion.1), channel_id=1, source_target_pairs={{0,6},{1,7},{2,4},{3,5},{4,2},{5,3},{6,0},{7,1},{16,17},{17,16},{1... | collective-permute-start | bytes 1376264 | tf_op jit(solution)/shard_map/ppermute | solution.py:171
  21.2 1.5 %collective-permute-start.4 = (bf16[8,7168]{1,0:T(8,128)(2,1)}, bf16[8,7168]{1,0:T(8,128)(2,1)S(1)}, u32[]{:S(2)}, u32[]{:S(2)}) collective-permute-start(bf16[8,7168]{1,0:T(8,128)(2,1)} %bitcast.13), channel_id=1, source_target_pairs={{0,8},{8,0},{1,9},{9,1},{2,10},{10,2},{3,11},{11,3},{4,12},{12,4},... | collective-permute-start | bytes 344072 | tf_op jit(solution)/shard_map/ppermute | solution.py:32
  22.7 5.1 %collective-permute-done.2 = bf16[32,7168]{1,0:T(8,128)(2,1)S(1)} collective-permute-done((bf16[32,7168]{1,0:T(8,128)(2,1)S(1)}, bf16[32,7168]{1,0:T(8,128)(2,1)S(1)}, u32[]{:S(2)}, u32[]{:S(2)}) %collective-permute-start.2) | collective-permute-done | bytes 458784 | tf_op jit(solution)/shard_map/ppermute | solution.py:171
  27.7 1.0 %pad_maximum_fusion.own_ref = bf16[64,7168]{1,0:T(8,128)(2,1)S(1)} fusion(bf16[32,7168]{1,0:T(8,128)(2,1)S(1)} %collective-permute-done.2, bf16[16,7168]{1,0:T(8,128)(2,1)S(1)} %collective-permute-done.1, bf16[8,7168]{1,0:T(8,128)(2,1)S(1)} %collective-permute-done, bf16[8,7168]{1,0:T(8,128)(2,1)} %bitcast.14), kind=kLoop, calls=%fused_computation | loop fusion | flops 3670016 | bytes 1835008 | tf_op jit(solution)/shard_map/concatenate | solution.py:171
  28.7 0.1 collective-permute-start.3
  28.8 0.1 select_reduce_fusion.1
  28.9 0.7 fusion.perm_ref
  29.6 0.7 select_select_fusion.meta_ref
  30.3 0.0 collective-permute-done.4.side_ref
  30.3 0.9 %collective-permute-done.3.twin_ref = bf16[64,7168]{1,0:T(8,128)(2,1)S(1)} collective-permute-done((bf16[64,7168]{1,0:T(8,128)(2,1)S(1)}, bf16[64,7168]{1,0:T(8,128)(2,1)S(1)}, u32[]{:S(2)}, u32[]{:S(2)}) %collective-permute-start.3) | collective-permute-done | bytes 917536 | tf_op jit(solution)/shard_map/ppermute | solution.py:32
  31.2 1.0 %copy-done.2 = bf16[64,7168]{1,0:T(8,128)(2,1)} copy-done((bf16[64,7168]{1,0:T(8,128)(2,1)}, bf16[64,7168]{1,0:T(8,128)(2,1)S(1)}, u32[]{:S(2)}) %copy-start.2) | copy-done | bytes 917528
  32.2 14.9 %logits.1 = (f32[1024,128]{1,0:T(8,128)}, f32[512,128]{1,0:T(8,128)}, f32[128,128]{1,0:T(8,128)}, f32[16,128]{1,0:T(8,128)}) custom-call(bf16[64,7168]{1,0:T(8,128)(2,1)} %copy-done, bf16[64,7168]{1,0:T(8,128)(2,1)} %copy-done.2, bf16[8,7168]{1,0:T(8,128)(2,1)} %copy-done.5, bf16[1010,7168]{1,0:T(8,128)(2,1)} %table_ref.1, f32[128,128]{1,0:T(8,128)} %fusion.perm_ref, ...), custom_call_target="tpu_custom_call" | custom-call | tf_op jit(solution)/shard_map/logits/pallas_call | solution.py:188
  47.1 1.4 %broadcast_in_dim.52 = f32[32,16,128]{2,1,0:T(8,128)} broadcast(f32[16,128]{1,0:T(8,128)} %get-tuple-element.14), dimensions={1,2} | broadcast | bytes 270336 | tf_op jit(solution)/shard_map/broadcast_in_dim | solution.py:153
  48.5 7.1 %all-to-all-start = ((f32[32,16,128]{2,1,0:T(8,128)}), f32[32,16,128]{2,1,0:T(8,128)S(1)}, u32[]{:S(2)}, u32[]{:S(2)}) async-start(f32[32,16,128]{2,1,0:T(8,128)} %broadcast_in_dim.52), calls=%async_computation | async-start | bytes 524288 | tf_op jit(solution)/shard_map/all_to_all | solution.py:154
  55.6 1.8 %collective-permute-start.5 = (f32[512,128]{1,0:T(8,128)}, f32[512,128]{1,0:T(8,128)S(1)}, u32[]{:S(2)}, u32[]{:S(2)}) collective-permute-start(f32[512,128]{1,0:T(8,128)} %get-tuple-element.13), channel_id=1, source_target_pairs={{0,8},{8,0},{1,9},{9,1},{2,10},{10,2},{3,11},{11,3},{4,12},{12,4},... | collective-permute-start | bytes 786440 | tf_op jit(solution)/shard_map/ppermute | solution.py:32
  57.5 9.4 %collective-permute-done.5.peer_ref = f32[512,128]{1,0:T(8,128)S(1)} collective-permute-done((f32[512,128]{1,0:T(8,128)}, f32[512,128]{1,0:T(8,128)S(1)}, u32[]{:S(2)}, u32[]{:S(2)}) %collective-permute-start.5) | collective-permute-done | bytes 262176 | tf_op jit(solution)/shard_map/ppermute | solution.py:32
  66.9 0.0 all-to-all-done
  66.9 0.7 copy-done.4
  67.6 0.1 copy-done.1
  67.7 3.2 %gradient.1 = (f32[8,128]{1,0:T(8,128)}, f32[8,128]{1,0:T(8,128)}) custom-call(f32[1024,128]{1,0:T(8,128)} %get-tuple-element.12.logits_ref, f32[512,128]{1,0:T(8,128)} %copy-done.4, f32[2,2,8,16,128]{4,3,2,1,0:T(8,128)} %bitcast.9, f32[128,128]{1,0:T(8,128)} %fusion.perm_ref, f32[128,128]{1,0:T(8,128)} %get-tuple-element.15.gram_ref, s32[1]{0:T(128)} %bitcast.4.base_ref), custom_call_target="tpu_custom_call" | custom-call | tf_op jit(solution)/shard_map/gradient/pallas_call | solution.py:221
  70.9 1.4 %broadcast_in_dim.53 = f32[32,8,128]{2,1,0:T(8,128)} broadcast(f32[8,128]{1,0:T(8,128)} %get-tuple-element.16), dimensions={1,2} | broadcast | bytes 135168 | tf_op jit(solution)/shard_map/broadcast_in_dim | solution.py:153
  72.3 4.5 %all-to-all-start.1 = ((f32[32,8,128]{2,1,0:T(8,128)}), f32[32,8,128]{2,1,0:T(8,128)S(1)}, u32[]{:S(2)}, u32[]{:S(2)}) async-start(f32[32,8,128]{2,1,0:T(8,128)} %broadcast_in_dim.53), calls=%async_computation.1 | async-start | bytes 262144 | tf_op jit(solution)/shard_map/all_to_all | solution.py:154
  76.9 8.1 %all-to-all-done.1.recv_ref = f32[32,8,128]{2,1,0:T(8,128)S(1)} async-done(((f32[32,8,128]{2,1,0:T(8,128)}), f32[32,8,128]{2,1,0:T(8,128)S(1)}, u32[]{:S(2)}, u32[]{:S(2)}) %all-to-all-start.1) | async-done | bytes 131104 | tf_op jit(solution)/shard_map/all_to_all | solution.py:154
  84.9 0.7 copy-done.3
  85.6 1.6 %final.1 = (f32[1,128]{1,0:T(1,128)}, f32[1,1]{1,0:T(1,128)}, f32[1,1]{1,0:T(1,128)}) custom-call(f32[32,8,128]{2,1,0:T(8,128)} %copy-done.3, f32[8,128]{1,0:T(8,128)} %get-tuple-element.17.keep_ref), custom_call_target="tpu_custom_call" | custom-call | tf_op jit(solution)/shard_map/final/pallas_call | solution.py:230
  87.9 1.2 %constant_dynamic-slice_fusion = f32[1,8]{1,0:T(1,128)} fusion(f32[1,128]{1,0:T(1,128)} %get-tuple-element.18, s32[]{:T(128)S(6)} %select_n.92), kind=kLoop, calls=%fused_computation.30 | loop fusion | bytes 68 | tf_op jit(solution)/shard_map/dynamic_slice | solution.py:242
  (16 shorter events, 0.1 us)
Async XLA Ops:
  0.6 28.2 %copy-start.6 = (s32[1,8]{1,0:T(1,128)S(1)}, s32[1,8]{1,0:T(1,128)}, u32[]{:S(2)}) copy-start(s32[1,8]{1,0:T(1,128)} %param.7) | copy-start | bytes 100
  0.6 28.2 %copy-start.7 = (s32[1,8]{1,0:T(1,128)S(1)}, s32[1,8]{1,0:T(1,128)}, u32[]{:S(2)}) copy-start(s32[1,8]{1,0:T(1,128)} %param.6) | copy-start | bytes 100
  0.7 6.0 %collective-permute-start = (bf16[8,7168]{1,0:T(8,128)(2,1)}, bf16[8,7168]{1,0:T(8,128)(2,1)S(1)}, u32[]{:S(2)}, u32[]{:S(2)}) collective-permute-start(bf16[8,7168]{1,0:T(8,128)(2,1)} %bitcast.10), channel_id=1, source_target_pairs={{0,1},{1,0},{2,3},{3,2},{4,5},{5,4},{6,7},{7,6},{16,18},{17,19},{1... | collective-permute-start | bytes 344072 | tf_op jit(solution)/shard_map/ppermute | solution.py:171
  7.6 8.6 %collective-permute-start.1 = (bf16[16,7168]{1,0:T(8,128)(2,1)S(1)}, bf16[16,7168]{1,0:T(8,128)(2,1)S(1)}, u32[]{:S(2)}, u32[]{:S(2)}) collective-permute-start(bf16[16,7168]{1,0:T(8,128)(2,1)S(1)} %pad_maximum_fusion.2), channel_id=1, source_target_pairs={{0,2},{1,3},{2,0},{3,1},{4,6},{5,7},{6,4},{7,5},{16,22},{17,23},{1... | collective-permute-start | bytes 688136 | tf_op jit(solution)/shard_map/ppermute | solution.py:171
  17.1 10.6 %collective-permute-start.2 = (bf16[32,7168]{1,0:T(8,128)(2,1)S(1)}, bf16[32,7168]{1,0:T(8,128)(2,1)S(1)}, u32[]{:S(2)}, u32[]{:S(2)}) collective-permute-start(bf16[32,7168]{1,0:T(8,128)(2,1)S(1)} %pad_maximum_fusion.1), channel_id=1, source_target_pairs={{0,6},{1,7},{2,4},{3,5},{4,2},{5,3},{6,0},{7,1},{16,17},{17,16},{1... | collective-permute-start | bytes 1376264 | tf_op jit(solution)/shard_map/ppermute | solution.py:171
  21.2 9.1 %collective-permute-start.4 = (bf16[8,7168]{1,0:T(8,128)(2,1)}, bf16[8,7168]{1,0:T(8,128)(2,1)S(1)}, u32[]{:S(2)}, u32[]{:S(2)}) collective-permute-start(bf16[8,7168]{1,0:T(8,128)(2,1)} %bitcast.13), channel_id=1, source_target_pairs={{0,8},{8,0},{1,9},{9,1},{2,10},{10,2},{3,11},{11,3},{4,12},{12,4},... | collective-permute-start | bytes 344072 | tf_op jit(solution)/shard_map/ppermute | solution.py:32
  28.7 2.6 %copy-start = (bf16[64,7168]{1,0:T(8,128)(2,1)}, bf16[64,7168]{1,0:T(8,128)(2,1)S(1)}, u32[]{:S(2)}) copy-start(bf16[64,7168]{1,0:T(8,128)(2,1)S(1)} %pad_maximum_fusion.own_ref) | copy-start | bytes 2752516
  28.7 2.5 %collective-permute-start.3 = (bf16[64,7168]{1,0:T(8,128)(2,1)S(1)}, bf16[64,7168]{1,0:T(8,128)(2,1)S(1)}, u32[]{:S(2)}, u32[]{:S(2)}) collective-permute-start(bf16[64,7168]{1,0:T(8,128)(2,1)S(1)} %pad_maximum_fusion.own_ref), channel_id=1, source_target_pairs={{0,16},{16,0},{1,17},{17,1},{2,18},{18,2},{3,19},{19,3},{4,20},{20... | collective-permute-start | bytes 2752520 | tf_op jit(solution)/shard_map/ppermute | solution.py:32
  30.3 0.9 %copy-start.5 = (bf16[8,7168]{1,0:T(8,128)(2,1)}, bf16[8,7168]{1,0:T(8,128)(2,1)S(1)}, u32[]{:S(2)}) copy-start(bf16[8,7168]{1,0:T(8,128)(2,1)S(1)} %collective-permute-done.4.side_ref) | copy-start | bytes 344068
  31.2 1.0 %copy-start.2 = (bf16[64,7168]{1,0:T(8,128)(2,1)}, bf16[64,7168]{1,0:T(8,128)(2,1)S(1)}, u32[]{:S(2)}) copy-start(bf16[64,7168]{1,0:T(8,128)(2,1)S(1)} %collective-permute-done.3.twin_ref) | copy-start | bytes 2752516
  48.5 18.4 %all-to-all-start = ((f32[32,16,128]{2,1,0:T(8,128)}), f32[32,16,128]{2,1,0:T(8,128)S(1)}, u32[]{:S(2)}, u32[]{:S(2)}) async-start(f32[32,16,128]{2,1,0:T(8,128)} %broadcast_in_dim.52), calls=%async_computation | async-start | bytes 524288 | tf_op jit(solution)/shard_map/all_to_all | solution.py:154
  55.6 11.3 %collective-permute-start.5 = (f32[512,128]{1,0:T(8,128)}, f32[512,128]{1,0:T(8,128)S(1)}, u32[]{:S(2)}, u32[]{:S(2)}) collective-permute-start(f32[512,128]{1,0:T(8,128)} %get-tuple-element.13), channel_id=1, source_target_pairs={{0,8},{8,0},{1,9},{9,1},{2,10},{10,2},{3,11},{11,3},{4,12},{12,4},... | collective-permute-start | bytes 786440 | tf_op jit(solution)/shard_map/ppermute | solution.py:32
  66.9 0.7 copy-start.4
  66.9 0.8 copy-start.1
  72.3 12.6 %all-to-all-start.1 = ((f32[32,8,128]{2,1,0:T(8,128)}), f32[32,8,128]{2,1,0:T(8,128)S(1)}, u32[]{:S(2)}, u32[]{:S(2)}) async-start(f32[32,8,128]{2,1,0:T(8,128)} %broadcast_in_dim.53), calls=%async_computation.1 | async-start | bytes 262144 | tf_op jit(solution)/shard_map/all_to_all | solution.py:154
  84.9 0.7 copy-start.3

commit v2 on v1

v2 whole, which is shorter than its diff:
```python
import functools

import jax
import jax.numpy as jnp
from jax import lax
from jax.experimental import pallas as pl
from jax.experimental.pallas import tpu as pltpu
from jax.sharding import PartitionSpec as P


GROUP = ("seq", "vocab")
EVERY = ("seq", "depth", "vocab")
SCALE = 2.0**40
WEIGHTS = (1.0, 0.3)
HIGH = lax.Precision.HIGHEST
LIMIT = 24 * 2**20
PIECES = 4
VMEM = pl.BlockSpec(memory_space=pltpu.VMEM)


def exchange_masks(size):
    bits = size.bit_length() - 1
    assert size == 2**bits and bits >= 2
    return [2**bit for bit in range(bits - 1, 1, -1)] + [1, 2]


def moved(value, axis, mask):
    return lax.ppermute(value, axis, [(at, at ^ mask) for at in range(lax.axis_size(axis))])


def token_order(masks, size, count):
    total = 2 * size * count
    row = lax.broadcasted_iota(jnp.int32, (total, 1), 0)
    core = lax.axis_index("seq") ^ (row // (size * count))
    slot = (row // count) % size
    at = jnp.broadcast_to(lax.axis_index("vocab"), row.shape)
    for turn, mask in enumerate(masks):
        at = at ^ (((slot >> turn) & 1) * mask)
    return (core * size + at) * count + row % count


def rows_dot(a, b, dims, precision=None):
    return lax.dot_general(
        a, b, ((dims[:1], dims[1:]), ((), ())), precision=precision, preferred_element_type=jnp.float32
    )


def fetch_kernel(start, table_ref, copy_ref, sems):
    pieces, columns = sems.shape[0], copy_ref.shape[1]
    chunk = columns // pieces
    copies = [
        pltpu.make_async_copy(
            table_ref.at[:, pl.ds(start + at * chunk, chunk)], copy_ref.at[:, pl.ds(at * chunk, chunk)], sems.at[at]
        )
        for at in range(pieces)
    ]
    for copy in copies:
        copy.start()
    for copy in copies:
        copy.wait()


def early_kernel(own_ref, twin_ref, table_ref, logits_ref):
    states = jnp.concatenate([own_ref[...], twin_ref[...]], axis=0)
    logits_ref[: table_ref.shape[0], :] = rows_dot(table_ref[...], states, (1, 1))


def folded(block, which):
    tokens = block.shape[1]
    turned = pltpu.roll(block, tokens // 2, 1)
    first = jnp.where(which == 0, block, turned)
    second = jnp.where(which == 0, turned, block)
    lane = lax.broadcasted_iota(jnp.int32, (4, tokens), 1)
    return [
        jnp.where(lane < tokens // 2, first[at : at + 4], second[at + 4 : at + 8])
        for at in range(0, block.shape[0], 8)
    ]


def logits_kernel(
    start, width, half, size, own_ref, twin_ref, table_ref, early_ref, own_early_ref, twin_early_ref, side_ref,
    perm_ref, meta_ref, logits_ref, send_ref, gram_ref, pack_ref,
):
    early = jnp.concatenate([own_early_ref[...], twin_early_ref[...]], axis=0)
    late = jnp.concatenate([own_ref[...], twin_ref[...]], axis=0)
    gram_ref[...] = rows_dot(early, early, (1, 1)) + rows_dot(late, late, (1, 1))
    cross = rows_dot(side_ref[:, :start], early, (1, 1)) + rows_dot(side_ref[:, start:], late, (1, 1))
    logits = rows_dot(table_ref[...], late, (1, 1)) + early_ref[:width, :]
    logits_ref[:width, :] = logits
    logits_ref[width:, :] = jnp.zeros((2 * half - width, logits.shape[1]), jnp.float32)
    depth = lax.axis_index("depth")
    send_ref[...] = logits_ref[pl.ds(pl.multiple_of((1 - depth) * half, 8), half), :]
    peak = jnp.max(logits, axis=0, keepdims=True)
    total = jnp.sum(jnp.exp(logits - peak), axis=0, keepdims=True)
    rows = lax.broadcasted_iota(jnp.int32, cross.shape, 0)
    stats = jnp.where(rows == 0, peak, jnp.where(rows == 1, total, 0.0))
    stats = rows_dot(stats, perm_ref[...], (1, 0), HIGH) + meta_ref[...]
    cross = rows_dot(cross, perm_ref[...], (1, 0), HIGH)
    parts = [stats[:4]] + folded(cross, lax.axis_index("seq") ^ depth)
    for peer in range(size):
        for at, part in enumerate(parts):
            pack_ref[peer * len(parts) + at] = part


def gradient_kernel(
    width, half, sizes, logits_ref, peer_ref, recv_ref, perm_ref, gram_ref, base_ref, pack_ref, keep_ref
):
    cores, vocabs, count = sizes
    depth = lax.axis_index("depth")
    tokens = perm_ref.shape[0]
    stride = 1 + count // 8
    peers = [(core, at) for core in range(cores) for at in range(vocabs)]

    def first(core, which, at):
        return ((core * 2 + which) * vocabs + at) * stride

    def head(which):
        parts = [recv_ref[first(core, which, at)] for core, at in peers]
        peak = functools.reduce(jnp.maximum, parts)[0:1, :]
        total = sum(part[1:2, :] * jnp.exp(part[0:1, :] - peak) for part in parts)
        meta = functools.reduce(jnp.add, parts)
        live = meta[3:4, :]
        weight = jnp.where(which == 0, jnp.float32(WEIGHTS[0]), jnp.float32(WEIGHTS[1]))
        scale = live * (weight / jnp.maximum(jnp.sum(live), 1.0))
        return peak + jnp.log(total), meta[2:3, :], scale

    lse, target, scale = head(depth)
    lse_peer, target_peer, scale_peer = head(1 - depth)
    rows = lax.broadcasted_iota(jnp.int32, (8, tokens), 0)
    vectors = jnp.zeros((8, tokens), jnp.float32)
    for at, vector in enumerate((lse, target, scale, lse_peer, target_peer, scale_peer)):
        vectors = jnp.where(rows == at, vector, vectors)
    keep_ref[...] = vectors
    vectors = rows_dot(vectors, perm_ref[...], (1, 1), HIGH)

    base = base_ref[0]
    shift = pl.multiple_of(depth * half, 8)

    def gradient(logits, at, start):
        row = lax.broadcasted_iota(jnp.int32, logits.shape, 0) + start
        hit = (row + base) == vectors[at + 1 : at + 2, :].astype(jnp.int32)
        soft = jnp.exp(logits - vectors[at : at + 1, :]) - jnp.where(hit, 1.0, 0.0)
        grad = (vectors[at + 2 : at + 3, :] * SCALE) * soft
        return hit & (row < width), jnp.where(row < width, grad, 0.0).astype(jnp.bfloat16)

    logits = logits_ref[...]
    hit, grad = gradient(logits, 0, 0)
    chosen = jnp.sum(jnp.where(hit, logits, 0.0), axis=0, keepdims=True)
    _, mine = gradient(logits_ref[pl.ds(shift, half), :], 0, shift)
    _, grad_peer = gradient(peer_ref[...], 3, shift)
    inner = rows_dot(grad, grad, (0, 0))
    cross = rows_dot(grad_peer, mine, (0, 0))
    cross = rows_dot(perm_ref[...], cross, (0, 0), HIGH)
    cross = rows_dot(cross, perm_ref[...], (1, 0), HIGH)
    square = inner * gram_ref[...]
    flat = jnp.transpose(cross)
    lines = []
    for core in range(cores):
        for matrix, which in ((cross, depth), (flat, 1 - depth)):
            start = core * vocabs * count
            blocks = folded(matrix[start : start + vocabs * count], which ^ core)
            for at in range(vocabs):
                for part in range(count // 8):
                    tile = recv_ref[first(core, which, at) + 1 + part]
                    lines.append(blocks[at * (count // 8) + part] * tile)
    square = jnp.sum(square, axis=0, keepdims=True) + 2.0 * jnp.sum(sum(lines), axis=0, keepdims=True)
    chosen = rows_dot(jnp.broadcast_to(chosen, (8, tokens)), perm_ref[...], (1, 0), HIGH)
    pack = jnp.where(rows == depth, chosen, jnp.where(rows == 2, square, 0.0))[:4]
    for peer in range(2 * len(peers)):
        pack_ref[peer] = pack


def final_kernel(sizes, recv_ref, keep_ref, nll_ref, loss_ref, norm_ref):
    _, vocabs, count = sizes
    depth = lax.axis_index("depth")
    total = jnp.sum(recv_ref[...], axis=0)
    keep = keep_ref[...]
    own = jnp.where(depth == 0, total[0:1, :], total[1:2, :])
    peer = jnp.where(depth == 0, total[1:2, :], total[0:1, :])
    nll = keep[0:1, :] - own
    parts = keep[2:3, :] * nll + keep[5:6, :] * (keep[3:4, :] - peer)
    loss_ref[...] = jnp.sum(parts, axis=1, keepdims=True)
    square = jnp.maximum(jnp.sum(total[2:3, :], axis=1, keepdims=True), 0.0)
    norm_ref[...] = jnp.sqrt(square) * (1.0 / SCALE)
    tokens = nll.shape[1]
    place = lax.axis_index("seq") * vocabs + lax.axis_index("vocab")
    turned = pltpu.roll(jnp.broadcast_to(nll, (8, tokens)), tokens - place * count, 1)
    nll_ref[...] = turned[:1, :count]


def program(hidden, embedding, targets, mask):
    cores, depths, vocabs = (lax.axis_size(axis) for axis in EVERY)
    count, dim = hidden.shape[1:]
    assert cores == 2 and depths == 2 and count % 8 == 0 and dim % (256 * PIECES) == 0
    width = embedding.shape[0]
    half = -(-width // 16) * 8
    tokens = cores * vocabs * count
    size = cores * depths * vocabs
    masks = exchange_masks(vocabs)
    place = lax.axis_index(GROUP)
    sizes = (cores, vocabs, count)
    f32 = jnp.float32
    split = dim // 2

    own = hidden[0]
    left, right = own[:, :split], own[:, split:]
    for mask_far in masks[:-2]:
        left = jnp.concatenate([left, moved(left, "vocab", mask_far)], axis=0)
        right = jnp.concatenate([right, moved(right, "vocab", mask_far)], axis=0)
    rows = left.shape[0]
    left = jnp.concatenate([left, moved(left, "vocab", masks[-2])], axis=0)
    near = moved(right, "vocab", masks[-1])
    right = jnp.concatenate([right, near], axis=0)
    left = jnp.concatenate([left, moved(left, "vocab", masks[-1])], axis=0)
    last = moved(right, "vocab", masks[-2])
    right = jnp.concatenate([right[:rows], last[:rows], near, last[rows:]], axis=0)
    left, own = lax.optimization_barrier((left, own))
    left_twin = moved(left, "seq", 1)
    side = moved(own, "depth", 1)
    right_twin = moved(right, "seq", 1)

    order = token_order(masks, vocabs, count)
    column = lax.broadcasted_iota(jnp.int32, (tokens, tokens), 1)
    perm = (order == column).astype(f32)
    lane = lax.broadcasted_iota(jnp.int32, (count, tokens), 1)
    spot = (lane == place * count + lax.broadcasted_iota(jnp.int32, (count, tokens), 0)).astype(f32)
    placed = [jnp.sum(spot * value[0][:, None].astype(f32), axis=0) for value in (targets, mask)]
    line = lax.broadcasted_iota(jnp.int32, (count, tokens), 0)
    meta = jnp.where(line == 2, placed[0][None, :], jnp.where(line == 3, placed[1][None, :], 0.0))

    shape = lambda *dims: jax.ShapeDtypeStruct(dims, f32)
    params = pltpu.CompilerParams(vmem_limit_bytes=LIMIT)
    tables = []
    for start in (0, split):
        tables.append(
            pl.pallas_call(
                functools.partial(fetch_kernel, start),
                in_specs=[pl.BlockSpec(memory_space=pltpu.HBM)],
                out_specs=VMEM,
                out_shape=pltpu.VMEM((width, split), embedding.dtype),
                scratch_shapes=[pltpu.SemaphoreType.DMA((PIECES,))],
                compiler_params=pltpu.CompilerParams(vmem_limit_bytes=46 * 2**20),
                cost_estimate=pl.CostEstimate(flops=0, transcendentals=0, bytes_accessed=4 * width * split),
            )(embedding)
        )
    tables = [pltpu.with_memory_space_constraint(table, pltpu.VMEM) for table in tables]
    early = pl.pallas_call(
        early_kernel,
        in_specs=[VMEM] * 3,
        out_specs=VMEM,
        out_shape=shape(2 * half, tokens),
        compiler_params=params,
        name="early",
    )(left, left_twin, tables[0])
    logits, send, gram, pack = pl.pallas_call(
        functools.partial(logits_kernel, split, width, half, size),
        in_specs=[VMEM] * 9,
        out_specs=[VMEM] * 4,
        out_shape=[
            shape(2 * half, tokens),
            shape(half, tokens),
            shape(tokens, tokens),
            shape(size * (1 + count // 8), 4, tokens),
        ],
        compiler_params=params,
        name="logits",
    )(right, right_twin, tables[1], early, left, left_twin, side, perm, meta)

    peer = moved(send, "depth", 1)
    recv = lax.all_to_all(pack, EVERY, 0, 0, tiled=True)
    base = (place * width).astype(jnp.int32).reshape(1)
    pack, keep = pl.pallas_call(
        functools.partial(gradient_kernel, width, half, sizes),
        in_specs=[VMEM] * 5 + [pl.BlockSpec(memory_space=pltpu.SMEM)],
        out_specs=[VMEM] * 2,
        out_shape=[shape(size, 4, tokens), shape(8, tokens)],
        compiler_params=params,
        name="gradient",
    )(logits, peer, recv, perm, gram, base)
    recv = lax.all_to_all(pack, EVERY, 0, 0, tiled=True)
    nll, loss, norm = pl.pallas_call(
        functools.partial(final_kernel, sizes),
        in_specs=[VMEM] * 2,
        out_specs=[VMEM] * 3,
        out_shape=[shape(1, count), shape(1, 1), shape(1, 1)],
        compiler_params=params,
        name="final",
    )(recv, keep)
    return (nll, loss[0, 0], norm[0, 0])


def solution(mesh):
    placed = (
        P("depth", GROUP, None),
        P(GROUP, None),
        P("depth", GROUP),
        P("depth", GROUP),
    )
    return jax.shard_map(
        program,
        mesh=mesh,
        in_specs=placed,
        out_specs=(P("depth", GROUP), P(), P()),
        check_vma=False,
    )
```

time: 90.9 us -> 66.4 us (0.73)
  waiting for transfers between devices: 32.9 us -> 19.2 us
  blocking collectives: 0 us -> 9.25 us
  local copies, waits for them, and re-layouts: 6.42 us -> 0.9 us
  Pallas kernels: 19.7 us -> 15 us
  starting transfers between devices: 24.3 us -> 19.9 us
  other arithmetic: 4.29 us -> 1.03 us
  between operations: 2.57 us -> 0.76 us
    ppermute x6 -> x10, waiting for transfers between devices: 24.9 us -> 11.2 us  [moved(): lax.ppermute(value, axis, [(at, at ^ mask) for at in range(lax.axis_size(...]
    all_to_all x0 -> x1, blocking collectives: none -> 9.25 us  [program(): recv = lax.all_to_all(pack, EVERY, 0, 0, tiled=True)]
    all_to_all x2 -> x1, starting transfers between devices: 11.6 us -> 4.97 us  [program(): recv = lax.all_to_all(pack, EVERY, 0, 0, tiled=True)]
    pallas_call x3 -> x6, Pallas kernels: 19.7 us -> 15 us  [the longest x2 6.41 us: program(): pl.pallas_call(functools.partial(fetch_kernel, start), in_specs=[pl.Block...]
    broadcast_in_dim x2 -> x0, local copies, waits for them, and re-layouts: 2.76 us -> none  [everyone(): spread = jnp.broadcast_to(value[None], (size,) + value.shape)]
    concatenate x3 -> x5, other arithmetic: 2.8 us -> 0.09 us  [the longest x1 0.04 us: program(): left = jnp.concatenate([left, moved(left, 'vocab', masks[-1])], axis=0)]
    unnamed x16 -> x5, local copies, waits for them, and re-layouts: 2.47 us -> 0.03 us
    ppermute x6 -> x10, starting transfers between devices: 12.6 us -> 14.9 us  [moved(): lax.ppermute(value, axis, [(at, at ^ mask) for at in range(lax.axis_size(...]
  transfers between devices with their start and end apart: 8 -> 11, of which waited for: 6 -> 7; matrix products, arithmetic and copies ran while one was open for 3% -> 2% of each run, Pallas kernels for 0% -> 13%
where the time goes in v2:
time: 66.4 us; the launch traced here: 66.1 us
  starting transfers between devices  19.9 us (30%)
  waiting for transfers between devices  19.2 us (29%)
  Pallas kernels  15 us (23%)
  blocking collectives  9.25 us (14%)
  other arithmetic  1.03 us (2%)
  local copies, waits for them, and re-layouts  0.9 us (1%)
  between operations  0.76 us (1%)
    ppermute x10, starting transfers between devices, moved(): lax.ppermute(value, axis, [(at, at ^ mask) for at in range(lax.axis_size(...  14.9 us
    ppermute x10, waiting for transfers between devices, moved(): lax.ppermute(value, axis, [(at, at ^ mask) for at in range(lax.axis_size(...  11.2 us
    all_to_all x1, blocking collectives, program(): recv = lax.all_to_all(pack, EVERY, 0, 0, tiled=True)  9.25 us
    all_to_all x1, waiting for transfers between devices, program(): recv = lax.all_to_all(pack, EVERY, 0, 0, tiled=True)  8.06 us
    pallas_call x2, Pallas kernels, program(): pl.pallas_call(functools.partial(fetch_kernel, start), in_specs=[pl.Block...  6.41 us
    all_to_all x1, starting transfers between devices, program(): recv = lax.all_to_all(pack, EVERY, 0, 0, tiled=True)  4.97 us
    pallas_call x1, Pallas kernels, program(): pl.pallas_call(functools.partial(logits_kernel, split, width, half, size)...  4.3 us
    pallas_call x1, Pallas kernels, program(): pl.pallas_call(early_kernel, in_specs=[VMEM] * 3, out_specs=VMEM, out_sha...  2.05 us
  transfers between devices with their start and end apart: 11, of which 7 were waited for; matrix products, arithmetic and copies ran while one was open for 2% of the time, Pallas kernels for 13%

profile of v2, /device:TPU:0, one launch (start us, length us, event | category | flops | bytes accessed | tf_op | source)
XLA Modules:
  0.0 66.1 jit_solution(1498984346177064909)
XLA Ops:
  0.6 0.9 %fusion.7 = (bf16[8,3584]{1,0:T(8,128)(2,1)S(1)}, bf16[64,3584]{1,0:T(8,128)(2,1)S(1)}, bf16[8,3584]{1,0:T(8,128)(2,1)S(1)}) fusion(bf16[8,7168]{1,0:T(8,128)(2,1)} %bitcast.8), kind=kLoop, calls=%fused_computation.38 | loop fusion | bytes 286720 | tf_op jit(solution)/shard_map/slice | solution.py:206
  1.5 4.1 %collective-permute-start = (bf16[8,3584]{1,0:T(8,128)(2,1)S(1)}, bf16[8,3584]{1,0:T(8,128)(2,1)S(1)}, u32[]{:S(2)}, u32[]{:S(2)}) collective-permute-start(bf16[8,3584]{1,0:T(8,128)(2,1)S(1)} %get-tuple-element.29), channel_id=1, source_target_pairs={{0,4},{1,5},{2,6},{3,7},{4,0},{5,1},{6,2},{7,3},{8,12},{9,13},{10,... | collective-permute-start | bytes 172040 | tf_op jit(solution)/shard_map/ppermute | solution.py:28
  5.6 0.1 collective-permute-start.4
  5.7 0.7 %convert_bitcast_fusion = (f32[8]{0:T(128)S(1)}, f32[8]{0:T(128)S(1)}) fusion(s32[1,8]{1,0:T(1,128)} %param.7, s32[1,8]{1,0:T(1,128)} %param.6), kind=kLoop, calls=%fused_computation.33 | loop fusion | flops 16 | bytes 128 | tf_op jit(solution)/shard_map/convert_element_type | solution.py:227
  6.4 0.1 select_reduce_fusion.1
  6.5 1.9 %collective-permute-done = bf16[8,3584]{1,0:T(8,128)(2,1)S(1)} collective-permute-done((bf16[8,3584]{1,0:T(8,128)(2,1)S(1)}, bf16[8,3584]{1,0:T(8,128)(2,1)S(1)}, u32[]{:S(2)}, u32[]{:S(2)}) %collective-permute-start) | collective-permute-done | bytes 57376 | tf_op jit(solution)/shard_map/ppermute | solution.py:28
  8.4 2.5 %collective-permute-start.1 = (bf16[16,3584]{1,0:T(8,128)(2,1)S(1)}, bf16[16,3584]{1,0:T(8,128)(2,1)S(1)}, u32[]{:S(2)}, u32[]{:S(2)}) collective-permute-start(bf16[16,3584]{1,0:T(8,128)(2,1)S(1)} %pad_maximum_fusion.3), channel_id=1, source_target_pairs={{0,2},{1,3},{2,0},{3,1},{4,6},{5,7},{6,4},{7,5},{8,10},{9,11},{10,... | collective-permute-start | bytes 344072 | tf_op jit(solution)/shard_map/ppermute | solution.py:28
  10.9 0.1 collective-permute-done.4
  11.0 1.7 %collective-permute-start.5 = (bf16[16,3584]{1,0:T(8,128)(2,1)S(1)}, bf16[16,3584]{1,0:T(8,128)(2,1)S(1)}, u32[]{:S(2)}, u32[]{:S(2)}) collective-permute-start(bf16[16,3584]{1,0:T(8,128)(2,1)S(1)} %pad_maximum_fusion.4), channel_id=1, source_target_pairs={{0,1},{1,0},{2,3},{3,2},{4,5},{5,4},{6,7},{7,6},{8,9},{9,8},{10,11... | collective-permute-start | bytes 344072 | tf_op jit(solution)/shard_map/ppermute | solution.py:28
  12.7 3.2 %collective-permute-done.5 = bf16[16,3584]{1,0:T(8,128)(2,1)S(1)} collective-permute-done((bf16[16,3584]{1,0:T(8,128)(2,1)S(1)}, bf16[16,3584]{1,0:T(8,128)(2,1)S(1)}, u32[]{:S(2)}, u32[]{:S(2)}) %collective-permute-start.5) | collective-permute-done | bytes 114720 | tf_op jit(solution)/shard_map/ppermute | solution.py:28
  15.9 1.4 %collective-permute-start.6 = (bf16[32,3584]{1,0:T(8,128)(2,1)S(1)}, bf16[32,3584]{1,0:T(8,128)(2,1)S(1)}, u32[]{:S(2)}, u32[]{:S(2)}) collective-permute-start(bf16[32,3584]{1,0:T(8,128)(2,1)S(1)} %pad_maximum_fusion.2), channel_id=1, source_target_pairs={{0,2},{1,3},{2,0},{3,1},{4,6},{5,7},{6,4},{7,5},{8,10},{9,11},{10,... | collective-permute-start | bytes 688136 | tf_op jit(solution)/shard_map/ppermute | solution.py:28
  17.2 0.0 collective-permute-done.1
  17.3 1.6 %collective-permute-start.2 = (bf16[32,3584]{1,0:T(8,128)(2,1)S(1)}, bf16[32,3584]{1,0:T(8,128)(2,1)S(1)}, u32[]{:S(2)}, u32[]{:S(2)}) collective-permute-start(bf16[32,3584]{1,0:T(8,128)(2,1)S(1)} %pad_maximum_fusion.1), channel_id=1, source_target_pairs={{0,1},{1,0},{2,3},{3,2},{4,5},{5,4},{6,7},{7,6},{8,9},{9,8},{10,11... | collective-permute-start | bytes 688136 | tf_op jit(solution)/shard_map/ppermute | solution.py:28
  18.8 3.1 %collective-permute-done.6 = bf16[32,3584]{1,0:T(8,128)(2,1)S(1)} collective-permute-done((bf16[32,3584]{1,0:T(8,128)(2,1)S(1)}, bf16[32,3584]{1,0:T(8,128)(2,1)S(1)}, u32[]{:S(2)}, u32[]{:S(2)}) %collective-permute-start.6) | collective-permute-done | bytes 229408 | tf_op jit(solution)/shard_map/ppermute | solution.py:28
  22.0 1.4 %collective-permute-done.2 = bf16[32,3584]{1,0:T(8,128)(2,1)S(1)} collective-permute-done((bf16[32,3584]{1,0:T(8,128)(2,1)S(1)}, bf16[32,3584]{1,0:T(8,128)(2,1)S(1)}, u32[]{:S(2)}, u32[]{:S(2)}) %collective-permute-start.2) | collective-permute-done | bytes 229408 | tf_op jit(solution)/shard_map/ppermute | solution.py:28
  23.4 0.1 collective-permute-start.3
  23.5 0.5 collective-permute-start.7
  24.0 3.2 %shard_map.68.table_ref = bf16[1010,3584]{1,0:T(8,128)(2,1)S(1)} custom-call(bf16[1010,7168]{1,0:T(8,128)(2,1)} %table_ref.3), custom_call_target="tpu_custom_call" | custom-call | bytes 14479360 | tf_op jit(solution)/shard_map/pallas_call | solution.py:236
  27.2 0.0 copy-start
  27.2 3.2 %shard_map.67.table_ref = bf16[1010,3584]{1,0:T(8,128)(2,1)S(1)} custom-call(bf16[1010,7168]{1,0:T(8,128)(2,1)} %table_ref.3), custom_call_target="tpu_custom_call" | custom-call | bytes 14479360 | tf_op jit(solution)/shard_map/pallas_call | solution.py:236
  30.5 0.1 fusion.perm_ref
  30.6 1.6 %collective-permute-start.8 = (bf16[8,7168]{1,0:T(8,128)(2,1)S(1)}, bf16[8,7168]{1,0:T(8,128)(2,1)S(1)}, u32[]{:S(2)}, u32[]{:S(2)}) collective-permute-start(bf16[8,7168]{1,0:T(8,128)(2,1)S(1)} %bitcast.9), channel_id=1, source_target_pairs={{0,8},{8,0},{1,9},{9,1},{2,10},{10,2},{3,11},{11,3},{4,12},{12,4},... | collective-permute-start | bytes 344072 | tf_op jit(solution)/shard_map/ppermute | solution.py:28
  32.1 0.1 select_select_fusion.meta_ref
  32.2 2.0 %early.1.early_ref = f32[1024,128]{1,0:T(8,128)S(1)} custom-call(bf16[64,3584]{1,0:T(8,128)(2,1)S(1)} %pad_maximum_fusion.own_ref.own_early_ref, bf16[64,3584]{1,0:T(8,128)(2,1)S(1)} %collective-permute-done.7.twin_ref.twin_early_ref, bf16[1010,3584]{1,0:T(8,128)(2,1)S(1)} %shard_map.68.table_ref), custom_call_target="tpu_custom_call" | custom-call | tf_op jit(solution)/shard_map/early/pallas_call | solution.py:247
  34.3 1.5 %collective-permute-done.8.side_ref = bf16[8,7168]{1,0:T(8,128)(2,1)S(1)} collective-permute-done((bf16[8,7168]{1,0:T(8,128)(2,1)S(1)}, bf16[8,7168]{1,0:T(8,128)(2,1)S(1)}, u32[]{:S(2)}, u32[]{:S(2)}) %collective-permute-start.8) | collective-permute-done | bytes 114720 | tf_op jit(solution)/shard_map/ppermute | solution.py:28
  35.8 4.3 %logits.1 = (f32[1024,128]{1,0:T(8,128)S(1)}, f32[512,128]{1,0:T(8,128)S(1)}, f32[128,128]{1,0:T(8,128)S(1)}, f32[64,4,128]{2,1,0:T(4,128)}) custom-call(bf16[64,3584]{1,0:T(8,128)(2,1)S(1)} %slice_dynamic-update-slice_fusion.own_ref, bf16[64,3584]{1,0:T(8,128)(2,1)S(1)} %collective-permute-done.3.twin_ref, bf16[1010,3584]{1,0:T(8,128)(2,1)S(1)} %shard_map.67.table_ref, ...), custom_call_target="tpu_custom_call" | custom-call | tf_op jit(solution)/shard_map/logits/pallas_call | solution.py:255
  40.1 1.5 %collective-permute-start.9 = (f32[512,128]{1,0:T(8,128)S(1)}, f32[512,128]{1,0:T(8,128)S(1)}, u32[]{:S(2)}, u32[]{:S(2)}) collective-permute-start(f32[512,128]{1,0:T(8,128)S(1)} %get-tuple-element.17), channel_id=1, source_target_pairs={{0,8},{8,0},{1,9},{9,1},{2,10},{10,2},{3,11},{11,3},{4,12},{12,4},... | collective-permute-start | bytes 786440 | tf_op jit(solution)/shard_map/ppermute | solution.py:28
  41.6 5.0 %all-to-all-start = ((f32[64,4,128]{2,1,0:T(4,128)}), f32[64,4,128]{2,1,0:T(4,128)S(1)}, u32[]{:S(2)}, u32[]{:S(2)}) async-start(f32[64,4,128]{2,1,0:T(4,128)} %get-tuple-element.18), calls=%async_computation | async-start | bytes 262144 | tf_op jit(solution)/shard_map/all_to_all | solution.py:270
  46.5 8.1 %all-to-all-done.recv_ref = f32[64,4,128]{2,1,0:T(4,128)S(1)} async-done(((f32[64,4,128]{2,1,0:T(4,128)}), f32[64,4,128]{2,1,0:T(4,128)S(1)}, u32[]{:S(2)}, u32[]{:S(2)}) %all-to-all-start) | async-done | bytes 131104 | tf_op jit(solution)/shard_map/all_to_all | solution.py:270
  54.6 1.6 %gradient.1 = (f32[32,4,128]{2,1,0:T(4,128)S(1)}, f32[8,128]{1,0:T(8,128)S(1)}) custom-call(f32[1024,128]{1,0:T(8,128)S(1)} %get-tuple-element.16.logits_ref, f32[512,128]{1,0:T(8,128)S(1)} %collective-permute-done.9.peer_ref, f32[64,4,128]{2,1,0:T(4,128)S(1)} %all-to-all-done.recv_ref, f32[128,128]{1,0:T(8,128)S(1)} %fusion.perm_ref, ...), custom_call_target="tpu_custom_call" | custom-call | tf_op jit(solution)/shard_map/gradient/pallas_call | solution.py:272
  56.2 9.2 %all_to_all.10.recv_ref = f32[32,4,128]{2,1,0:T(4,128)S(1)} all-to-all(f32[32,4,128]{2,1,0:T(4,128)S(1)} %get-tuple-element.20), channel_id=1, replica_groups=mesh['seq'=2,'depth'=2,'vocab'=8] {'seq','depth','vocab'}, dimensions={0} | all-to-all | bytes 131072 | tf_op jit(solution)/shard_map/all_to_all | solution.py:280
  65.5 0.6 final.1
  (16 shorter events, 0.2 us)
Async XLA Ops:
  1.5 6.9 %collective-permute-start = (bf16[8,3584]{1,0:T(8,128)(2,1)S(1)}, bf16[8,3584]{1,0:T(8,128)(2,1)S(1)}, u32[]{:S(2)}, u32[]{:S(2)}) collective-permute-start(bf16[8,3584]{1,0:T(8,128)(2,1)S(1)} %get-tuple-element.29), channel_id=1, source_target_pairs={{0,4},{1,5},{2,6},{3,7},{4,0},{5,1},{6,2},{7,3},{8,12},{9,13},{10,... | collective-permute-start | bytes 172040 | tf_op jit(solution)/shard_map/ppermute | solution.py:28
  5.6 5.3 %collective-permute-start.4 = (bf16[8,3584]{1,0:T(8,128)(2,1)S(1)}, bf16[8,3584]{1,0:T(8,128)(2,1)S(1)}, u32[]{:S(2)}, u32[]{:S(2)}) collective-permute-start(bf16[8,3584]{1,0:T(8,128)(2,1)S(1)} %get-tuple-element.27), channel_id=1, source_target_pairs={{0,4},{1,5},{2,6},{3,7},{4,0},{5,1},{6,2},{7,3},{8,12},{9,13},{10,... | collective-permute-start | bytes 172040 | tf_op jit(solution)/shard_map/ppermute | solution.py:28
  8.4 8.8 %collective-permute-start.1 = (bf16[16,3584]{1,0:T(8,128)(2,1)S(1)}, bf16[16,3584]{1,0:T(8,128)(2,1)S(1)}, u32[]{:S(2)}, u32[]{:S(2)}) collective-permute-start(bf16[16,3584]{1,0:T(8,128)(2,1)S(1)} %pad_maximum_fusion.3), channel_id=1, source_target_pairs={{0,2},{1,3},{2,0},{3,1},{4,6},{5,7},{6,4},{7,5},{8,10},{9,11},{10,... | collective-permute-start | bytes 344072 | tf_op jit(solution)/shard_map/ppermute | solution.py:28
  11.0 4.9 %collective-permute-start.5 = (bf16[16,3584]{1,0:T(8,128)(2,1)S(1)}, bf16[16,3584]{1,0:T(8,128)(2,1)S(1)}, u32[]{:S(2)}, u32[]{:S(2)}) collective-permute-start(bf16[16,3584]{1,0:T(8,128)(2,1)S(1)} %pad_maximum_fusion.4), channel_id=1, source_target_pairs={{0,1},{1,0},{2,3},{3,2},{4,5},{5,4},{6,7},{7,6},{8,9},{9,8},{10,11... | collective-permute-start | bytes 344072 | tf_op jit(solution)/shard_map/ppermute | solution.py:28
  15.9 6.1 %collective-permute-start.6 = (bf16[32,3584]{1,0:T(8,128)(2,1)S(1)}, bf16[32,3584]{1,0:T(8,128)(2,1)S(1)}, u32[]{:S(2)}, u32[]{:S(2)}) collective-permute-start(bf16[32,3584]{1,0:T(8,128)(2,1)S(1)} %pad_maximum_fusion.2), channel_id=1, source_target_pairs={{0,2},{1,3},{2,0},{3,1},{4,6},{5,7},{6,4},{7,5},{8,10},{9,11},{10,... | collective-permute-start | bytes 688136 | tf_op jit(solution)/shard_map/ppermute | solution.py:28
  17.3 6.1 %collective-permute-start.2 = (bf16[32,3584]{1,0:T(8,128)(2,1)S(1)}, bf16[32,3584]{1,0:T(8,128)(2,1)S(1)}, u32[]{:S(2)}, u32[]{:S(2)}) collective-permute-start(bf16[32,3584]{1,0:T(8,128)(2,1)S(1)} %pad_maximum_fusion.1), channel_id=1, source_target_pairs={{0,1},{1,0},{2,3},{3,2},{4,5},{5,4},{6,7},{7,6},{8,9},{9,8},{10,11... | collective-permute-start | bytes 688136 | tf_op jit(solution)/shard_map/ppermute | solution.py:28
  23.4 12.3 %collective-permute-start.3 = (bf16[64,3584]{1,0:T(8,128)(2,1)S(1)}, bf16[64,3584]{1,0:T(8,128)(2,1)S(1)}, u32[]{:S(2)}, u32[]{:S(2)}) collective-permute-start(bf16[64,3584]{1,0:T(8,128)(2,1)S(1)} %slice_dynamic-update-slice_fusion.own_ref), channel_id=1, source_target_pairs={{0,16},{16,0},{1,17},{17,1},{2,18},{18,2},{3,19},{19,3},{4,20},{20... | collective-permute-start | bytes 1376264 | tf_op jit(solution)/shard_map/ppermute | solution.py:28
  23.5 8.7 %collective-permute-start.7 = (bf16[64,3584]{1,0:T(8,128)(2,1)S(1)}, bf16[64,3584]{1,0:T(8,128)(2,1)S(1)}, u32[]{:S(2)}, u32[]{:S(2)}) collective-permute-start(bf16[64,3584]{1,0:T(8,128)(2,1)S(1)} %pad_maximum_fusion.own_ref.own_early_ref), channel_id=1, source_target_pairs={{0,16},{16,0},{1,17},{17,1},{2,18},{18,2},{3,19},{19,3},{4,20},{20... | collective-permute-start | bytes 1376264 | tf_op jit(solution)/shard_map/ppermute | solution.py:28
  27.2 3.3 %copy-start = (bf16[1,8,7168]{2,1,0:T(8,128)(2,1)S(1)}, bf16[1,8,7168]{2,1,0:T(8,128)(2,1)}, u32[]{:S(2)}) copy-start(bf16[1,8,7168]{2,1,0:T(8,128)(2,1)} %param.4) | copy-start | bytes 344068
  30.6 5.2 %collective-permute-start.8 = (bf16[8,7168]{1,0:T(8,128)(2,1)S(1)}, bf16[8,7168]{1,0:T(8,128)(2,1)S(1)}, u32[]{:S(2)}, u32[]{:S(2)}) collective-permute-start(bf16[8,7168]{1,0:T(8,128)(2,1)S(1)} %bitcast.9), channel_id=1, source_target_pairs={{0,8},{8,0},{1,9},{9,1},{2,10},{10,2},{3,11},{11,3},{4,12},{12,4},... | collective-permute-start | bytes 344072 | tf_op jit(solution)/shard_map/ppermute | solution.py:28
  40.1 14.5 %collective-permute-start.9 = (f32[512,128]{1,0:T(8,128)S(1)}, f32[512,128]{1,0:T(8,128)S(1)}, u32[]{:S(2)}, u32[]{:S(2)}) collective-permute-start(f32[512,128]{1,0:T(8,128)S(1)} %get-tuple-element.17), channel_id=1, source_target_pairs={{0,8},{8,0},{1,9},{9,1},{2,10},{10,2},{3,11},{11,3},{4,12},{12,4},... | collective-permute-start | bytes 786440 | tf_op jit(solution)/shard_map/ppermute | solution.py:28
  41.6 13.0 %all-to-all-start = ((f32[64,4,128]{2,1,0:T(4,128)}), f32[64,4,128]{2,1,0:T(4,128)S(1)}, u32[]{:S(2)}, u32[]{:S(2)}) async-start(f32[64,4,128]{2,1,0:T(4,128)} %get-tuple-element.18), calls=%async_computation | async-start | bytes 262144 | tf_op jit(solution)/shard_map/all_to_all | solution.py:270

commit v3 on v2

v3 whole, which is shorter than its diff:
```python
import functools

import jax
import jax.numpy as jnp
from jax import lax
from jax.experimental import pallas as pl
from jax.experimental.pallas import tpu as pltpu
from jax.sharding import PartitionSpec as P


GROUP = ("seq", "vocab")
EVERY = ("seq", "depth", "vocab")
SCALE = 2.0**40
WEIGHTS = (1.0, 0.3)
LIMIT = 24 * 2**20
PIECES = 2
LEAN = -256
VMEM = pl.BlockSpec(memory_space=pltpu.VMEM)


def exchange_masks(size):
    bits = size.bit_length() - 1
    assert size == 2**bits and bits >= 2
    return [2**bit for bit in range(bits - 1, 1, -1)] + [1, 2]


def moved(value, axis, mask):
    return lax.ppermute(value, axis, [(at, at ^ mask) for at in range(lax.axis_size(axis))])


def joined(value, other, mask):
    later = (lax.axis_index("vocab") & mask) != 0
    return jnp.concatenate([jnp.where(later, other, value), jnp.where(later, value, other)], axis=0)


def slot_of(masks):
    at = lax.axis_index("vocab")
    return sum(jnp.where((at & mask) != 0, 1, 0) << turn for turn, mask in enumerate(masks))


def rows_dot(a, b, dims):
    return lax.dot_general(a, b, ((dims[:1], dims[1:]), ((), ())), preferred_element_type=jnp.float32)


def fetch_kernel(start, table_ref, copy_ref, sems):
    pieces, columns = sems.shape[0], copy_ref.shape[1]
    chunk = columns // pieces
    copies = [
        pltpu.make_async_copy(
            table_ref.at[:, pl.ds(start + at * chunk, chunk)], copy_ref.at[:, pl.ds(at * chunk, chunk)], sems.at[at]
        )
        for at in range(pieces)
    ]
    for copy in copies:
        copy.start()
    for copy in copies:
        copy.wait()


def merged(own_ref, twin_ref):
    first = lax.axis_index("seq") == 0
    own, twin = own_ref[...], twin_ref[...]
    return jnp.concatenate([jnp.where(first, own, twin), jnp.where(first, twin, own)], axis=0)


def early_kernel(own_ref, twin_ref, table_ref, logits_ref, gram_ref, states_ref):
    states = merged(own_ref, twin_ref)
    states_ref[...] = states
    logits_ref[: table_ref.shape[0], :] = rows_dot(table_ref[...], states, (1, 1))
    gram_ref[...] = rows_dot(states, states, (1, 1))


def folded(block, which):
    tokens = block.shape[1]
    turned = pltpu.roll(block, tokens // 2, 1)
    first = jnp.where(which == 0, block, turned)
    second = jnp.where(which == 0, turned, block)
    lane = lax.broadcasted_iota(jnp.int32, (4, tokens), 1)
    return [
        jnp.where(lane < tokens // 2, first[at : at + 4], second[at + 4 : at + 8])
        for at in range(0, block.shape[0], 8)
    ]


def logits_kernel(
    width, half, size, own_ref, twin_ref, table_ref, early_ref, gram_early_ref, states_ref, side_ref, meta_ref,
    logits_ref, send_ref, gram_ref, pack_ref,
):
    early = states_ref[...]
    late = merged(own_ref, twin_ref)
    start = early.shape[1]
    logits = rows_dot(table_ref[...], late, (1, 1)) + early_ref[:width, :]
    logits_ref[:width, :] = logits
    logits_ref[width:, :] = jnp.zeros((2 * half - width, logits.shape[1]), jnp.float32)
    gram_ref[...] = gram_early_ref[...] + rows_dot(late, late, (1, 1))
    cross = rows_dot(side_ref[:, :start], early, (1, 1)) + rows_dot(side_ref[:, start:], late, (1, 1))
    depth = lax.axis_index("depth")
    send_ref[...] = logits_ref[pl.ds(pl.multiple_of((1 - depth) * half, 8), half), :]
    peak = jnp.max(logits, axis=0, keepdims=True)
    total = jnp.sum(jnp.exp(logits - peak), axis=0, keepdims=True)
    rows = lax.broadcasted_iota(jnp.int32, meta_ref.shape, 0)
    stats = jnp.where(rows == 0, peak, jnp.where(rows == 1, total, meta_ref[...]))
    parts = [stats] + folded(cross, lax.axis_index("seq") ^ depth)
    for peer in range(size):
        for at, part in enumerate(parts):
            pack_ref[peer * len(parts) + at] = part


def gradient_kernel(
    masks, width, half, sizes, logits_ref, peer_ref, recv_ref, gram_ref, base_ref, pack_ref, keep_ref
):
    cores, vocabs, count = sizes
    depth = lax.axis_index("depth")
    tokens = gram_ref.shape[0]
    stride = 1 + count // 8
    peers = [(core, at) for core in range(cores) for at in range(vocabs)]

    def first(core, which, at):
        return ((core * 2 + which) * vocabs + at) * stride

    def head(which):
        parts = [recv_ref[first(core, which, at)] for core, at in peers]
        peak = functools.reduce(jnp.maximum, parts)[0:1, :]
        total = sum(part[1:2, :] * jnp.exp(part[0:1, :] - peak) for part in parts)
        meta = functools.reduce(jnp.add, parts)
        live = meta[3:4, :]
        weight = jnp.where(which == 0, jnp.float32(WEIGHTS[0]), jnp.float32(WEIGHTS[1]))
        scale = live * (weight / jnp.maximum(jnp.sum(live), 1.0))
        return peak + jnp.log(total), meta[2:3, :], scale

    lse, target, scale = head(depth)
    lse_peer, target_peer, scale_peer = head(1 - depth)
    rows = lax.broadcasted_iota(jnp.int32, (8, tokens), 0)
    vectors = jnp.zeros((8, tokens), jnp.float32)
    for at, vector in enumerate((lse, target, scale, lse_peer, target_peer, scale_peer)):
        vectors = jnp.where(rows == at, vector, vectors)
    keep_ref[...] = vectors

    base = base_ref[0]
    shift = pl.multiple_of(depth * half, 8)

    def gradient(logits, at, start):
        row = lax.broadcasted_iota(jnp.int32, logits.shape, 0) + start
        hit = (row + base) == vectors[at + 1 : at + 2, :].astype(jnp.int32)
        soft = jnp.exp(logits - vectors[at : at + 1, :]) - jnp.where(hit, 1.0, 0.0)
        grad = (vectors[at + 2 : at + 3, :] * SCALE) * soft
        return hit & (row < width), jnp.where(row < width, grad, 0.0).astype(jnp.bfloat16)

    logits = logits_ref[...]
    hit, grad = gradient(logits, 0, 0)
    chosen = jnp.sum(jnp.where(hit, logits, 0.0), axis=0, keepdims=True)
    _, mine = gradient(logits_ref[pl.ds(shift, half), :], 0, shift)
    _, grad_peer = gradient(peer_ref[...], 3, shift)
    inner = rows_dot(grad, grad, (0, 0))
    cross = rows_dot(grad_peer, mine, (0, 0))
    square = inner * gram_ref[...]
    flat = jnp.transpose(cross)
    lines = []
    for core in range(cores):
        for matrix, which in ((cross, depth), (flat, 1 - depth)):
            start = core * vocabs * count
            blocks = folded(matrix[start : start + vocabs * count], which ^ core)
            for at in range(vocabs):
                slot = sum(1 << turn for turn, mask in enumerate(masks) if at & mask)
                for part in range(count // 8):
                    tile = recv_ref[first(core, which, at) + 1 + part]
                    lines.append(blocks[slot * (count // 8) + part] * tile)
    square = jnp.sum(square, axis=0, keepdims=True) + 2.0 * jnp.sum(sum(lines), axis=0, keepdims=True)
    pack = jnp.where(rows == depth, chosen, jnp.where(rows == 2, square, 0.0))[:4]
    for peer in range(2 * len(peers)):
        pack_ref[peer] = pack


def final_kernel(masks, sizes, recv_ref, keep_ref, nll_ref, loss_ref, norm_ref):
    _, vocabs, count = sizes
    depth = lax.axis_index("depth")
    total = jnp.sum(recv_ref[...], axis=0)
    keep = keep_ref[...]
    own = jnp.where(depth == 0, total[0:1, :], total[1:2, :])
    peer = jnp.where(depth == 0, total[1:2, :], total[0:1, :])
    nll = keep[0:1, :] - own
    parts = keep[2:3, :] * nll + keep[5:6, :] * (keep[3:4, :] - peer)
    loss_ref[...] = jnp.sum(parts, axis=1, keepdims=True)
    square = jnp.maximum(jnp.sum(total[2:3, :], axis=1, keepdims=True), 0.0)
    norm_ref[...] = jnp.sqrt(square) * (1.0 / SCALE)
    tokens = nll.shape[1]
    place = lax.axis_index("seq") * vocabs + slot_of(masks)
    turned = pltpu.roll(jnp.broadcast_to(nll, (8, tokens)), tokens - place * count, 1)
    nll_ref[...] = turned[:1, :count]


def program(hidden, embedding, targets, mask):
    cores, depths, vocabs = (lax.axis_size(axis) for axis in EVERY)
    count, dim = hidden.shape[1:]
    assert cores == 2 and depths == 2 and count % 8 == 0 and dim % 512 == 0
    width = embedding.shape[0]
    half = -(-width // 16) * 8
    tokens = cores * vocabs * count
    size = cores * depths * vocabs
    masks = exchange_masks(vocabs)
    place = lax.axis_index(GROUP)
    sizes = (cores, vocabs, count)
    f32 = jnp.float32
    split = dim // 2 + LEAN
    assert split % 256 == 0

    own = hidden[0]
    side = moved(own, "depth", 1)
    held = own
    for mask_far in masks[:-2]:
        other = moved(held, "vocab", mask_far)
        held = joined(held, other, mask_far)
    left, right = held[:, :split], held[:, split:]
    rows = left.shape[0]
    low, high = masks[-2:]
    other = moved(left, "vocab", low)
    left = joined(left, other, low)
    other = moved(right, "vocab", high)
    right = joined(right, other, high)
    left = joined(left, moved(left, "vocab", high), high)
    last = moved(right, "vocab", low)
    parts = [joined(right[at : at + rows], last[at : at + rows], low) for at in (0, rows)]
    right = jnp.concatenate(parts, axis=0)
    left_twin = moved(left, "seq", 1)
    right_twin = moved(right, "seq", 1)

    spot_at = (lax.axis_index("seq") * vocabs + slot_of(masks)) * count
    lane = lax.broadcasted_iota(jnp.int32, (count, tokens), 1)
    spot = (lane == spot_at + lax.broadcasted_iota(jnp.int32, (count, tokens), 0)).astype(f32)
    placed = [jnp.sum(spot * value[0][:, None].astype(f32), axis=0) for value in (targets, mask)]
    line = lax.broadcasted_iota(jnp.int32, (4, tokens), 0)
    meta = jnp.where(line == 2, placed[0][None, :], jnp.where(line == 3, placed[1][None, :], 0.0))

    shape = lambda *dims: jax.ShapeDtypeStruct(dims, f32)
    params = pltpu.CompilerParams(vmem_limit_bytes=LIMIT)
    tables = []
    for start, columns in ((0, split), (split, dim - split)):
        tables.append(
            pl.pallas_call(
                functools.partial(fetch_kernel, start),
                in_specs=[pl.BlockSpec(memory_space=pltpu.HBM)],
                out_specs=VMEM,
                out_shape=pltpu.VMEM((width, columns), embedding.dtype),
                scratch_shapes=[pltpu.SemaphoreType.DMA((PIECES,))],
                compiler_params=pltpu.CompilerParams(vmem_limit_bytes=46 * 2**20),
                cost_estimate=pl.CostEstimate(flops=0, transcendentals=0, bytes_accessed=4 * width * columns),
            )(embedding)
        )
    tables = [pltpu.with_memory_space_constraint(table, pltpu.VMEM) for table in tables]
    early = pl.pallas_call(
        early_kernel,
        in_specs=[VMEM] * 3,
        out_specs=[VMEM] * 3,
        out_shape=[shape(2 * half, tokens), shape(tokens, tokens), jax.ShapeDtypeStruct((tokens, split), hidden.dtype)],
        compiler_params=params,
        name="early",
    )(left, left_twin, tables[0])
    logits, send, gram, pack = pl.pallas_call(
        functools.partial(logits_kernel, width, half, size),
        in_specs=[VMEM] * 8,
        out_specs=[VMEM] * 4,
        out_shape=[
            shape(2 * half, tokens),
            shape(half, tokens),
            shape(tokens, tokens),
            shape(size * (1 + count // 8), 4, tokens),
        ],
        compiler_params=params,
        name="logits",
    )(right, right_twin, tables[1], *early, side, meta)

    peer = moved(send, "depth", 1)
    recv = lax.all_to_all(pack, EVERY, 0, 0, tiled=True)
    base = (place * width).astype(jnp.int32).reshape(1)
    pack, keep = pl.pallas_call(
        functools.partial(gradient_kernel, masks, width, half, sizes),
        in_specs=[VMEM] * 4 + [pl.BlockSpec(memory_space=pltpu.SMEM)],
        out_specs=[VMEM] * 2,
        out_shape=[shape(size, 4, tokens), shape(8, tokens)],
        compiler_params=params,
        name="gradient",
    )(logits, peer, recv, gram, base)
    recv = lax.all_to_all(pack, EVERY, 0, 0, tiled=True)
    nll, loss, norm = pl.pallas_call(
        functools.partial(final_kernel, masks, sizes),
        in_specs=[VMEM] * 2,
        out_specs=[VMEM] * 3,
        out_shape=[shape(1, count), shape(1, 1), shape(1, 1)],
        compiler_params=params,
        name="final",
    )(recv, keep)
    return (nll, loss[0, 0], norm[0, 0])


def solution(mesh):
    placed = (
        P("depth", GROUP, None),
        P(GROUP, None),
        P("depth", GROUP),
        P("depth", GROUP),
    )
    return jax.shard_map(
        program,
        mesh=mesh,
        in_specs=placed,
        out_specs=(P("depth", GROUP), P(), P()),
        check_vma=False,
    )
```

time: 66.4 us -> 67.1 us (1.011)
  local copies, waits for them, and re-layouts: 0.9 us -> 8.79 us
  starting transfers between devices: 19.9 us -> 15.1 us
  waiting for transfers between devices: 19.2 us -> 17.9 us
  Pallas kernels: 15 us -> 13.8 us
    unnamed x5 -> x12, local copies, waits for them, and re-layouts: 0.03 us -> 8.79 us
    ppermute x10 -> x9, starting transfers between devices: 14.9 us -> 12.2 us  [moved(): lax.ppermute(value, axis, [(at, at ^ mask) for at in range(lax.axis_size(...]
    all_to_all x1, starting transfers between devices: 4.97 us -> 2.87 us  [program(): recv = lax.all_to_all(pack, EVERY, 0, 0, tiled=True)]
    ppermute x10 -> x9, waiting for transfers between devices: 11.2 us -> 9.88 us  [moved(): lax.ppermute(value, axis, [(at, at ^ mask) for at in range(lax.axis_size(...]
    pallas_call x4, Pallas kernels: 8.59 us -> 7.47 us  [the longest x1 3.77 us: program(): pl.pallas_call(functools.partial(logits_kernel, width, half, size), in_sp...]
    slice x1 -> x0, local copies, waits for them, and re-layouts: 0.86 us -> none  [program(): left, right = (own[:, :split], own[:, split:])]
  transfers between devices with their start and end apart: 11 -> 10, of which waited for: 7 -> 6; matrix products, arithmetic and copies ran while one was open for 2% -> 2% of each run, Pallas kernels for 13% -> 13%
where the time goes in v3:
time: 67.1 us; the launch traced here: 66.8 us
  waiting for transfers between devices  17.9 us (27%)
  starting transfers between devices  15.1 us (23%)
  Pallas kernels  13.8 us (21%)
  blocking collectives  9.25 us (14%)
  local copies, waits for them, and re-layouts  8.79 us (13%)
  other arithmetic  1.14 us (2%)
  between operations  0.82 us (1%)
    ppermute x9, starting transfers between devices, moved(): lax.ppermute(value, axis, [(at, at ^ mask) for at in range(lax.axis_size(...  12.2 us
    ppermute x9, waiting for transfers between devices, moved(): lax.ppermute(value, axis, [(at, at ^ mask) for at in range(lax.axis_size(...  9.88 us
    all_to_all x1, blocking collectives, program(): recv = lax.all_to_all(pack, EVERY, 0, 0, tiled=True)  9.25 us
    unnamed x12, local copies, waits for them, and re-layouts  8.79 us
    all_to_all x1, waiting for transfers between devices, program(): recv = lax.all_to_all(pack, EVERY, 0, 0, tiled=True)  8.06 us
    pallas_call x2, Pallas kernels, program(): pl.pallas_call(functools.partial(fetch_kernel, start), in_specs=[pl.Block...  6.35 us
    pallas_call x1, Pallas kernels, program(): pl.pallas_call(functools.partial(logits_kernel, width, half, size), in_sp...  3.77 us
    all_to_all x1, starting transfers between devices, program(): recv = lax.all_to_all(pack, EVERY, 0, 0, tiled=True)  2.87 us
  transfers between devices with their start and end apart: 10, of which 6 were waited for; matrix products, arithmetic and copies ran while one was open for 2% of the time, Pallas kernels for 13%

profile of v3, /device:TPU:0, one launch (start us, length us, event | category | flops | bytes accessed | tf_op | source)
XLA Modules:
  0.0 66.8 jit_solution(8781427930319197783)
XLA Ops:
  0.6 3.0 %collective-permute-start.7 = (bf16[8,7168]{1,0:T(8,128)(2,1)}, bf16[8,7168]{1,0:T(8,128)(2,1)S(1)}, u32[]{:S(2)}, u32[]{:S(2)}) collective-permute-start(bf16[8,7168]{1,0:T(8,128)(2,1)} %bitcast.12), channel_id=1, source_target_pairs={{0,8},{8,0},{1,9},{9,1},{2,10},{10,2},{3,11},{11,3},{4,12},{12,4},... | collective-permute-start | bytes 344072 | tf_op jit(solution)/shard_map/ppermute | solution.py:28
  3.7 2.6 %collective-permute-start = (bf16[8,7168]{1,0:T(8,128)(2,1)}, bf16[8,7168]{1,0:T(8,128)(2,1)S(1)}, u32[]{:S(2)}, u32[]{:S(2)}) collective-permute-start(bf16[8,7168]{1,0:T(8,128)(2,1)} %bitcast.13), channel_id=1, source_target_pairs={{0,4},{1,5},{2,6},{3,7},{4,0},{5,1},{6,2},{7,3},{8,12},{9,13},{10,... | collective-permute-start | bytes 344072 | tf_op jit(solution)/shard_map/ppermute | solution.py:28
  6.3 0.7 %convert_bitcast_fusion = (f32[8]{0:T(128)S(1)}, f32[8]{0:T(128)S(1)}) fusion(s32[1,8]{1,0:T(1,128)} %param.7, s32[1,8]{1,0:T(1,128)} %param.6), kind=kLoop, calls=%fused_computation.24 | loop fusion | flops 16 | bytes 128 | tf_op jit(solution)/shard_map/convert_element_type | solution.py:230
  6.9 3.0 %shard_map.68.table_ref = bf16[1010,3328]{1,0:T(8,128)(2,1)S(1)} custom-call(bf16[1010,7168]{1,0:T(8,128)(2,1)} %table_ref.3), custom_call_target="tpu_custom_call" | custom-call | bytes 13445120 | tf_op jit(solution)/shard_map/pallas_call | solution.py:239
  10.0 2.8 %copy-done.1 = bf16[1010,3328]{1,0:T(8,128)(2,1)} copy-done((bf16[1010,3328]{1,0:T(8,128)(2,1)}, bf16[1010,3328]{1,0:T(8,128)(2,1)S(1)}, u32[]{:S(2)}) %copy-start.1) | copy-done | bytes 6722584
  12.8 3.3 %shard_map.67.table_ref = bf16[1010,3840]{1,0:T(8,128)(2,1)S(1)} custom-call(bf16[1010,7168]{1,0:T(8,128)(2,1)} %table_ref.3), custom_call_target="tpu_custom_call" | custom-call | bytes 15513600 | tf_op jit(solution)/shard_map/pallas_call | solution.py:239
  16.2 3.0 %copy-done = bf16[1010,3840]{1,0:T(8,128)(2,1)} copy-done((bf16[1010,3840]{1,0:T(8,128)(2,1)}, bf16[1010,3840]{1,0:T(8,128)(2,1)S(1)}, u32[]{:S(2)}) %copy-start) | copy-done | bytes 7756824
  19.2 0.0 collective-permute-done
  19.2 1.6 %collective-permute-start.4 = (bf16[16,3328]{1,0:T(8,128)(2,1)S(1)}, bf16[16,3328]{1,0:T(8,128)(2,1)S(1)}, u32[]{:S(2)}, u32[]{:S(2)}) collective-permute-start(bf16[16,3328]{1,0:T(8,128)(2,1)S(1)} %pad_maximum_fusion.4), channel_id=1, source_target_pairs={{0,1},{1,0},{2,3},{3,2},{4,5},{5,4},{6,7},{7,6},{8,9},{9,8},{10,11... | collective-permute-start | bytes 319496 | tf_op jit(solution)/shard_map/ppermute | solution.py:28
  20.8 1.6 %collective-permute-start.1 = (bf16[16,3840]{1,0:T(8,128)(2,1)S(1)}, bf16[16,3840]{1,0:T(8,128)(2,1)S(1)}, u32[]{:S(2)}, u32[]{:S(2)}) collective-permute-start(bf16[16,3840]{1,0:T(8,128)(2,1)S(1)} %fusion), channel_id=1, source_target_pairs={{0,2},{1,3},{2,0},{3,1},{4,6},{5,7},{6,4},{7,5},{8,10},{9,11},{10,... | collective-permute-start | bytes 368648 | tf_op jit(solution)/shard_map/ppermute | solution.py:28
  22.5 1.5 %collective-permute-done.4 = bf16[16,3328]{1,0:T(8,128)(2,1)S(1)} collective-permute-done((bf16[16,3328]{1,0:T(8,128)(2,1)S(1)}, bf16[16,3328]{1,0:T(8,128)(2,1)S(1)}, u32[]{:S(2)}, u32[]{:S(2)}) %collective-permute-start.4) | collective-permute-done | bytes 106528 | tf_op jit(solution)/shard_map/ppermute | solution.py:28
  24.1 1.6 %collective-permute-start.5 = (bf16[32,3328]{1,0:T(8,128)(2,1)S(1)}, bf16[32,3328]{1,0:T(8,128)(2,1)S(1)}, u32[]{:S(2)}, u32[]{:S(2)}) collective-permute-start(bf16[32,3328]{1,0:T(8,128)(2,1)S(1)} %pad_maximum_fusion.3), channel_id=1, source_target_pairs={{0,2},{1,3},{2,0},{3,1},{4,6},{5,7},{6,4},{7,5},{8,10},{9,11},{10,... | collective-permute-start | bytes 638984 | tf_op jit(solution)/shard_map/ppermute | solution.py:28
  25.7 1.0 %collective-permute-done.1 = bf16[16,3840]{1,0:T(8,128)(2,1)S(1)} collective-permute-done((bf16[16,3840]{1,0:T(8,128)(2,1)S(1)}, bf16[16,3840]{1,0:T(8,128)(2,1)S(1)}, u32[]{:S(2)}, u32[]{:S(2)}) %collective-permute-start.1) | collective-permute-done | bytes 122912 | tf_op jit(solution)/shard_map/ppermute | solution.py:28
  26.8 0.6 collective-permute-start.2
  27.3 3.0 %collective-permute-done.5 = bf16[32,3328]{1,0:T(8,128)(2,1)S(1)} collective-permute-done((bf16[32,3328]{1,0:T(8,128)(2,1)S(1)}, bf16[32,3328]{1,0:T(8,128)(2,1)S(1)}, u32[]{:S(2)}, u32[]{:S(2)}) %collective-permute-start.5) | collective-permute-done | bytes 213024 | tf_op jit(solution)/shard_map/ppermute | solution.py:28
  30.3 0.1 broadcast_select_fusion.1
  30.4 2.6 %collective-permute-done.2 = bf16[32,3840]{1,0:T(8,128)(2,1)S(1)} collective-permute-done((bf16[32,3840]{1,0:T(8,128)(2,1)S(1)}, bf16[32,3840]{1,0:T(8,128)(2,1)S(1)}, u32[]{:S(2)}, u32[]{:S(2)}) %collective-permute-start.2) | collective-permute-done | bytes 245792 | tf_op jit(solution)/shard_map/ppermute | solution.py:28
  33.1 0.1 collective-permute-start.3
  33.2 0.6 collective-permute-start.6
  33.8 0.1 select_reduce_fusion.1
  33.9 0.1 select_select_fusion.meta_ref
  34.0 1.7 %collective-permute-done.6.twin_ref = bf16[64,3328]{1,0:T(8,128)(2,1)S(1)} collective-permute-done((bf16[64,3328]{1,0:T(8,128)(2,1)S(1)}, bf16[64,3328]{1,0:T(8,128)(2,1)S(1)}, u32[]{:S(2)}, u32[]{:S(2)}) %collective-permute-start.6) | collective-permute-done | bytes 426016 | tf_op jit(solution)/shard_map/ppermute | solution.py:28
  35.7 2.9 %copy-done.2 = bf16[1010,3328]{1,0:T(8,128)(2,1)S(1)} copy-done((bf16[1010,3328]{1,0:T(8,128)(2,1)S(1)}, bf16[1010,3328]{1,0:T(8,128)(2,1)}, u32[]{:S(2)}) %copy-start.2) | copy-done | bytes 6722584
  38.6 2.1 %early.1 = (f32[1024,128]{1,0:T(8,128)S(1)}, f32[128,128]{1,0:T(8,128)S(1)}, bf16[128,3328]{1,0:T(8,128)(2,1)S(1)}) custom-call(bf16[64,3328]{1,0:T(8,128)(2,1)S(1)} %pad_maximum_fusion.1.own_ref, bf16[64,3328]{1,0:T(8,128)(2,1)S(1)} %collective-permute-done.6.twin_ref, bf16[1010,3328]{1,0:T(8,128)(2,1)S(1)} %copy-done.2), custom_call_target="tpu_custom_call" | custom-call | tf_op jit(solution)/shard_map/early/pallas_call | solution.py:250
  40.7 0.0 collective-permute-done.3.twin_ref
  40.8 3.8 %logits.1 = (f32[1024,128]{1,0:T(8,128)S(1)}, f32[512,128]{1,0:T(8,128)S(1)}, f32[128,128]{1,0:T(8,128)S(1)}, f32[64,4,128]{2,1,0:T(4,128)}) custom-call(bf16[64,3840]{1,0:T(8,128)(2,1)S(1)} %pad_maximum_fusion.own_ref, bf16[64,3840]{1,0:T(8,128)(2,1)S(1)} %collective-permute-done.3.twin_ref, bf16[1010,3840]{1,0:T(8,128)(2,1)S(1)} %bitcast.11, ...), custom_call_target="tpu_custom_call" | custom-call | tf_op jit(solution)/shard_map/logits/pallas_call | solution.py:258
  44.5 0.5 collective-permute-start.8
  45.1 2.9 %all-to-all-start = ((f32[64,4,128]{2,1,0:T(4,128)}), f32[64,4,128]{2,1,0:T(4,128)S(1)}, u32[]{:S(2)}, u32[]{:S(2)}) async-start(f32[64,4,128]{2,1,0:T(4,128)} %get-tuple-element.20), calls=%async_computation | async-start | bytes 262144 | tf_op jit(solution)/shard_map/all_to_all | solution.py:273
  48.0 8.1 %all-to-all-done.recv_ref = f32[64,4,128]{2,1,0:T(4,128)S(1)} async-done(((f32[64,4,128]{2,1,0:T(4,128)}), f32[64,4,128]{2,1,0:T(4,128)S(1)}, u32[]{:S(2)}, u32[]{:S(2)}) %all-to-all-start) | async-done | bytes 131104 | tf_op jit(solution)/shard_map/all_to_all | solution.py:273
  56.0 0.9 %gradient.1 = (f32[32,4,128]{2,1,0:T(4,128)S(1)}, f32[8,128]{1,0:T(8,128)S(1)}) custom-call(f32[1024,128]{1,0:T(8,128)S(1)} %get-tuple-element.18.logits_ref, f32[512,128]{1,0:T(8,128)S(1)} %collective-permute-done.8.peer_ref, f32[64,4,128]{2,1,0:T(4,128)S(1)} %all-to-all-done.recv_ref, f32[128,128]{1,0:T(8,128)S(1)} %get-tuple-element.21.gram_ref, ...), custom_call_target="tpu_custom_call" | custom-call | tf_op jit(solution)/shard_map/gradient/pallas_call | solution.py:275
  57.0 9.2 %all_to_all.10.recv_ref = f32[32,4,128]{2,1,0:T(4,128)S(1)} all-to-all(f32[32,4,128]{2,1,0:T(4,128)S(1)} %get-tuple-element.22), channel_id=1, replica_groups=mesh['seq'=2,'depth'=2,'vocab'=8] {'seq','depth','vocab'}, dimensions={0} | all-to-all | bytes 131072 | tf_op jit(solution)/shard_map/all_to_all | solution.py:283
  66.2 0.6 final.1
  (24 shorter events, 0.3 us)
Async XLA Ops:
  0.6 40.1 %collective-permute-start.7 = (bf16[8,7168]{1,0:T(8,128)(2,1)}, bf16[8,7168]{1,0:T(8,128)(2,1)S(1)}, u32[]{:S(2)}, u32[]{:S(2)}) collective-permute-start(bf16[8,7168]{1,0:T(8,128)(2,1)} %bitcast.12), channel_id=1, source_target_pairs={{0,8},{8,0},{1,9},{9,1},{2,10},{10,2},{3,11},{11,3},{4,12},{12,4},... | collective-permute-start | bytes 344072 | tf_op jit(solution)/shard_map/ppermute | solution.py:28
  3.7 15.5 %collective-permute-start = (bf16[8,7168]{1,0:T(8,128)(2,1)}, bf16[8,7168]{1,0:T(8,128)(2,1)S(1)}, u32[]{:S(2)}, u32[]{:S(2)}) collective-permute-start(bf16[8,7168]{1,0:T(8,128)(2,1)} %bitcast.13), channel_id=1, source_target_pairs={{0,4},{1,5},{2,6},{3,7},{4,0},{5,1},{6,2},{7,3},{8,12},{9,13},{10,... | collective-permute-start | bytes 344072 | tf_op jit(solution)/shard_map/ppermute | solution.py:28
  9.9 2.8 %copy-start.1 = (bf16[1010,3328]{1,0:T(8,128)(2,1)}, bf16[1010,3328]{1,0:T(8,128)(2,1)S(1)}, u32[]{:S(2)}) copy-start(bf16[1010,3328]{1,0:T(8,128)(2,1)S(1)} %shard_map.68.table_ref) | copy-start | bytes 20167684
  12.8 6.4 %copy-start.3 = (bf16[1,8,7168]{2,1,0:T(8,128)(2,1)S(1)}, bf16[1,8,7168]{2,1,0:T(8,128)(2,1)}, u32[]{:S(2)}) copy-start(bf16[1,8,7168]{2,1,0:T(8,128)(2,1)} %param.4) | copy-start | bytes 344068
  16.1 3.0 %copy-start = (bf16[1010,3840]{1,0:T(8,128)(2,1)}, bf16[1010,3840]{1,0:T(8,128)(2,1)S(1)}, u32[]{:S(2)}) copy-start(bf16[1010,3840]{1,0:T(8,128)(2,1)S(1)} %shard_map.67.table_ref) | copy-start | bytes 23270404
  19.2 21.6 %slice-start = ((s8[7802880]{0:T(1024)(128)(4,1)}), s8[4194304]{0:T(1024)(128)(4,1)S(1)}, s32[]{:S(2)}) async-start(s8[7802880]{0:T(1024)(128)(4,1)} %bitcast.10), calls=%async_computation.2 | async-start | bytes 8388608
  19.2 4.8 %collective-permute-start.4 = (bf16[16,3328]{1,0:T(8,128)(2,1)S(1)}, bf16[16,3328]{1,0:T(8,128)(2,1)S(1)}, u32[]{:S(2)}, u32[]{:S(2)}) collective-permute-start(bf16[16,3328]{1,0:T(8,128)(2,1)S(1)} %pad_maximum_fusion.4), channel_id=1, source_target_pairs={{0,1},{1,0},{2,3},{3,2},{4,5},{5,4},{6,7},{7,6},{8,9},{9,8},{10,11... | collective-permute-start | bytes 319496 | tf_op jit(solution)/shard_map/ppermute | solution.py:28
  20.8 5.9 %collective-permute-start.1 = (bf16[16,3840]{1,0:T(8,128)(2,1)S(1)}, bf16[16,3840]{1,0:T(8,128)(2,1)S(1)}, u32[]{:S(2)}, u32[]{:S(2)}) collective-permute-start(bf16[16,3840]{1,0:T(8,128)(2,1)S(1)} %fusion), channel_id=1, source_target_pairs={{0,2},{1,3},{2,0},{3,1},{4,6},{5,7},{6,4},{7,5},{8,10},{9,11},{10,... | collective-permute-start | bytes 368648 | tf_op jit(solution)/shard_map/ppermute | solution.py:28
  24.1 6.3 %collective-permute-start.5 = (bf16[32,3328]{1,0:T(8,128)(2,1)S(1)}, bf16[32,3328]{1,0:T(8,128)(2,1)S(1)}, u32[]{:S(2)}, u32[]{:S(2)}) collective-permute-start(bf16[32,3328]{1,0:T(8,128)(2,1)S(1)} %pad_maximum_fusion.3), channel_id=1, source_target_pairs={{0,2},{1,3},{2,0},{3,1},{4,6},{5,7},{6,4},{7,5},{8,10},{9,11},{10,... | collective-permute-start | bytes 638984 | tf_op jit(solution)/shard_map/ppermute | solution.py:28
  26.8 6.3 %collective-permute-start.2 = (bf16[32,3840]{1,0:T(8,128)(2,1)S(1)}, bf16[32,3840]{1,0:T(8,128)(2,1)S(1)}, u32[]{:S(2)}, u32[]{:S(2)}) collective-permute-start(bf16[32,3840]{1,0:T(8,128)(2,1)S(1)} %pad_maximum_fusion.2), channel_id=1, source_target_pairs={{0,1},{1,0},{2,3},{3,2},{4,5},{5,4},{6,7},{7,6},{8,9},{9,8},{10,11... | collective-permute-start | bytes 737288 | tf_op jit(solution)/shard_map/ppermute | solution.py:28
  33.1 7.6 %collective-permute-start.3 = (bf16[64,3840]{1,0:T(8,128)(2,1)S(1)}, bf16[64,3840]{1,0:T(8,128)(2,1)S(1)}, u32[]{:S(2)}, u32[]{:S(2)}) collective-permute-start(bf16[64,3840]{1,0:T(8,128)(2,1)S(1)} %pad_maximum_fusion.own_ref), channel_id=1, source_target_pairs={{0,16},{16,0},{1,17},{17,1},{2,18},{18,2},{3,19},{19,3},{4,20},{20... | collective-permute-start | bytes 1474568 | tf_op jit(solution)/shard_map/ppermute | solution.py:28
  33.2 2.4 %collective-permute-start.6 = (bf16[64,3328]{1,0:T(8,128)(2,1)S(1)}, bf16[64,3328]{1,0:T(8,128)(2,1)S(1)}, u32[]{:S(2)}, u32[]{:S(2)}) collective-permute-start(bf16[64,3328]{1,0:T(8,128)(2,1)S(1)} %pad_maximum_fusion.1.own_ref), channel_id=1, source_target_pairs={{0,16},{16,0},{1,17},{17,1},{2,18},{18,2},{3,19},{19,3},{4,20},{20... | collective-permute-start | bytes 1277960 | tf_op jit(solution)/shard_map/ppermute | solution.py:28
  34.0 6.8 %slice-start.1 = ((s8[7802880]{0:T(1024)(128)(4,1)}), s8[3608576]{0:T(1024)(128)(4,1)S(1)}, s32[]{:S(2)}) async-start(s8[7802880]{0:T(1024)(128)(4,1)} %bitcast.10), calls=%async_computation.3 | async-start | bytes 7217152
  35.7 2.9 %copy-start.2 = (bf16[1010,3328]{1,0:T(8,128)(2,1)S(1)}, bf16[1010,3328]{1,0:T(8,128)(2,1)}, u32[]{:S(2)}) copy-start(bf16[1010,3328]{1,0:T(8,128)(2,1)} %copy-done.1) | copy-start | bytes 20167684
  44.5 11.5 %collective-permute-start.8 = (f32[512,128]{1,0:T(8,128)S(1)}, f32[512,128]{1,0:T(8,128)S(1)}, u32[]{:S(2)}, u32[]{:S(2)}) collective-permute-start(f32[512,128]{1,0:T(8,128)S(1)} %get-tuple-element.19), channel_id=1, source_target_pairs={{0,8},{8,0},{1,9},{9,1},{2,10},{10,2},{3,11},{11,3},{4,12},{12,4},... | collective-permute-start | bytes 786440 | tf_op jit(solution)/shard_map/ppermute | solution.py:28
  45.1 10.9 %all-to-all-start = ((f32[64,4,128]{2,1,0:T(4,128)}), f32[64,4,128]{2,1,0:T(4,128)S(1)}, u32[]{:S(2)}, u32[]{:S(2)}) async-start(f32[64,4,128]{2,1,0:T(4,128)} %get-tuple-element.20), calls=%async_computation | async-start | bytes 262144 | tf_op jit(solution)/shard_map/all_to_all | solution.py:273

commit v4 on v3

--- a/solution.py
+++ b/solution.py
@@ -18,24 +18,27 @@
 VMEM = pl.BlockSpec(memory_space=pltpu.VMEM)
 
 
-def exchange_masks(size):
+def exchange_steps(size):
     bits = size.bit_length() - 1
-    assert size == 2**bits and bits >= 2
-    return [2**bit for bit in range(bits - 1, 1, -1)] + [1, 2]
+    assert size == 2**bits and bits >= 3
+    return [(2**bit, 2**bit) for bit in range(bits - 1, 2, -1)] + [(6, 4), (1, 1), (2, 6)]
+
+
+def parity(at, bits):
+    return functools.reduce(lambda x, y: x ^ y, [(at >> bit) & 1 for bit in range(bits.bit_length()) if bits >> bit & 1])
 
 
 def moved(value, axis, mask):
     return lax.ppermute(value, axis, [(at, at ^ mask) for at in range(lax.axis_size(axis))])
 
 
-def joined(value, other, mask):
-    later = (lax.axis_index("vocab") & mask) != 0
+def joined(value, other, bits):
+    later = parity(lax.axis_index("vocab"), bits) != 0
     return jnp.concatenate([jnp.where(later, other, value), jnp.where(later, value, other)], axis=0)
 
 
-def slot_of(masks):
-    at = lax.axis_index("vocab")
-    return sum(jnp.where((at & mask) != 0, 1, 0) << turn for turn, mask in enumerate(masks))
+def slot_of(steps, at):
+    return sum(parity(at, bits) << turn for turn, (_, bits) in enumerate(steps))
 
 
 def rows_dot(a, b, dims):
@@ -63,11 +66,21 @@
     return jnp.concatenate([jnp.where(first, own, twin), jnp.where(first, twin, own)], axis=0)
 
 
-def early_kernel(own_ref, twin_ref, table_ref, logits_ref, gram_ref, states_ref):
+def first_kernel(cut, own_ref, twin_ref, table_ref, logits_ref):
+    states = merged(own_ref.at[:, :cut], twin_ref.at[:, :cut])
+    logits_ref[: table_ref.shape[0], :] = rows_dot(table_ref[:, :cut], states, (1, 1))
+
+
+def second_kernel(cut, own_ref, twin_ref, table_ref, first_ref, logits_ref, states_ref):
     states = merged(own_ref, twin_ref)
     states_ref[...] = states
-    logits_ref[: table_ref.shape[0], :] = rows_dot(table_ref[...], states, (1, 1))
-    gram_ref[...] = rows_dot(states, states, (1, 1))
+    width = table_ref.shape[0]
+    logits_ref[:width, :] = first_ref[:width, :] + rows_dot(table_ref[:, cut:], states[:, cut:], (1, 1))
+
+
+def gram_kernel(early_ref, own_ref, twin_ref, gram_ref):
+    early, late = early_ref[...], merged(own_ref, twin_ref)
+    gram_ref[...] = rows_dot(early, early, (1, 1)) + rows_dot(late, late, (1, 1))
 
 
 def folded(block, which):
@@ -83,8 +96,8 @@
 
 
 def logits_kernel(
-    width, half, size, own_ref, twin_ref, table_ref, early_ref, gram_early_ref, states_ref, side_ref, meta_ref,
-    logits_ref, send_ref, gram_ref, pack_ref,
+    width, half, size, own_ref, twin_ref, table_ref, early_ref, states_ref, side_ref, meta_ref,
+    logits_ref, send_ref, pack_ref,
 ):
     early = states_ref[...]
     late = merged(own_ref, twin_ref)
@@ -92,7 +105,6 @@
     logits = rows_dot(table_ref[...], late, (1, 1)) + early_ref[:width, :]
     logits_ref[:width, :] = logits
     logits_ref[width:, :] = jnp.zeros((2 * half - width, logits.shape[1]), jnp.float32)
-    gram_ref[...] = gram_early_ref[...] + rows_dot(late, late, (1, 1))
     cross = rows_dot(side_ref[:, :start], early, (1, 1)) + rows_dot(side_ref[:, start:], late, (1, 1))
     depth = lax.axis_index("depth")
     send_ref[...] = logits_ref[pl.ds(pl.multiple_of((1 - depth) * half, 8), half), :]
@@ -107,7 +119,7 @@
 
 
 def gradient_kernel(
-    masks, width, half, sizes, logits_ref, peer_ref, recv_ref, gram_ref, base_ref, pack_ref, keep_ref
+    steps, width, half, sizes, logits_ref, peer_ref, recv_ref, gram_ref, base_ref, pack_ref, keep_ref
 ):
     cores, vocabs, count = sizes
     depth = lax.axis_index("depth")
@@ -161,7 +173,7 @@
             start = core * vocabs * count
             blocks = folded(matrix[start : start + vocabs * count], which ^ core)
             for at in range(vocabs):
-                slot = sum(1 << turn for turn, mask in enumerate(masks) if at & mask)
+                slot = slot_of(steps, at)
                 for part in range(count // 8):
                     tile = recv_ref[first(core, which, at) + 1 + part]
                     lines.append(blocks[slot * (count // 8) + part] * tile)
@@ -171,7 +183,7 @@
         pack_ref[peer] = pack
 
 
-def final_kernel(masks, sizes, recv_ref, keep_ref, nll_ref, loss_ref, norm_ref):
+def final_kernel(steps, sizes, recv_ref, keep_ref, nll_ref, loss_ref, norm_ref):
     _, vocabs, count = sizes
     depth = lax.axis_index("depth")
     total = jnp.sum(recv_ref[...], axis=0)
@@ -184,7 +196,7 @@
     square = jnp.maximum(jnp.sum(total[2:3, :], axis=1, keepdims=True), 0.0)
     norm_ref[...] = jnp.sqrt(square) * (1.0 / SCALE)
     tokens = nll.shape[1]
-    place = lax.axis_index("seq") * vocabs + slot_of(masks)
+    place = lax.axis_index("seq") * vocabs + slot_of(steps, lax.axis_index("vocab"))
     turned = pltpu.roll(jnp.broadcast_to(nll, (8, tokens)), tokens - place * count, 1)
     nll_ref[...] = turned[:1, :count]
 
@@ -197,7 +209,7 @@
     half = -(-width // 16) * 8
     tokens = cores * vocabs * count
     size = cores * depths * vocabs
-    masks = exchange_masks(vocabs)
+    steps = exchange_steps(vocabs)
     place = lax.axis_index(GROUP)
     sizes = (cores, vocabs, count)
     f32 = jnp.float32
@@ -207,24 +219,24 @@
     own = hidden[0]
     side = moved(own, "depth", 1)
     held = own
-    for mask_far in masks[:-2]:
-        other = moved(held, "vocab", mask_far)
-        held = joined(held, other, mask_far)
+    *far, low, high = steps
+    for step in far:
+        other = moved(held, "vocab", step[0])
+        held = joined(held, other, step[1])
     left, right = held[:, :split], held[:, split:]
     rows = left.shape[0]
-    low, high = masks[-2:]
-    other = moved(left, "vocab", low)
-    left = joined(left, other, low)
-    other = moved(right, "vocab", high)
-    right = joined(right, other, high)
-    left = joined(left, moved(left, "vocab", high), high)
-    last = moved(right, "vocab", low)
-    parts = [joined(right[at : at + rows], last[at : at + rows], low) for at in (0, rows)]
+    other = moved(left, "vocab", low[0])
+    left = joined(left, other, low[1])
+    other = moved(right, "vocab", high[0])
+    right = joined(right, other, high[1])
+    left = joined(left, moved(left, "vocab", high[0]), high[1])
+    last = moved(right, "vocab", low[0])
+    parts = [joined(right[at : at + rows], last[at : at + rows], low[1]) for at in (0, rows)]
     right = jnp.concatenate(parts, axis=0)
     left_twin = moved(left, "seq", 1)
     right_twin = moved(right, "seq", 1)
 
-    spot_at = (lax.axis_index("seq") * vocabs + slot_of(masks)) * count
+    spot_at = (lax.axis_index("seq") * vocabs + slot_of(steps, lax.axis_index("vocab"))) * count
     lane = lax.broadcasted_iota(jnp.int32, (count, tokens), 1)
     spot = (lane == spot_at + lax.broadcasted_iota(jnp.int32, (count, tokens), 0)).astype(f32)
     placed = [jnp.sum(spot * value[0][:, None].astype(f32), axis=0) for value in (targets, mask)]
@@ -242,38 +254,54 @@
                 out_specs=VMEM,
                 out_shape=pltpu.VMEM((width, columns), embedding.dtype),
                 scratch_shapes=[pltpu.SemaphoreType.DMA((PIECES,))],
-                compiler_params=pltpu.CompilerParams(vmem_limit_bytes=46 * 2**20),
+                compiler_params=pltpu.CompilerParams(vmem_limit_bytes=4 * 2**20),
                 cost_estimate=pl.CostEstimate(flops=0, transcendentals=0, bytes_accessed=4 * width * columns),
-            )(embedding)
+            )(pltpu.with_memory_space_constraint(embedding, pltpu.HBM))
         )
     tables = [pltpu.with_memory_space_constraint(table, pltpu.VMEM) for table in tables]
-    early = pl.pallas_call(
-        early_kernel,
+    cut = split // 2
+    first = pl.pallas_call(
+        functools.partial(first_kernel, cut),
         in_specs=[VMEM] * 3,
+        out_specs=VMEM,
+        out_shape=shape(2 * half, tokens),
+        compiler_params=params,
+        name="first",
+    )(left, left_twin, tables[0])
+    early, states = pl.pallas_call(
+        functools.partial(second_kernel, cut),
+        in_specs=[VMEM] * 4,
+        out_specs=[VMEM] * 2,
+        out_shape=[shape(2 * half, tokens), jax.ShapeDtypeStruct((tokens, split), hidden.dtype)],
+        compiler_params=params,
+        name="second",
+    )(left, left_twin, tables[0], first)
+    logits, send, pack = pl.pallas_call(
+        functools.partial(logits_kernel, width, half, size),
+        in_specs=[VMEM] * 7,
         out_specs=[VMEM] * 3,
-        out_shape=[shape(2 * half, tokens), shape(tokens, tokens), jax.ShapeDtypeStruct((tokens, split), hidden.dtype)],
-        compiler_params=params,
-        name="early",
-    )(left, left_twin, tables[0])
-    logits, send, gram, pack = pl.pallas_call(
-        functools.partial(logits_kernel, width, half, size),
-        in_specs=[VMEM] * 8,
-        out_specs=[VMEM] * 4,
         out_shape=[
             shape(2 * half, tokens),
             shape(half, tokens),
-            shape(tokens, tokens),
             shape(size * (1 + count // 8), 4, tokens),
         ],
         compiler_params=params,
         name="logits",
-    )(right, right_twin, tables[1], *early, side, meta)
+    )(right, right_twin, tables[1], early, states, side, meta)
 
     peer = moved(send, "depth", 1)
     recv = lax.all_to_all(pack, EVERY, 0, 0, tiled=True)
+    gram = pl.pallas_call(
+        gram_kernel,
+        in_specs=[VMEM] * 3,
+        out_specs=VMEM,
+        out_shape=shape(tokens, tokens),
+        compiler_params=params,
+        name="gram",
+    )(states, right, right_twin)
     base = (place * width).astype(jnp.int32).reshape(1)
     pack, keep = pl.pallas_call(
-        functools.partial(gradient_kernel, masks, width, half, sizes),
+        functools.partial(gradient_kernel, steps, width, half, sizes),
         in_specs=[VMEM] * 4 + [pl.BlockSpec(memory_space=pltpu.SMEM)],
         out_specs=[VMEM] * 2,
         out_shape=[shape(size, 4, tokens), shape(8, tokens)],
@@ -282,7 +310,7 @@
     )(logits, peer, recv, gram, base)
     recv = lax.all_to_all(pack, EVERY, 0, 0, tiled=True)
     nll, loss, norm = pl.pallas_call(
-        functools.partial(final_kernel, masks, sizes),
+        functools.partial(final_kernel, steps, sizes),
         in_specs=[VMEM] * 2,
         out_specs=[VMEM] * 3,
         out_shape=[shape(1, count), shape(1, 1), shape(1, 1)],

time: 67.1 us -> 68.8 us (1.025)
  waiting for transfers between devices: 17.9 us -> 20.9 us
  starting transfers between devices: 15.1 us -> 12.2 us
  local copies, waits for them, and re-layouts: 8.79 us -> 10.1 us
    ppermute x9, waiting for transfers between devices: 9.88 us -> 13.5 us  [moved(): lax.ppermute(value, axis, [(at, at ^ mask) for at in range(lax.axis_size(...]
    ppermute x9, starting transfers between devices: 12.2 us -> 9.59 us  [moved(): lax.ppermute(value, axis, [(at, at ^ mask) for at in range(lax.axis_size(...]
    unnamed x12, local copies, waits for them, and re-layouts: 8.79 us -> 10.1 us
    pallas_call x3 -> x5, Pallas kernels: 3.7 us -> 4.38 us  [the longest x1 1.12 us: program(): pl.pallas_call(functools.partial(second_kernel, cut), in_specs=[VMEM] * 4...]
where the time goes in v4:
time: 68.8 us; the launch traced here: 68.5 us
  waiting for transfers between devices  20.9 us (30%)
  Pallas kernels  14.2 us (21%)
  starting transfers between devices  12.2 us (18%)
  local copies, waits for them, and re-layouts  10.1 us (15%)
  blocking collectives  9.15 us (13%)
  other arithmetic  1.15 us (2%)
  between operations  0.84 us (1%)
    ppermute x9, waiting for transfers between devices, moved(): lax.ppermute(value, axis, [(at, at ^ mask) for at in range(lax.axis_size(...  13.5 us
    unnamed x12, local copies, waits for them, and re-layouts  10.1 us
    ppermute x9, starting transfers between devices, moved(): lax.ppermute(value, axis, [(at, at ^ mask) for at in range(lax.axis_size(...  9.59 us
    all_to_all x1, blocking collectives, program(): recv = lax.all_to_all(pack, EVERY, 0, 0, tiled=True)  9.15 us
    all_to_all x1, waiting for transfers between devices, program(): recv = lax.all_to_all(pack, EVERY, 0, 0, tiled=True)  7.41 us
    pallas_call x2, Pallas kernels, program(): pl.pallas_call(functools.partial(fetch_kernel, start), in_specs=[pl.Block...  6.35 us
    pallas_call x1, Pallas kernels, program(): pl.pallas_call(functools.partial(logits_kernel, width, half, size), in_sp...  3.51 us
    all_to_all x1, starting transfers between devices, program(): recv = lax.all_to_all(pack, EVERY, 0, 0, tiled=True)  2.57 us
  transfers between devices with their start and end apart: 10, of which 6 were waited for; matrix products, arithmetic and copies ran while one was open for 2% of the time, Pallas kernels for 13%

profile of v4, /device:TPU:0, one launch (start us, length us, event | category | flops | bytes accessed | tf_op | source)
XLA Modules:
  0.0 68.5 jit_solution(7882061634960774634)
XLA Ops:
  0.6 3.0 %collective-permute-start.7 = (bf16[8,7168]{1,0:T(8,128)(2,1)}, bf16[8,7168]{1,0:T(8,128)(2,1)S(1)}, u32[]{:S(2)}, u32[]{:S(2)}) collective-permute-start(bf16[8,7168]{1,0:T(8,128)(2,1)} %bitcast.12), channel_id=1, source_target_pairs={{0,8},{8,0},{1,9},{9,1},{2,10},{10,2},{3,11},{11,3},{4,12},{12,4},... | collective-permute-start | bytes 344072 | tf_op jit(solution)/shard_map/ppermute | solution.py:32
  3.7 3.6 %collective-permute-start = (bf16[8,7168]{1,0:T(8,128)(2,1)}, bf16[8,7168]{1,0:T(8,128)(2,1)S(1)}, u32[]{:S(2)}, u32[]{:S(2)}) collective-permute-start(bf16[8,7168]{1,0:T(8,128)(2,1)} %bitcast.13), channel_id=1, source_target_pairs={{0,6},{1,7},{2,4},{3,5},{4,2},{5,3},{6,0},{7,1},{8,14},{9,15},{10,... | collective-permute-start | bytes 344072 | tf_op jit(solution)/shard_map/ppermute | solution.py:32
  7.3 0.7 convert_bitcast_fusion
  7.9 3.0 %shard_map.68.table_ref = bf16[1010,3328]{1,0:T(8,128)(2,1)S(1)} custom-call(bf16[1010,7168]{1,0:T(8,128)(2,1)} %table_ref.3), custom_call_target="tpu_custom_call" | custom-call | bytes 13445120 | tf_op jit(solution)/shard_map/pallas_call | solution.py:251
  11.0 2.8 %copy-done = bf16[1010,3328]{1,0:T(8,128)(2,1)} copy-done((bf16[1010,3328]{1,0:T(8,128)(2,1)}, bf16[1010,3328]{1,0:T(8,128)(2,1)S(1)}, u32[]{:S(2)}) %copy-start) | copy-done | bytes 6722584
  13.8 3.3 %shard_map.67.table_ref = bf16[1010,3840]{1,0:T(8,128)(2,1)S(1)} custom-call(bf16[1010,7168]{1,0:T(8,128)(2,1)} %table_ref.3), custom_call_target="tpu_custom_call" | custom-call | bytes 15513600 | tf_op jit(solution)/shard_map/pallas_call | solution.py:251
  17.2 3.0 %copy-done.2 = bf16[1010,3840]{1,0:T(8,128)(2,1)} copy-done((bf16[1010,3840]{1,0:T(8,128)(2,1)}, bf16[1010,3840]{1,0:T(8,128)(2,1)S(1)}, u32[]{:S(2)}) %copy-start.2) | copy-done | bytes 7756824
  20.2 1.6 %collective-permute-start.4 = (bf16[16,3328]{1,0:T(8,128)(2,1)S(1)}, bf16[16,3328]{1,0:T(8,128)(2,1)S(1)}, u32[]{:S(2)}, u32[]{:S(2)}) collective-permute-start(bf16[16,3328]{1,0:T(8,128)(2,1)S(1)} %pad_maximum_fusion.4), channel_id=1, source_target_pairs={{0,1},{1,0},{2,3},{3,2},{4,5},{5,4},{6,7},{7,6},{8,9},{9,8},{10,11... | collective-permute-start | bytes 319496 | tf_op jit(solution)/shard_map/ppermute | solution.py:32
  21.8 0.1 collective-permute-start.1
  21.9 3.1 %collective-permute-done.4 = bf16[16,3328]{1,0:T(8,128)(2,1)S(1)} collective-permute-done((bf16[16,3328]{1,0:T(8,128)(2,1)S(1)}, bf16[16,3328]{1,0:T(8,128)(2,1)S(1)}, u32[]{:S(2)}, u32[]{:S(2)}) %collective-permute-start.4) | collective-permute-done | bytes 106528 | tf_op jit(solution)/shard_map/ppermute | solution.py:32
  25.1 0.1 collective-permute-start.5
  25.1 2.6 %collective-permute-done.1 = bf16[16,3840]{1,0:T(8,128)(2,1)S(1)} collective-permute-done((bf16[16,3840]{1,0:T(8,128)(2,1)S(1)}, bf16[16,3840]{1,0:T(8,128)(2,1)S(1)}, u32[]{:S(2)}, u32[]{:S(2)}) %collective-permute-start.1) | collective-permute-done | bytes 122912 | tf_op jit(solution)/shard_map/ppermute | solution.py:32
  27.8 0.1 collective-permute-start.2
  27.9 3.5 %collective-permute-done.5 = bf16[32,3328]{1,0:T(8,128)(2,1)S(1)} collective-permute-done((bf16[32,3328]{1,0:T(8,128)(2,1)S(1)}, bf16[32,3328]{1,0:T(8,128)(2,1)S(1)}, u32[]{:S(2)}, u32[]{:S(2)}) %collective-permute-start.5) | collective-permute-done | bytes 213024 | tf_op jit(solution)/shard_map/ppermute | solution.py:32
  31.4 0.1 broadcast_select_fusion.1
  31.4 2.6 %collective-permute-done.2 = bf16[32,3840]{1,0:T(8,128)(2,1)S(1)} collective-permute-done((bf16[32,3840]{1,0:T(8,128)(2,1)S(1)}, bf16[32,3840]{1,0:T(8,128)(2,1)S(1)}, u32[]{:S(2)}, u32[]{:S(2)}) %collective-permute-start.2) | collective-permute-done | bytes 245792 | tf_op jit(solution)/shard_map/ppermute | solution.py:32
  34.2 0.6 collective-permute-start.6
  34.8 0.1 select_reduce_fusion.1
  34.9 0.1 select_select_fusion.meta_ref
  35.0 1.7 %collective-permute-done.6.twin_ref = bf16[64,3328]{1,0:T(8,128)(2,1)S(1)} collective-permute-done((bf16[64,3328]{1,0:T(8,128)(2,1)S(1)}, bf16[64,3328]{1,0:T(8,128)(2,1)S(1)}, u32[]{:S(2)}, u32[]{:S(2)}) %collective-permute-start.6) | collective-permute-done | bytes 426016 | tf_op jit(solution)/shard_map/ppermute | solution.py:32
  36.7 2.9 %copy-done.1 = bf16[1010,3328]{1,0:T(8,128)(2,1)S(1)} copy-done((bf16[1010,3328]{1,0:T(8,128)(2,1)S(1)}, bf16[1010,3328]{1,0:T(8,128)(2,1)}, u32[]{:S(2)}) %copy-start.1) | copy-done | bytes 6722584
  39.6 1.1 %first.1.first_ref = f32[1024,128]{1,0:T(8,128)S(1)} custom-call(bf16[64,3328]{1,0:T(8,128)(2,1)S(1)} %pad_maximum_fusion.1.own_ref, bf16[64,3328]{1,0:T(8,128)(2,1)S(1)} %collective-permute-done.6.twin_ref, bf16[1010,3328]{1,0:T(8,128)(2,1)S(1)} %copy-done.1), custom_call_target="tpu_custom_call" | custom-call | tf_op jit(solution)/shard_map/first/pallas_call | solution.py:263
  40.7 1.1 %second.1 = (f32[1024,128]{1,0:T(8,128)S(1)}, bf16[128,3328]{1,0:T(8,128)(2,1)S(1)}) custom-call(bf16[64,3328]{1,0:T(8,128)(2,1)S(1)} %pad_maximum_fusion.1.own_ref, bf16[64,3328]{1,0:T(8,128)(2,1)S(1)} %collective-permute-done.6.twin_ref, bf16[1010,3328]{1,0:T(8,128)(2,1)S(1)} %copy-done.1, f32[1024,128]{1,0:T(8,128)S(1)} %first.1.first_ref), custom_call_target="tpu_custom_call" | custom-call | tf_op jit(solution)/shard_map/second/pallas_call | solution.py:271
  41.8 1.3 %slice-done.1 = s8[3608576]{0:T(1024)(128)(4,1)S(1)} async-done(((s8[7802880]{0:T(1024)(128)(4,1)}), s8[3608576]{0:T(1024)(128)(4,1)S(1)}, s32[]{:S(2)}) %slice-start.1) | async-done | bytes 3608600
  43.1 3.5 %logits.1 = (f32[1024,128]{1,0:T(8,128)S(1)}, f32[512,128]{1,0:T(8,128)S(1)}, f32[64,4,128]{2,1,0:T(4,128)}) custom-call(bf16[64,3840]{1,0:T(8,128)(2,1)S(1)} %pad_maximum_fusion.own_ref, bf16[64,3840]{1,0:T(8,128)(2,1)S(1)} %collective-permute-done.3.twin_ref, bf16[1010,3840]{1,0:T(8,128)(2,1)S(1)} %bitcast.11, ...), custom_call_target="tpu_custom_call" | custom-call | tf_op jit(solution)/shard_map/logits/pallas_call | solution.py:279
  46.6 0.5 collective-permute-start.8
  47.2 2.6 %all-to-all-start = ((f32[64,4,128]{2,1,0:T(4,128)}), f32[64,4,128]{2,1,0:T(4,128)S(1)}, u32[]{:S(2)}, u32[]{:S(2)}) async-start(f32[64,4,128]{2,1,0:T(4,128)} %get-tuple-element.17), calls=%async_computation | async-start | bytes 262144 | tf_op jit(solution)/shard_map/all_to_all | solution.py:293
  49.7 0.6 gram.1.gram_ref
  50.4 7.4 %all-to-all-done.recv_ref = f32[64,4,128]{2,1,0:T(4,128)S(1)} async-done(((f32[64,4,128]{2,1,0:T(4,128)}), f32[64,4,128]{2,1,0:T(4,128)S(1)}, u32[]{:S(2)}, u32[]{:S(2)}) %all-to-all-start) | async-done | bytes 131104 | tf_op jit(solution)/shard_map/all_to_all | solution.py:293
  57.8 0.9 %gradient.1 = (f32[32,4,128]{2,1,0:T(4,128)S(1)}, f32[8,128]{1,0:T(8,128)S(1)}) custom-call(f32[1024,128]{1,0:T(8,128)S(1)} %get-tuple-element.15.logits_ref, f32[512,128]{1,0:T(8,128)S(1)} %collective-permute-done.8.peer_ref, f32[64,4,128]{2,1,0:T(4,128)S(1)} %all-to-all-done.recv_ref, f32[128,128]{1,0:T(8,128)S(1)} %gram.1.gram_ref, s32[1]{0:T(128)} %bitcast.3.base_ref), custom_call_target="tpu_custom_call" | custom-call | tf_op jit(solution)/shard_map/gradient/pallas_call | solution.py:303
  58.7 9.2 %all_to_all.10.recv_ref = f32[32,4,128]{2,1,0:T(4,128)S(1)} all-to-all(f32[32,4,128]{2,1,0:T(4,128)S(1)} %get-tuple-element.18), channel_id=1, replica_groups=mesh['seq'=2,'depth'=2,'vocab'=8] {'seq','depth','vocab'}, dimensions={0} | all-to-all | bytes 131072 | tf_op jit(solution)/shard_map/all_to_all | solution.py:311
  67.9 0.6 final.1
  (26 shorter events, 0.3 us)
Async XLA Ops:
  0.6 41.2 %collective-permute-start.7 = (bf16[8,7168]{1,0:T(8,128)(2,1)}, bf16[8,7168]{1,0:T(8,128)(2,1)S(1)}, u32[]{:S(2)}, u32[]{:S(2)}) collective-permute-start(bf16[8,7168]{1,0:T(8,128)(2,1)} %bitcast.12), channel_id=1, source_target_pairs={{0,8},{8,0},{1,9},{9,1},{2,10},{10,2},{3,11},{11,3},{4,12},{12,4},... | collective-permute-start | bytes 344072 | tf_op jit(solution)/shard_map/ppermute | solution.py:32
  3.7 16.5 %collective-permute-start = (bf16[8,7168]{1,0:T(8,128)(2,1)}, bf16[8,7168]{1,0:T(8,128)(2,1)S(1)}, u32[]{:S(2)}, u32[]{:S(2)}) collective-permute-start(bf16[8,7168]{1,0:T(8,128)(2,1)} %bitcast.13), channel_id=1, source_target_pairs={{0,6},{1,7},{2,4},{3,5},{4,2},{5,3},{6,0},{7,1},{8,14},{9,15},{10,... | collective-permute-start | bytes 344072 | tf_op jit(solution)/shard_map/ppermute | solution.py:32
  11.0 2.8 %copy-start = (bf16[1010,3328]{1,0:T(8,128)(2,1)}, bf16[1010,3328]{1,0:T(8,128)(2,1)S(1)}, u32[]{:S(2)}) copy-start(bf16[1010,3328]{1,0:T(8,128)(2,1)S(1)} %shard_map.68.table_ref) | copy-start | bytes 20167684
  13.8 6.4 %copy-start.3 = (bf16[1,8,7168]{2,1,0:T(8,128)(2,1)S(1)}, bf16[1,8,7168]{2,1,0:T(8,128)(2,1)}, u32[]{:S(2)}) copy-start(bf16[1,8,7168]{2,1,0:T(8,128)(2,1)} %param.4) | copy-start | bytes 344068
  17.2 3.0 %copy-start.2 = (bf16[1010,3840]{1,0:T(8,128)(2,1)}, bf16[1010,3840]{1,0:T(8,128)(2,1)S(1)}, u32[]{:S(2)}) copy-start(bf16[1010,3840]{1,0:T(8,128)(2,1)S(1)} %shard_map.67.table_ref) | copy-start | bytes 23270404
  20.2 4.8 %collective-permute-start.4 = (bf16[16,3328]{1,0:T(8,128)(2,1)S(1)}, bf16[16,3328]{1,0:T(8,128)(2,1)S(1)}, u32[]{:S(2)}, u32[]{:S(2)}) collective-permute-start(bf16[16,3328]{1,0:T(8,128)(2,1)S(1)} %pad_maximum_fusion.4), channel_id=1, source_target_pairs={{0,1},{1,0},{2,3},{3,2},{4,5},{5,4},{6,7},{7,6},{8,9},{9,8},{10,11... | collective-permute-start | bytes 319496 | tf_op jit(solution)/shard_map/ppermute | solution.py:32
  21.8 5.9 %collective-permute-start.1 = (bf16[16,3840]{1,0:T(8,128)(2,1)S(1)}, bf16[16,3840]{1,0:T(8,128)(2,1)S(1)}, u32[]{:S(2)}, u32[]{:S(2)}) collective-permute-start(bf16[16,3840]{1,0:T(8,128)(2,1)S(1)} %fusion), channel_id=1, source_target_pairs={{0,2},{1,3},{2,0},{3,1},{4,6},{5,7},{6,4},{7,5},{8,10},{9,11},{10,... | collective-permute-start | bytes 368648 | tf_op jit(solution)/shard_map/ppermute | solution.py:32
  25.1 6.3 %collective-permute-start.5 = (bf16[32,3328]{1,0:T(8,128)(2,1)S(1)}, bf16[32,3328]{1,0:T(8,128)(2,1)S(1)}, u32[]{:S(2)}, u32[]{:S(2)}) collective-permute-start(bf16[32,3328]{1,0:T(8,128)(2,1)S(1)} %pad_maximum_fusion.3), channel_id=1, source_target_pairs={{0,2},{1,3},{2,0},{3,1},{4,6},{5,7},{6,4},{7,5},{8,10},{9,11},{10,... | collective-permute-start | bytes 638984 | tf_op jit(solution)/shard_map/ppermute | solution.py:32
  27.8 6.3 %collective-permute-start.2 = (bf16[32,3840]{1,0:T(8,128)(2,1)S(1)}, bf16[32,3840]{1,0:T(8,128)(2,1)S(1)}, u32[]{:S(2)}, u32[]{:S(2)}) collective-permute-start(bf16[32,3840]{1,0:T(8,128)(2,1)S(1)} %pad_maximum_fusion.2), channel_id=1, source_target_pairs={{0,1},{1,0},{2,3},{3,2},{4,5},{5,4},{6,7},{7,6},{8,9},{9,8},{10,11... | collective-permute-start | bytes 737288 | tf_op jit(solution)/shard_map/ppermute | solution.py:32
  34.1 7.7 %collective-permute-start.3 = (bf16[64,3840]{1,0:T(8,128)(2,1)S(1)}, bf16[64,3840]{1,0:T(8,128)(2,1)S(1)}, u32[]{:S(2)}, u32[]{:S(2)}) collective-permute-start(bf16[64,3840]{1,0:T(8,128)(2,1)S(1)} %pad_maximum_fusion.own_ref), channel_id=1, source_target_pairs={{0,16},{16,0},{1,17},{17,1},{2,18},{18,2},{3,19},{19,3},{4,20},{20... | collective-permute-start | bytes 1474568 | tf_op jit(solution)/shard_map/ppermute | solution.py:32
  34.2 2.4 %collective-permute-start.6 = (bf16[64,3328]{1,0:T(8,128)(2,1)S(1)}, bf16[64,3328]{1,0:T(8,128)(2,1)S(1)}, u32[]{:S(2)}, u32[]{:S(2)}) collective-permute-start(bf16[64,3328]{1,0:T(8,128)(2,1)S(1)} %pad_maximum_fusion.1.own_ref), channel_id=1, source_target_pairs={{0,16},{16,0},{1,17},{17,1},{2,18},{18,2},{3,19},{19,3},{4,20},{20... | collective-permute-start | bytes 1277960 | tf_op jit(solution)/shard_map/ppermute | solution.py:32
  36.7 2.9 %copy-start.1 = (bf16[1010,3328]{1,0:T(8,128)(2,1)S(1)}, bf16[1010,3328]{1,0:T(8,128)(2,1)}, u32[]{:S(2)}) copy-start(bf16[1010,3328]{1,0:T(8,128)(2,1)} %copy-done) | copy-start | bytes 20167684
  39.6 2.2 %slice-start = ((s8[7802880]{0:T(1024)(128)(4,1)}), s8[4194304]{0:T(1024)(128)(4,1)S(1)}, s32[]{:S(2)}) async-start(s8[7802880]{0:T(1024)(128)(4,1)} %bitcast.10), calls=%async_computation.2 | async-start | bytes 8388608
  40.6 2.5 %slice-start.1 = ((s8[7802880]{0:T(1024)(128)(4,1)}), s8[3608576]{0:T(1024)(128)(4,1)S(1)}, s32[]{:S(2)}) async-start(s8[7802880]{0:T(1024)(128)(4,1)} %bitcast.10), calls=%async_computation.3 | async-start | bytes 7217152
  46.6 11.2 %collective-permute-start.8 = (f32[512,128]{1,0:T(8,128)S(1)}, f32[512,128]{1,0:T(8,128)S(1)}, u32[]{:S(2)}, u32[]{:S(2)}) collective-permute-start(f32[512,128]{1,0:T(8,128)S(1)} %get-tuple-element.16), channel_id=1, source_target_pairs={{0,8},{8,0},{1,9},{9,1},{2,10},{10,2},{3,11},{11,3},{4,12},{12,4},... | collective-permute-start | bytes 786440 | tf_op jit(solution)/shard_map/ppermute | solution.py:32
  47.2 10.6 %all-to-all-start = ((f32[64,4,128]{2,1,0:T(4,128)}), f32[64,4,128]{2,1,0:T(4,128)S(1)}, u32[]{:S(2)}, u32[]{:S(2)}) async-start(f32[64,4,128]{2,1,0:T(4,128)} %get-tuple-element.17), calls=%async_computation | async-start | bytes 262144 | tf_op jit(solution)/shard_map/all_to_all | solution.py:293

commit v5 on v4

--- a/solution.py
+++ b/solution.py
@@ -13,8 +13,8 @@
 SCALE = 2.0**40
 WEIGHTS = (1.0, 0.3)
 LIMIT = 24 * 2**20
-PIECES = 2
-LEAN = -256
+PIECES = 1
+LEAN = 256
 VMEM = pl.BlockSpec(memory_space=pltpu.VMEM)
 
 
@@ -68,14 +68,14 @@
 
 def first_kernel(cut, own_ref, twin_ref, table_ref, logits_ref):
     states = merged(own_ref.at[:, :cut], twin_ref.at[:, :cut])
-    logits_ref[: table_ref.shape[0], :] = rows_dot(table_ref[:, :cut], states, (1, 1))
+    logits_ref[: table_ref.shape[0], :] = rows_dot(table_ref[...], states, (1, 1))
 
 
 def second_kernel(cut, own_ref, twin_ref, table_ref, first_ref, logits_ref, states_ref):
     states = merged(own_ref, twin_ref)
     states_ref[...] = states
     width = table_ref.shape[0]
-    logits_ref[:width, :] = first_ref[:width, :] + rows_dot(table_ref[:, cut:], states[:, cut:], (1, 1))
+    logits_ref[:width, :] = first_ref[:width, :] + rows_dot(table_ref[...], states[:, cut:], (1, 1))
 
 
 def gram_kernel(early_ref, own_ref, twin_ref, gram_ref):
@@ -245,8 +245,10 @@
 
     shape = lambda *dims: jax.ShapeDtypeStruct(dims, f32)
     params = pltpu.CompilerParams(vmem_limit_bytes=LIMIT)
+    cut = split // 2
+    fetches = ((0, cut), (cut, cut), (split, dim - split))
     tables = []
-    for start, columns in ((0, split), (split, dim - split)):
+    for start, columns in fetches:
         tables.append(
             pl.pallas_call(
                 functools.partial(fetch_kernel, start),
@@ -259,7 +261,6 @@
             )(pltpu.with_memory_space_constraint(embedding, pltpu.HBM))
         )
     tables = [pltpu.with_memory_space_constraint(table, pltpu.VMEM) for table in tables]
-    cut = split // 2
     first = pl.pallas_call(
         functools.partial(first_kernel, cut),
         in_specs=[VMEM] * 3,
@@ -275,7 +276,7 @@
         out_shape=[shape(2 * half, tokens), jax.ShapeDtypeStruct((tokens, split), hidden.dtype)],
         compiler_params=params,
         name="second",
-    )(left, left_twin, tables[0], first)
+    )(left, left_twin, tables[1], first)
     logits, send, pack = pl.pallas_call(
         functools.partial(logits_kernel, width, half, size),
         in_specs=[VMEM] * 7,
@@ -287,7 +288,7 @@
         ],
         compiler_params=params,
         name="logits",
-    )(right, right_twin, tables[1], early, states, side, meta)
+    )(right, right_twin, tables[2], early, states, side, meta)
 
     peer = moved(send, "depth", 1)
     recv = lax.all_to_all(pack, EVERY, 0, 0, tiled=True)

time: 68.8 us -> 68.5 us (level)
  waiting for transfers between devices: 20.9 us -> 15.9 us
  starting transfers between devices: 12.2 us -> 16.9 us
  local copies, waits for them, and re-layouts: 10.1 us -> 8.91 us
  Pallas kernels: 14.2 us -> 15.1 us
    ppermute x9, waiting for transfers between devices: 13.5 us -> 8.52 us  [moved(): lax.ppermute(value, axis, [(at, at ^ mask) for at in range(lax.axis_size(...]
    ppermute x9, starting transfers between devices: 9.59 us -> 12.9 us  [moved(): lax.ppermute(value, axis, [(at, at ^ mask) for at in range(lax.axis_size(...]
    all_to_all x1, starting transfers between devices: 2.57 us -> 4.04 us  [program(): recv = lax.all_to_all(pack, EVERY, 0, 0, tiled=True)]
    unnamed x12 -> x16, local copies, waits for them, and re-layouts: 10.1 us -> 8.91 us
    pallas_call x2 -> x3, Pallas kernels: 6.35 us -> 7.18 us  [program(): pl.pallas_call(functools.partial(fetch_kernel, start), in_specs=[pl.Block...]
  transfers between devices with their start and end apart: 10 -> 10, of which waited for: 6 -> 5; matrix products, arithmetic and copies ran while one was open for 2% -> 2% of each run, Pallas kernels for 13% -> 15%
where the time goes in v5:
time: 68.5 us; the launch traced here: 68.2 us
  starting transfers between devices  16.9 us (25%)
  waiting for transfers between devices  15.9 us (23%)
  Pallas kernels  15.1 us (22%)
  blocking collectives  9.24 us (13%)
  local copies, waits for them, and re-layouts  8.91 us (13%)
  other arithmetic  1.16 us (2%)
  between operations  0.87 us (1%)
    ppermute x9, starting transfers between devices, moved(): lax.ppermute(value, axis, [(at, at ^ mask) for at in range(lax.axis_size(...  12.9 us
    all_to_all x1, blocking collectives, program(): recv = lax.all_to_all(pack, EVERY, 0, 0, tiled=True)  9.24 us
    unnamed x16, local copies, waits for them, and re-layouts  8.91 us
    ppermute x9, waiting for transfers between devices, moved(): lax.ppermute(value, axis, [(at, at ^ mask) for at in range(lax.axis_size(...  8.52 us
    all_to_all x1, waiting for transfers between devices, program(): recv = lax.all_to_all(pack, EVERY, 0, 0, tiled=True)  7.42 us
    pallas_call x3, Pallas kernels, program(): pl.pallas_call(functools.partial(fetch_kernel, start), in_specs=[pl.Block...  7.18 us
    all_to_all x1, starting transfers between devices, program(): recv = lax.all_to_all(pack, EVERY, 0, 0, tiled=True)  4.04 us
    pallas_call x1, Pallas kernels, program(): pl.pallas_call(functools.partial(logits_kernel, width, half, size), in_sp...  3.24 us
  transfers between devices with their start and end apart: 10, of which 5 were waited for; matrix products, arithmetic and copies ran while one was open for 2% of the time, Pallas kernels for 15%

profile of v5, /device:TPU:0, one launch (start us, length us, event | category | flops | bytes accessed | tf_op | source)
XLA Modules:
  0.0 68.2 jit_solution(10254472039090688753)
XLA Ops:
  0.6 3.0 %collective-permute-start.7 = (bf16[8,7168]{1,0:T(8,128)(2,1)}, bf16[8,7168]{1,0:T(8,128)(2,1)S(1)}, u32[]{:S(2)}, u32[]{:S(2)}) collective-permute-start(bf16[8,7168]{1,0:T(8,128)(2,1)} %bitcast.12), channel_id=1, source_target_pairs={{0,8},{8,0},{1,9},{9,1},{2,10},{10,2},{3,11},{11,3},{4,12},{12,4},... | collective-permute-start | bytes 344072 | tf_op jit(solution)/shard_map/ppermute | solution.py:32
  3.7 3.6 %collective-permute-start = (bf16[8,7168]{1,0:T(8,128)(2,1)}, bf16[8,7168]{1,0:T(8,128)(2,1)S(1)}, u32[]{:S(2)}, u32[]{:S(2)}) collective-permute-start(bf16[8,7168]{1,0:T(8,128)(2,1)} %bitcast.13), channel_id=1, source_target_pairs={{0,6},{1,7},{2,4},{3,5},{4,2},{5,3},{6,0},{7,1},{8,14},{9,15},{10,... | collective-permute-start | bytes 344072 | tf_op jit(solution)/shard_map/ppermute | solution.py:32
  7.3 0.7 convert_bitcast_fusion
  7.9 2.1 %shard_map.69.table_ref = bf16[1010,1920]{1,0:T(8,128)(2,1)S(1)} custom-call(bf16[1010,7168]{1,0:T(8,128)(2,1)} %table_ref.5), custom_call_target="tpu_custom_call" | custom-call | bytes 7756800 | tf_op jit(solution)/shard_map/pallas_call | solution.py:253
  10.1 2.0 %copy-done.3 = bf16[1010,1920]{1,0:T(8,128)(2,1)} copy-done((bf16[1010,1920]{1,0:T(8,128)(2,1)}, bf16[1010,1920]{1,0:T(8,128)(2,1)S(1)}, u32[]{:S(2)}) %copy-start.3) | copy-done | bytes 3878424
  12.0 2.1 %shard_map.68.table_ref = bf16[1010,1920]{1,0:T(8,128)(2,1)S(1)} custom-call(bf16[1010,7168]{1,0:T(8,128)(2,1)} %table_ref.5), custom_call_target="tpu_custom_call" | custom-call | bytes 7756800 | tf_op jit(solution)/shard_map/pallas_call | solution.py:253
  14.2 2.0 %copy-done.1 = bf16[1010,1920]{1,0:T(8,128)(2,1)} copy-done((bf16[1010,1920]{1,0:T(8,128)(2,1)}, bf16[1010,1920]{1,0:T(8,128)(2,1)S(1)}, u32[]{:S(2)}) %copy-start.1) | copy-done | bytes 3878424
  16.2 3.0 %shard_map.67.table_ref = bf16[1010,3328]{1,0:T(8,128)(2,1)S(1)} custom-call(bf16[1010,7168]{1,0:T(8,128)(2,1)} %table_ref.5), custom_call_target="tpu_custom_call" | custom-call | bytes 13445120 | tf_op jit(solution)/shard_map/pallas_call | solution.py:253
  19.1 2.8 %copy-done = bf16[1010,3328]{1,0:T(8,128)(2,1)} copy-done((bf16[1010,3328]{1,0:T(8,128)(2,1)}, bf16[1010,3328]{1,0:T(8,128)(2,1)S(1)}, u32[]{:S(2)}) %copy-start) | copy-done | bytes 6722584
  22.0 0.1 collective-permute-start.1
  22.1 1.6 %collective-permute-start.4 = (bf16[16,3840]{1,0:T(8,128)(2,1)S(1)}, bf16[16,3840]{1,0:T(8,128)(2,1)S(1)}, u32[]{:S(2)}, u32[]{:S(2)}) collective-permute-start(bf16[16,3840]{1,0:T(8,128)(2,1)S(1)} %pad_maximum_fusion.4), channel_id=1, source_target_pairs={{0,1},{1,0},{2,3},{3,2},{4,5},{5,4},{6,7},{7,6},{8,9},{9,8},{10,11... | collective-permute-start | bytes 368648 | tf_op jit(solution)/shard_map/ppermute | solution.py:32
  23.7 3.1 %collective-permute-done.1 = bf16[16,3328]{1,0:T(8,128)(2,1)S(1)} collective-permute-done((bf16[16,3328]{1,0:T(8,128)(2,1)S(1)}, bf16[16,3328]{1,0:T(8,128)(2,1)S(1)}, u32[]{:S(2)}, u32[]{:S(2)}) %collective-permute-start.1) | collective-permute-done | bytes 106528 | tf_op jit(solution)/shard_map/ppermute | solution.py:32
  26.9 1.6 %collective-permute-start.2 = (bf16[32,3328]{1,0:T(8,128)(2,1)S(1)}, bf16[32,3328]{1,0:T(8,128)(2,1)S(1)}, u32[]{:S(2)}, u32[]{:S(2)}) collective-permute-start(bf16[32,3328]{1,0:T(8,128)(2,1)S(1)} %pad_maximum_fusion.3), channel_id=1, source_target_pairs={{0,1},{1,0},{2,3},{3,2},{4,5},{5,4},{6,7},{7,6},{8,9},{9,8},{10,11... | collective-permute-start | bytes 638984 | tf_op jit(solution)/shard_map/ppermute | solution.py:32
  28.5 1.9 %collective-permute-start.5 = (bf16[32,3840]{1,0:T(8,128)(2,1)S(1)}, bf16[32,3840]{1,0:T(8,128)(2,1)S(1)}, u32[]{:S(2)}, u32[]{:S(2)}) collective-permute-start(bf16[32,3840]{1,0:T(8,128)(2,1)S(1)} %pad_maximum_fusion.2), channel_id=1, source_target_pairs={{0,2},{1,3},{2,0},{3,1},{4,6},{5,7},{6,4},{7,5},{8,10},{9,11},{10,... | collective-permute-start | bytes 737288 | tf_op jit(solution)/shard_map/ppermute | solution.py:32
  30.4 2.4 %collective-permute-done.2 = bf16[32,3328]{1,0:T(8,128)(2,1)S(1)} collective-permute-done((bf16[32,3328]{1,0:T(8,128)(2,1)S(1)}, bf16[32,3328]{1,0:T(8,128)(2,1)S(1)}, u32[]{:S(2)}, u32[]{:S(2)}) %collective-permute-start.2) | collective-permute-done | bytes 213024 | tf_op jit(solution)/shard_map/ppermute | solution.py:32
  32.8 1.9 %collective-permute-done.5 = bf16[32,3840]{1,0:T(8,128)(2,1)S(1)} collective-permute-done((bf16[32,3840]{1,0:T(8,128)(2,1)S(1)}, bf16[32,3840]{1,0:T(8,128)(2,1)S(1)}, u32[]{:S(2)}, u32[]{:S(2)}) %collective-permute-start.5) | collective-permute-done | bytes 245792 | tf_op jit(solution)/shard_map/ppermute | solution.py:32
  34.8 0.1 broadcast_select_fusion.1
  35.0 0.6 collective-permute-start.3
  35.6 0.1 select_reduce_fusion.1
  35.6 0.1 select_select_fusion.meta_ref
  35.7 1.1 %collective-permute-done.6.twin_ref = bf16[64,3840]{1,0:T(8,128)(2,1)S(1)} collective-permute-done((bf16[64,3840]{1,0:T(8,128)(2,1)S(1)}, bf16[64,3840]{1,0:T(8,128)(2,1)S(1)}, u32[]{:S(2)}, u32[]{:S(2)}) %collective-permute-start.6) | collective-permute-done | bytes 491552 | tf_op jit(solution)/shard_map/ppermute | solution.py:32
  36.8 2.1 %copy-done.4 = bf16[1010,1920]{1,0:T(8,128)(2,1)S(1)} copy-done((bf16[1010,1920]{1,0:T(8,128)(2,1)S(1)}, bf16[1010,1920]{1,0:T(8,128)(2,1)}, u32[]{:S(2)}) %copy-start.4) | copy-done | bytes 3878424
  38.9 1.2 %first.1.first_ref = f32[1024,128]{1,0:T(8,128)S(1)} custom-call(bf16[64,3840]{1,0:T(8,128)(2,1)S(1)} %pad_maximum_fusion.own_ref, bf16[64,3840]{1,0:T(8,128)(2,1)S(1)} %collective-permute-done.6.twin_ref, bf16[1010,1920]{1,0:T(8,128)(2,1)S(1)} %copy-done.4), custom_call_target="tpu_custom_call" | custom-call | tf_op jit(solution)/shard_map/first/pallas_call | solution.py:264
  40.1 1.3 %second.1 = (f32[1024,128]{1,0:T(8,128)S(1)}, bf16[128,3840]{1,0:T(8,128)(2,1)S(1)}) custom-call(bf16[64,3840]{1,0:T(8,128)(2,1)S(1)} %pad_maximum_fusion.own_ref, bf16[64,3840]{1,0:T(8,128)(2,1)S(1)} %collective-permute-done.6.twin_ref, bf16[1010,1920]{1,0:T(8,128)(2,1)S(1)} %copy-done.2, f32[1024,128]{1,0:T(8,128)S(1)} %first.1.first_ref), custom_call_target="tpu_custom_call" | custom-call | tf_op jit(solution)/shard_map/second/pallas_call | solution.py:272
  41.4 3.2 %logits.1 = (f32[1024,128]{1,0:T(8,128)S(1)}, f32[512,128]{1,0:T(8,128)S(1)}, f32[64,4,128]{2,1,0:T(4,128)}) custom-call(bf16[64,3328]{1,0:T(8,128)(2,1)S(1)} %pad_maximum_fusion.1.own_ref, bf16[64,3328]{1,0:T(8,128)(2,1)S(1)} %collective-permute-done.3.twin_ref, bf16[1010,3328]{1,0:T(8,128)(2,1)S(1)} %bitcast.11, ...), custom_call_target="tpu_custom_call" | custom-call | tf_op jit(solution)/shard_map/logits/pallas_call | solution.py:280
  44.7 0.5 collective-permute-start.8
  45.2 4.0 %all-to-all-start = ((f32[64,4,128]{2,1,0:T(4,128)}), f32[64,4,128]{2,1,0:T(4,128)S(1)}, u32[]{:S(2)}, u32[]{:S(2)}) async-start(f32[64,4,128]{2,1,0:T(4,128)} %get-tuple-element.17), calls=%async_computation | async-start | bytes 262144 | tf_op jit(solution)/shard_map/all_to_all | solution.py:294
  49.3 0.6 gram.1.gram_ref
  49.9 7.4 %all-to-all-done.recv_ref = f32[64,4,128]{2,1,0:T(4,128)S(1)} async-done(((f32[64,4,128]{2,1,0:T(4,128)}), f32[64,4,128]{2,1,0:T(4,128)S(1)}, u32[]{:S(2)}, u32[]{:S(2)}) %all-to-all-start) | async-done | bytes 131104 | tf_op jit(solution)/shard_map/all_to_all | solution.py:294
  57.3 0.9 %gradient.1 = (f32[32,4,128]{2,1,0:T(4,128)S(1)}, f32[8,128]{1,0:T(8,128)S(1)}) custom-call(f32[1024,128]{1,0:T(8,128)S(1)} %get-tuple-element.15.logits_ref, f32[512,128]{1,0:T(8,128)S(1)} %collective-permute-done.8.peer_ref, f32[64,4,128]{2,1,0:T(4,128)S(1)} %all-to-all-done.recv_ref, f32[128,128]{1,0:T(8,128)S(1)} %gram.1.gram_ref, s32[1]{0:T(128)} %bitcast.3.base_ref), custom_call_target="tpu_custom_call" | custom-call | tf_op jit(solution)/shard_map/gradient/pallas_call | solution.py:304
  58.3 9.2 %all_to_all.10.recv_ref = f32[32,4,128]{2,1,0:T(4,128)S(1)} all-to-all(f32[32,4,128]{2,1,0:T(4,128)S(1)} %get-tuple-element.18), channel_id=1, replica_groups=mesh['seq'=2,'depth'=2,'vocab'=8] {'seq','depth','vocab'}, dimensions={0} | all-to-all | bytes 131072 | tf_op jit(solution)/shard_map/all_to_all | solution.py:312
  67.5 0.6 final.1
  (31 shorter events, 0.3 us)
Async XLA Ops:
  0.6 40.8 %collective-permute-start.7 = (bf16[8,7168]{1,0:T(8,128)(2,1)}, bf16[8,7168]{1,0:T(8,128)(2,1)S(1)}, u32[]{:S(2)}, u32[]{:S(2)}) collective-permute-start(bf16[8,7168]{1,0:T(8,128)(2,1)} %bitcast.12), channel_id=1, source_target_pairs={{0,8},{8,0},{1,9},{9,1},{2,10},{10,2},{3,11},{11,3},{4,12},{12,4},... | collective-permute-start | bytes 344072 | tf_op jit(solution)/shard_map/ppermute | solution.py:32
  3.7 18.3 %collective-permute-start = (bf16[8,7168]{1,0:T(8,128)(2,1)}, bf16[8,7168]{1,0:T(8,128)(2,1)S(1)}, u32[]{:S(2)}, u32[]{:S(2)}) collective-permute-start(bf16[8,7168]{1,0:T(8,128)(2,1)} %bitcast.13), channel_id=1, source_target_pairs={{0,6},{1,7},{2,4},{3,5},{4,2},{5,3},{6,0},{7,1},{8,14},{9,15},{10,... | collective-permute-start | bytes 344072 | tf_op jit(solution)/shard_map/ppermute | solution.py:32
  10.1 2.0 %copy-start.3 = (bf16[1010,1920]{1,0:T(8,128)(2,1)}, bf16[1010,1920]{1,0:T(8,128)(2,1)S(1)}, u32[]{:S(2)}) copy-start(bf16[1010,1920]{1,0:T(8,128)(2,1)S(1)} %shard_map.69.table_ref) | copy-start | bytes 11635204
  14.2 2.0 %copy-start.1 = (bf16[1010,1920]{1,0:T(8,128)(2,1)}, bf16[1010,1920]{1,0:T(8,128)(2,1)S(1)}, u32[]{:S(2)}) copy-start(bf16[1010,1920]{1,0:T(8,128)(2,1)S(1)} %shard_map.68.table_ref) | copy-start | bytes 11635204
  16.2 5.8 %copy-start.5 = (bf16[1,8,7168]{2,1,0:T(8,128)(2,1)S(1)}, bf16[1,8,7168]{2,1,0:T(8,128)(2,1)}, u32[]{:S(2)}) copy-start(bf16[1,8,7168]{2,1,0:T(8,128)(2,1)} %param.4) | copy-start | bytes 344068
  19.1 2.8 %copy-start = (bf16[1010,3328]{1,0:T(8,128)(2,1)}, bf16[1010,3328]{1,0:T(8,128)(2,1)S(1)}, u32[]{:S(2)}) copy-start(bf16[1010,3328]{1,0:T(8,128)(2,1)S(1)} %shard_map.67.table_ref) | copy-start | bytes 20167684
  22.0 18.1 %copy-start.2 = (bf16[1010,1920]{1,0:T(8,128)(2,1)S(1)}, bf16[1010,1920]{1,0:T(8,128)(2,1)}, u32[]{:S(2)}) copy-start(bf16[1010,1920]{1,0:T(8,128)(2,1)} %copy-done.1) | copy-start | bytes 11635204
  22.0 4.8 %collective-permute-start.1 = (bf16[16,3328]{1,0:T(8,128)(2,1)S(1)}, bf16[16,3328]{1,0:T(8,128)(2,1)S(1)}, u32[]{:S(2)}, u32[]{:S(2)}) collective-permute-start(bf16[16,3328]{1,0:T(8,128)(2,1)S(1)} %pad_maximum_fusion.5), channel_id=1, source_target_pairs={{0,2},{1,3},{2,0},{3,1},{4,6},{5,7},{6,4},{7,5},{8,10},{9,11},{10,... | collective-permute-start | bytes 319496 | tf_op jit(solution)/shard_map/ppermute | solution.py:32
  22.1 6.3 %collective-permute-start.4 = (bf16[16,3840]{1,0:T(8,128)(2,1)S(1)}, bf16[16,3840]{1,0:T(8,128)(2,1)S(1)}, u32[]{:S(2)}, u32[]{:S(2)}) collective-permute-start(bf16[16,3840]{1,0:T(8,128)(2,1)S(1)} %pad_maximum_fusion.4), channel_id=1, source_target_pairs={{0,1},{1,0},{2,3},{3,2},{4,5},{5,4},{6,7},{7,6},{8,9},{9,8},{10,11... | collective-permute-start | bytes 368648 | tf_op jit(solution)/shard_map/ppermute | solution.py:32
  26.9 5.9 %collective-permute-start.2 = (bf16[32,3328]{1,0:T(8,128)(2,1)S(1)}, bf16[32,3328]{1,0:T(8,128)(2,1)S(1)}, u32[]{:S(2)}, u32[]{:S(2)}) collective-permute-start(bf16[32,3328]{1,0:T(8,128)(2,1)S(1)} %pad_maximum_fusion.3), channel_id=1, source_target_pairs={{0,1},{1,0},{2,3},{3,2},{4,5},{5,4},{6,7},{7,6},{8,9},{9,8},{10,11... | collective-permute-start | bytes 638984 | tf_op jit(solution)/shard_map/ppermute | solution.py:32
  28.5 6.3 %collective-permute-start.5 = (bf16[32,3840]{1,0:T(8,128)(2,1)S(1)}, bf16[32,3840]{1,0:T(8,128)(2,1)S(1)}, u32[]{:S(2)}, u32[]{:S(2)}) collective-permute-start(bf16[32,3840]{1,0:T(8,128)(2,1)S(1)} %pad_maximum_fusion.2), channel_id=1, source_target_pairs={{0,2},{1,3},{2,0},{3,1},{4,6},{5,7},{6,4},{7,5},{8,10},{9,11},{10,... | collective-permute-start | bytes 737288 | tf_op jit(solution)/shard_map/ppermute | solution.py:32
  32.8 8.6 %slice-start = ((s8[6762496]{0:T(1024)(128)(4,1)}), s8[4194304]{0:T(1024)(128)(4,1)S(1)}, s32[]{:S(2)}) async-start(s8[6762496]{0:T(1024)(128)(4,1)} %bitcast.10), calls=%async_computation.2 | async-start | bytes 8388608
  34.9 1.9 %collective-permute-start.6 = (bf16[64,3840]{1,0:T(8,128)(2,1)S(1)}, bf16[64,3840]{1,0:T(8,128)(2,1)S(1)}, u32[]{:S(2)}, u32[]{:S(2)}) collective-permute-start(bf16[64,3840]{1,0:T(8,128)(2,1)S(1)} %pad_maximum_fusion.own_ref), channel_id=1, source_target_pairs={{0,16},{16,0},{1,17},{17,1},{2,18},{18,2},{3,19},{19,3},{4,20},{20... | collective-permute-start | bytes 1474568 | tf_op jit(solution)/shard_map/ppermute | solution.py:32
  35.0 6.4 %collective-permute-start.3 = (bf16[64,3328]{1,0:T(8,128)(2,1)S(1)}, bf16[64,3328]{1,0:T(8,128)(2,1)S(1)}, u32[]{:S(2)}, u32[]{:S(2)}) collective-permute-start(bf16[64,3328]{1,0:T(8,128)(2,1)S(1)} %pad_maximum_fusion.1.own_ref), channel_id=1, source_target_pairs={{0,16},{16,0},{1,17},{17,1},{2,18},{18,2},{3,19},{19,3},{4,20},{20... | collective-permute-start | bytes 1277960 | tf_op jit(solution)/shard_map/ppermute | solution.py:32
  35.7 5.7 %slice-start.1 = ((s8[6762496]{0:T(1024)(128)(4,1)}), s8[2568192]{0:T(1024)(128)(4,1)S(1)}, s32[]{:S(2)}) async-start(s8[6762496]{0:T(1024)(128)(4,1)} %bitcast.10), calls=%async_computation.3 | async-start | bytes 5136384
  36.8 2.1 %copy-start.4 = (bf16[1010,1920]{1,0:T(8,128)(2,1)S(1)}, bf16[1010,1920]{1,0:T(8,128)(2,1)}, u32[]{:S(2)}) copy-start(bf16[1010,1920]{1,0:T(8,128)(2,1)} %copy-done.3) | copy-start | bytes 11635204
  44.7 12.7 %collective-permute-start.8 = (f32[512,128]{1,0:T(8,128)S(1)}, f32[512,128]{1,0:T(8,128)S(1)}, u32[]{:S(2)}, u32[]{:S(2)}) collective-permute-start(f32[512,128]{1,0:T(8,128)S(1)} %get-tuple-element.16), channel_id=1, source_target_pairs={{0,8},{8,0},{1,9},{9,1},{2,10},{10,2},{3,11},{11,3},{4,12},{12,4},... | collective-permute-start | bytes 786440 | tf_op jit(solution)/shard_map/ppermute | solution.py:32
  45.2 12.1 %all-to-all-start = ((f32[64,4,128]{2,1,0:T(4,128)}), f32[64,4,128]{2,1,0:T(4,128)S(1)}, u32[]{:S(2)}, u32[]{:S(2)}) async-start(f32[64,4,128]{2,1,0:T(4,128)} %get-tuple-element.17), calls=%async_computation | async-start | bytes 262144 | tf_op jit(solution)/shard_map/all_to_all | solution.py:294

commit v6 on v4

--- a/solution.py
+++ b/solution.py
@@ -119,7 +119,7 @@
 
 
 def gradient_kernel(
-    steps, width, half, sizes, logits_ref, peer_ref, recv_ref, gram_ref, base_ref, pack_ref, keep_ref
+    steps, width, half, sizes, logits_ref, peer_ref, recv_ref, gram_ref, pack_ref, keep_ref
 ):
     cores, vocabs, count = sizes
     depth = lax.axis_index("depth")
@@ -148,7 +148,7 @@
         vectors = jnp.where(rows == at, vector, vectors)
     keep_ref[...] = vectors
 
-    base = base_ref[0]
+    base = (lax.axis_index("seq") * vocabs + lax.axis_index("vocab")) * width
     shift = pl.multiple_of(depth * half, 8)
 
     def gradient(logits, at, start):
@@ -210,7 +210,6 @@
     tokens = cores * vocabs * count
     size = cores * depths * vocabs
     steps = exchange_steps(vocabs)
-    place = lax.axis_index(GROUP)
     sizes = (cores, vocabs, count)
     f32 = jnp.float32
     split = dim // 2 + LEAN
@@ -299,15 +298,14 @@
         compiler_params=params,
         name="gram",
     )(states, right, right_twin)
-    base = (place * width).astype(jnp.int32).reshape(1)
     pack, keep = pl.pallas_call(
         functools.partial(gradient_kernel, steps, width, half, sizes),
-        in_specs=[VMEM] * 4 + [pl.BlockSpec(memory_space=pltpu.SMEM)],
+        in_specs=[VMEM] * 4,
         out_specs=[VMEM] * 2,
         out_shape=[shape(size, 4, tokens), shape(8, tokens)],
         compiler_params=params,
         name="gradient",
-    )(logits, peer, recv, gram, base)
+    )(logits, peer, recv, gram)
     recv = lax.all_to_all(pack, EVERY, 0, 0, tiled=True)
     nll, loss, norm = pl.pallas_call(
         functools.partial(final_kernel, steps, sizes),

time: 68.8 us -> 68.8 us (level)
  no operation moved by 1% of the time
where the time goes in v6:
time: 68.8 us; the launch traced here: 68.5 us
  waiting for transfers between devices  20.9 us (30%)
  Pallas kernels  14.2 us (21%)
  starting transfers between devices  12.2 us (18%)
  local copies, waits for them, and re-layouts  10.1 us (15%)
  blocking collectives  9.15 us (13%)
  other arithmetic  1.15 us (2%)
  between operations  0.84 us (1%)
    ppermute x9, waiting for transfers between devices, moved(): lax.ppermute(value, axis, [(at, at ^ mask) for at in range(lax.axis_size(...  13.5 us
    unnamed x12, local copies, waits for them, and re-layouts  10.1 us
    ppermute x9, starting transfers between devices, moved(): lax.ppermute(value, axis, [(at, at ^ mask) for at in range(lax.axis_size(...  9.59 us
    all_to_all x1, blocking collectives, program(): recv = lax.all_to_all(pack, EVERY, 0, 0, tiled=True)  9.15 us
    all_to_all x1, waiting for transfers between devices, program(): recv = lax.all_to_all(pack, EVERY, 0, 0, tiled=True)  7.41 us
    pallas_call x2, Pallas kernels, program(): pl.pallas_call(functools.partial(fetch_kernel, start), in_specs=[pl.Block...  6.35 us
    pallas_call x1, Pallas kernels, program(): pl.pallas_call(functools.partial(logits_kernel, width, half, size), in_sp...  3.51 us
    all_to_all x1, starting transfers between devices, program(): recv = lax.all_to_all(pack, EVERY, 0, 0, tiled=True)  2.57 us
  transfers between devices with their start and end apart: 10, of which 6 were waited for; matrix products, arithmetic and copies ran while one was open for 2% of the time, Pallas kernels for 13%

profile of v6, /device:TPU:0, one launch (start us, length us, event | category | flops | bytes accessed | tf_op | source)
XLA Modules:
  0.0 68.5 jit_solution(8526495704437160711)
XLA Ops:
  0.6 3.0 %collective-permute-start.7 = (bf16[8,7168]{1,0:T(8,128)(2,1)}, bf16[8,7168]{1,0:T(8,128)(2,1)S(1)}, u32[]{:S(2)}, u32[]{:S(2)}) collective-permute-start(bf16[8,7168]{1,0:T(8,128)(2,1)} %bitcast.11), channel_id=1, source_target_pairs={{0,8},{8,0},{1,9},{9,1},{2,10},{10,2},{3,11},{11,3},{4,12},{12,4},... | collective-permute-start | bytes 344072 | tf_op jit(solution)/shard_map/ppermute | solution.py:32
  3.7 3.6 %collective-permute-start = (bf16[8,7168]{1,0:T(8,128)(2,1)}, bf16[8,7168]{1,0:T(8,128)(2,1)S(1)}, u32[]{:S(2)}, u32[]{:S(2)}) collective-permute-start(bf16[8,7168]{1,0:T(8,128)(2,1)} %bitcast.12), channel_id=1, source_target_pairs={{0,6},{1,7},{2,4},{3,5},{4,2},{5,3},{6,0},{7,1},{8,14},{9,15},{10,... | collective-permute-start | bytes 344072 | tf_op jit(solution)/shard_map/ppermute | solution.py:32
  7.3 0.7 convert_bitcast_fusion
  7.9 3.0 %shard_map.68.table_ref = bf16[1010,3328]{1,0:T(8,128)(2,1)S(1)} custom-call(bf16[1010,7168]{1,0:T(8,128)(2,1)} %table_ref.3), custom_call_target="tpu_custom_call" | custom-call | bytes 13445120 | tf_op jit(solution)/shard_map/pallas_call | solution.py:250
  11.0 2.8 %copy-done = bf16[1010,3328]{1,0:T(8,128)(2,1)} copy-done((bf16[1010,3328]{1,0:T(8,128)(2,1)}, bf16[1010,3328]{1,0:T(8,128)(2,1)S(1)}, u32[]{:S(2)}) %copy-start) | copy-done | bytes 6722584
  13.8 3.3 %shard_map.67.table_ref = bf16[1010,3840]{1,0:T(8,128)(2,1)S(1)} custom-call(bf16[1010,7168]{1,0:T(8,128)(2,1)} %table_ref.3), custom_call_target="tpu_custom_call" | custom-call | bytes 15513600 | tf_op jit(solution)/shard_map/pallas_call | solution.py:250
  17.2 3.0 %copy-done.2 = bf16[1010,3840]{1,0:T(8,128)(2,1)} copy-done((bf16[1010,3840]{1,0:T(8,128)(2,1)}, bf16[1010,3840]{1,0:T(8,128)(2,1)S(1)}, u32[]{:S(2)}) %copy-start.2) | copy-done | bytes 7756824
  20.2 1.6 %collective-permute-start.4 = (bf16[16,3328]{1,0:T(8,128)(2,1)S(1)}, bf16[16,3328]{1,0:T(8,128)(2,1)S(1)}, u32[]{:S(2)}, u32[]{:S(2)}) collective-permute-start(bf16[16,3328]{1,0:T(8,128)(2,1)S(1)} %pad_maximum_fusion.4), channel_id=1, source_target_pairs={{0,1},{1,0},{2,3},{3,2},{4,5},{5,4},{6,7},{7,6},{8,9},{9,8},{10,11... | collective-permute-start | bytes 319496 | tf_op jit(solution)/shard_map/ppermute | solution.py:32
  21.8 0.1 collective-permute-start.1
  21.9 3.1 %collective-permute-done.4 = bf16[16,3328]{1,0:T(8,128)(2,1)S(1)} collective-permute-done((bf16[16,3328]{1,0:T(8,128)(2,1)S(1)}, bf16[16,3328]{1,0:T(8,128)(2,1)S(1)}, u32[]{:S(2)}, u32[]{:S(2)}) %collective-permute-start.4) | collective-permute-done | bytes 106528 | tf_op jit(solution)/shard_map/ppermute | solution.py:32
  25.1 0.1 collective-permute-start.5
  25.1 2.6 %collective-permute-done.1 = bf16[16,3840]{1,0:T(8,128)(2,1)S(1)} collective-permute-done((bf16[16,3840]{1,0:T(8,128)(2,1)S(1)}, bf16[16,3840]{1,0:T(8,128)(2,1)S(1)}, u32[]{:S(2)}, u32[]{:S(2)}) %collective-permute-start.1) | collective-permute-done | bytes 122912 | tf_op jit(solution)/shard_map/ppermute | solution.py:32
  27.8 0.1 collective-permute-start.2
  27.9 3.5 %collective-permute-done.5 = bf16[32,3328]{1,0:T(8,128)(2,1)S(1)} collective-permute-done((bf16[32,3328]{1,0:T(8,128)(2,1)S(1)}, bf16[32,3328]{1,0:T(8,128)(2,1)S(1)}, u32[]{:S(2)}, u32[]{:S(2)}) %collective-permute-start.5) | collective-permute-done | bytes 213024 | tf_op jit(solution)/shard_map/ppermute | solution.py:32
  31.4 0.1 broadcast_select_fusion.1
  31.4 2.6 %collective-permute-done.2 = bf16[32,3840]{1,0:T(8,128)(2,1)S(1)} collective-permute-done((bf16[32,3840]{1,0:T(8,128)(2,1)S(1)}, bf16[32,3840]{1,0:T(8,128)(2,1)S(1)}, u32[]{:S(2)}, u32[]{:S(2)}) %collective-permute-start.2) | collective-permute-done | bytes 245792 | tf_op jit(solution)/shard_map/ppermute | solution.py:32
  34.2 0.6 collective-permute-start.6
  34.8 0.1 select_reduce_fusion.1
  34.9 0.1 select_select_fusion.meta_ref
  35.0 1.7 %collective-permute-done.6.twin_ref = bf16[64,3328]{1,0:T(8,128)(2,1)S(1)} collective-permute-done((bf16[64,3328]{1,0:T(8,128)(2,1)S(1)}, bf16[64,3328]{1,0:T(8,128)(2,1)S(1)}, u32[]{:S(2)}, u32[]{:S(2)}) %collective-permute-start.6) | collective-permute-done | bytes 426016 | tf_op jit(solution)/shard_map/ppermute | solution.py:32
  36.7 2.9 %copy-done.1 = bf16[1010,3328]{1,0:T(8,128)(2,1)S(1)} copy-done((bf16[1010,3328]{1,0:T(8,128)(2,1)S(1)}, bf16[1010,3328]{1,0:T(8,128)(2,1)}, u32[]{:S(2)}) %copy-start.1) | copy-done | bytes 6722584
  39.6 1.1 %first.1.first_ref = f32[1024,128]{1,0:T(8,128)S(1)} custom-call(bf16[64,3328]{1,0:T(8,128)(2,1)S(1)} %pad_maximum_fusion.1.own_ref, bf16[64,3328]{1,0:T(8,128)(2,1)S(1)} %collective-permute-done.6.twin_ref, bf16[1010,3328]{1,0:T(8,128)(2,1)S(1)} %copy-done.1), custom_call_target="tpu_custom_call" | custom-call | tf_op jit(solution)/shard_map/first/pallas_call | solution.py:262
  40.7 1.1 %second.1 = (f32[1024,128]{1,0:T(8,128)S(1)}, bf16[128,3328]{1,0:T(8,128)(2,1)S(1)}) custom-call(bf16[64,3328]{1,0:T(8,128)(2,1)S(1)} %pad_maximum_fusion.1.own_ref, bf16[64,3328]{1,0:T(8,128)(2,1)S(1)} %collective-permute-done.6.twin_ref, bf16[1010,3328]{1,0:T(8,128)(2,1)S(1)} %copy-done.1, f32[1024,128]{1,0:T(8,128)S(1)} %first.1.first_ref), custom_call_target="tpu_custom_call" | custom-call | tf_op jit(solution)/shard_map/second/pallas_call | solution.py:270
  41.8 1.3 %slice-done.1 = s8[3608576]{0:T(1024)(128)(4,1)S(1)} async-done(((s8[7802880]{0:T(1024)(128)(4,1)}), s8[3608576]{0:T(1024)(128)(4,1)S(1)}, s32[]{:S(2)}) %slice-start.1) | async-done | bytes 3608600
  43.1 3.5 %logits.1 = (f32[1024,128]{1,0:T(8,128)S(1)}, f32[512,128]{1,0:T(8,128)S(1)}, f32[64,4,128]{2,1,0:T(4,128)}) custom-call(bf16[64,3840]{1,0:T(8,128)(2,1)S(1)} %pad_maximum_fusion.own_ref, bf16[64,3840]{1,0:T(8,128)(2,1)S(1)} %collective-permute-done.3.twin_ref, bf16[1010,3840]{1,0:T(8,128)(2,1)S(1)} %bitcast.10, ...), custom_call_target="tpu_custom_call" | custom-call | tf_op jit(solution)/shard_map/logits/pallas_call | solution.py:278
  46.6 0.5 collective-permute-start.8
  47.2 2.6 %all-to-all-start = ((f32[64,4,128]{2,1,0:T(4,128)}), f32[64,4,128]{2,1,0:T(4,128)S(1)}, u32[]{:S(2)}, u32[]{:S(2)}) async-start(f32[64,4,128]{2,1,0:T(4,128)} %get-tuple-element.17), calls=%async_computation | async-start | bytes 262144 | tf_op jit(solution)/shard_map/all_to_all | solution.py:292
  49.7 0.7 gram.1.gram_ref
  50.4 7.4 %all-to-all-done.recv_ref = f32[64,4,128]{2,1,0:T(4,128)S(1)} async-done(((f32[64,4,128]{2,1,0:T(4,128)}), f32[64,4,128]{2,1,0:T(4,128)S(1)}, u32[]{:S(2)}, u32[]{:S(2)}) %all-to-all-start) | async-done | bytes 131104 | tf_op jit(solution)/shard_map/all_to_all | solution.py:292
  57.8 0.9 %gradient.1 = (f32[32,4,128]{2,1,0:T(4,128)S(1)}, f32[8,128]{1,0:T(8,128)S(1)}) custom-call(f32[1024,128]{1,0:T(8,128)S(1)} %get-tuple-element.15.logits_ref, f32[512,128]{1,0:T(8,128)S(1)} %collective-permute-done.8.peer_ref, f32[64,4,128]{2,1,0:T(4,128)S(1)} %all-to-all-done.recv_ref, f32[128,128]{1,0:T(8,128)S(1)} %gram.1.gram_ref), custom_call_target="tpu_custom_call" | custom-call | tf_op jit(solution)/shard_map/gradient/pallas_call | solution.py:301
  58.7 9.2 %all_to_all.10.recv_ref = f32[32,4,128]{2,1,0:T(4,128)S(1)} all-to-all(f32[32,4,128]{2,1,0:T(4,128)S(1)} %get-tuple-element.18), channel_id=1, replica_groups=mesh['seq'=2,'depth'=2,'vocab'=8] {'seq','depth','vocab'}, dimensions={0} | all-to-all | bytes 131072 | tf_op jit(solution)/shard_map/all_to_all | solution.py:309
  67.9 0.6 final.1
  (26 shorter events, 0.3 us)
Async XLA Ops:
  0.6 41.2 %collective-permute-start.7 = (bf16[8,7168]{1,0:T(8,128)(2,1)}, bf16[8,7168]{1,0:T(8,128)(2,1)S(1)}, u32[]{:S(2)}, u32[]{:S(2)}) collective-permute-start(bf16[8,7168]{1,0:T(8,128)(2,1)} %bitcast.11), channel_id=1, source_target_pairs={{0,8},{8,0},{1,9},{9,1},{2,10},{10,2},{3,11},{11,3},{4,12},{12,4},... | collective-permute-start | bytes 344072 | tf_op jit(solution)/shard_map/ppermute | solution.py:32
  3.7 16.5 %collective-permute-start = (bf16[8,7168]{1,0:T(8,128)(2,1)}, bf16[8,7168]{1,0:T(8,128)(2,1)S(1)}, u32[]{:S(2)}, u32[]{:S(2)}) collective-permute-start(bf16[8,7168]{1,0:T(8,128)(2,1)} %bitcast.12), channel_id=1, source_target_pairs={{0,6},{1,7},{2,4},{3,5},{4,2},{5,3},{6,0},{7,1},{8,14},{9,15},{10,... | collective-permute-start | bytes 344072 | tf_op jit(solution)/shard_map/ppermute | solution.py:32
  11.0 2.8 %copy-start = (bf16[1010,3328]{1,0:T(8,128)(2,1)}, bf16[1010,3328]{1,0:T(8,128)(2,1)S(1)}, u32[]{:S(2)}) copy-start(bf16[1010,3328]{1,0:T(8,128)(2,1)S(1)} %shard_map.68.table_ref) | copy-start | bytes 20167684
  13.8 6.4 %copy-start.3 = (bf16[1,8,7168]{2,1,0:T(8,128)(2,1)S(1)}, bf16[1,8,7168]{2,1,0:T(8,128)(2,1)}, u32[]{:S(2)}) copy-start(bf16[1,8,7168]{2,1,0:T(8,128)(2,1)} %param.4) | copy-start | bytes 344068
  17.2 3.0 %copy-start.2 = (bf16[1010,3840]{1,0:T(8,128)(2,1)}, bf16[1010,3840]{1,0:T(8,128)(2,1)S(1)}, u32[]{:S(2)}) copy-start(bf16[1010,3840]{1,0:T(8,128)(2,1)S(1)} %shard_map.67.table_ref) | copy-start | bytes 23270404
  20.2 4.8 %collective-permute-start.4 = (bf16[16,3328]{1,0:T(8,128)(2,1)S(1)}, bf16[16,3328]{1,0:T(8,128)(2,1)S(1)}, u32[]{:S(2)}, u32[]{:S(2)}) collective-permute-start(bf16[16,3328]{1,0:T(8,128)(2,1)S(1)} %pad_maximum_fusion.4), channel_id=1, source_target_pairs={{0,1},{1,0},{2,3},{3,2},{4,5},{5,4},{6,7},{7,6},{8,9},{9,8},{10,11... | collective-permute-start | bytes 319496 | tf_op jit(solution)/shard_map/ppermute | solution.py:32
  21.8 5.9 %collective-permute-start.1 = (bf16[16,3840]{1,0:T(8,128)(2,1)S(1)}, bf16[16,3840]{1,0:T(8,128)(2,1)S(1)}, u32[]{:S(2)}, u32[]{:S(2)}) collective-permute-start(bf16[16,3840]{1,0:T(8,128)(2,1)S(1)} %fusion), channel_id=1, source_target_pairs={{0,2},{1,3},{2,0},{3,1},{4,6},{5,7},{6,4},{7,5},{8,10},{9,11},{10,... | collective-permute-start | bytes 368648 | tf_op jit(solution)/shard_map/ppermute | solution.py:32
  25.1 6.3 %collective-permute-start.5 = (bf16[32,3328]{1,0:T(8,128)(2,1)S(1)}, bf16[32,3328]{1,0:T(8,128)(2,1)S(1)}, u32[]{:S(2)}, u32[]{:S(2)}) collective-permute-start(bf16[32,3328]{1,0:T(8,128)(2,1)S(1)} %pad_maximum_fusion.3), channel_id=1, source_target_pairs={{0,2},{1,3},{2,0},{3,1},{4,6},{5,7},{6,4},{7,5},{8,10},{9,11},{10,... | collective-permute-start | bytes 638984 | tf_op jit(solution)/shard_map/ppermute | solution.py:32
  27.8 6.3 %collective-permute-start.2 = (bf16[32,3840]{1,0:T(8,128)(2,1)S(1)}, bf16[32,3840]{1,0:T(8,128)(2,1)S(1)}, u32[]{:S(2)}, u32[]{:S(2)}) collective-permute-start(bf16[32,3840]{1,0:T(8,128)(2,1)S(1)} %pad_maximum_fusion.2), channel_id=1, source_target_pairs={{0,1},{1,0},{2,3},{3,2},{4,5},{5,4},{6,7},{7,6},{8,9},{9,8},{10,11... | collective-permute-start | bytes 737288 | tf_op jit(solution)/shard_map/ppermute | solution.py:32
  34.1 7.7 %collective-permute-start.3 = (bf16[64,3840]{1,0:T(8,128)(2,1)S(1)}, bf16[64,3840]{1,0:T(8,128)(2,1)S(1)}, u32[]{:S(2)}, u32[]{:S(2)}) collective-permute-start(bf16[64,3840]{1,0:T(8,128)(2,1)S(1)} %pad_maximum_fusion.own_ref), channel_id=1, source_target_pairs={{0,16},{16,0},{1,17},{17,1},{2,18},{18,2},{3,19},{19,3},{4,20},{20... | collective-permute-start | bytes 1474568 | tf_op jit(solution)/shard_map/ppermute | solution.py:32
  34.2 2.4 %collective-permute-start.6 = (bf16[64,3328]{1,0:T(8,128)(2,1)S(1)}, bf16[64,3328]{1,0:T(8,128)(2,1)S(1)}, u32[]{:S(2)}, u32[]{:S(2)}) collective-permute-start(bf16[64,3328]{1,0:T(8,128)(2,1)S(1)} %pad_maximum_fusion.1.own_ref), channel_id=1, source_target_pairs={{0,16},{16,0},{1,17},{17,1},{2,18},{18,2},{3,19},{19,3},{4,20},{20... | collective-permute-start | bytes 1277960 | tf_op jit(solution)/shard_map/ppermute | solution.py:32
  36.7 2.9 %copy-start.1 = (bf16[1010,3328]{1,0:T(8,128)(2,1)S(1)}, bf16[1010,3328]{1,0:T(8,128)(2,1)}, u32[]{:S(2)}) copy-start(bf16[1010,3328]{1,0:T(8,128)(2,1)} %copy-done) | copy-start | bytes 20167684
  39.6 2.2 %slice-start = ((s8[7802880]{0:T(1024)(128)(4,1)}), s8[4194304]{0:T(1024)(128)(4,1)S(1)}, s32[]{:S(2)}) async-start(s8[7802880]{0:T(1024)(128)(4,1)} %bitcast.9), calls=%async_computation.2 | async-start | bytes 8388608
  40.6 2.5 %slice-start.1 = ((s8[7802880]{0:T(1024)(128)(4,1)}), s8[3608576]{0:T(1024)(128)(4,1)S(1)}, s32[]{:S(2)}) async-start(s8[7802880]{0:T(1024)(128)(4,1)} %bitcast.9), calls=%async_computation.3 | async-start | bytes 7217152
  46.6 11.2 %collective-permute-start.8 = (f32[512,128]{1,0:T(8,128)S(1)}, f32[512,128]{1,0:T(8,128)S(1)}, u32[]{:S(2)}, u32[]{:S(2)}) collective-permute-start(f32[512,128]{1,0:T(8,128)S(1)} %get-tuple-element.16), channel_id=1, source_target_pairs={{0,8},{8,0},{1,9},{9,1},{2,10},{10,2},{3,11},{11,3},{4,12},{12,4},... | collective-permute-start | bytes 786440 | tf_op jit(solution)/shard_map/ppermute | solution.py:32
  47.2 10.6 %all-to-all-start = ((f32[64,4,128]{2,1,0:T(4,128)}), f32[64,4,128]{2,1,0:T(4,128)S(1)}, u32[]{:S(2)}, u32[]{:S(2)}) async-start(f32[64,4,128]{2,1,0:T(4,128)} %get-tuple-element.17), calls=%async_computation | async-start | bytes 262144 | tf_op jit(solution)/shard_map/all_to_all | solution.py:292
